TPU v7x, 32 devices: a whole 2x2x4 slice. The times are simulated.
32 devices in a mesh: dp: 16 (over z, y, x), tensor: 2 (over core).
Axes of the slice: x: 2, y: 2, z: 4, core: 2. Of those that a mesh axis runs over, the one named last changes fastest.
Arguments:
- tokens_in: bfloat16 [8192, 2048], P(('dp', 'tensor')), may hold values from -6 to 6
- cotangent: bfloat16 [8192, 2048], P(('dp', 'tensor')), may hold values from -6 to 6
- segment_ids: int32 [8192], P('dp'), may hold values from 0 to 3, as said below
- destination: int32 [8192], P(('dp', 'tensor')), may hold values from 0 to 8191, as said below
- source: int32 [8192], P(('dp', 'tensor')), may hold values from 0 to 8191, as said below
- w_query: float32 [2048, 2048], P('dp', 'tensor'), may hold values from -0.125 to 0.125
- w_key: float32 [2048, 2048], P('dp', 'tensor'), may hold values from -0.125 to 0.125
- w_value: float32 [2048, 2048], P('dp', 'tensor'), may hold values from -0.125 to 0.125
- w_out: float32 [2048, 2048], P('tensor', 'dp'), may hold values from -0.5 to 0.5
- w_gate: float32 [2048, 8192], P('dp', 'tensor'), may hold values from -0.125 to 0.125
- w_up: float32 [2048, 8192], P('dp', 'tensor'), may hold values from -0.125 to 0.125
- w_down: float32 [8192, 2048], P('tensor', 'dp'), may hold values from -0.0625 to 0.0625
Outputs:
- layer_out: float32 [8192, 2048], P(('dp', 'tensor'))
- grad_in: float32 [8192, 2048], P(('dp', 'tensor'))
- grad_w_query: float32 [2048, 2048], P('dp', 'tensor')
- grad_w_key: float32 [2048, 2048], P('dp', 'tensor')
- grad_w_value: float32 [2048, 2048], P('dp', 'tensor')
- grad_w_out: float32 [2048, 2048], P('tensor', 'dp')
- grad_w_gate: float32 [2048, 8192], P('dp', 'tensor')
- grad_w_up: float32 [2048, 8192], P('dp', 'tensor')
- grad_w_down: float32 [8192, 2048], P('tensor', 'dp')
Inputs may be any that keep to these rules, and one draw needn't show every extreme that they name: `segment_ids`: within each group of 512 balanced rows, the number of the sequence a row belongs to, never falling, all 4 sequences present, each of 1 to 255 rows, one of exactly 255 rows; sequences 2 k and 2 k + 1 together fill rows k * 256 to (k + 1) * 256 - 1 of the group. `destination`: a permutation of the 8192 rows; the 256 rows of each device go, 8 of them, to each device. The inverse of destination: source[destination[i]] = i.
All inputs are finite; a program needn't handle non-finite values.
Results may differ from a plain program's by a relative error of at most 0.014.
Values may be sent and summed in bfloat16 or wider, within the bound.
A program may use at most 320 MiB of HBM per device.

v0:
```python
import math

import jax
import jax.numpy as jnp
from jax import lax
from jax.sharding import PartitionSpec as P

HEAD_DIM = 128
SEGS = 4


EPSILON = 1e-05
NEG_LARGE = -1e30


def project(left, right):
    return jnp.dot(left, right, preferred_element_type=jnp.float32)


def project_t(left, right):
    return lax.dot_general(
        left, right, (((1,), (1,)), ((), ())), preferred_element_type=jnp.float32
    )


def outer_sum(left, right):
    return lax.dot_general(
        left, right, (((0,), (0,)), ((), ())), preferred_element_type=jnp.float32
    )


def layer_norm(values):
    center = values - jnp.mean(values, axis=-1, keepdims=True)
    spread = jnp.mean(center * center, axis=-1, keepdims=True)
    return center * lax.rsqrt(spread + EPSILON)


def norm_back(values, gradient):
    _, backward = jax.vjp(layer_norm, values)
    return backward(gradient)[0]


def swiglu(gate_lin, up_lin):
    return jax.nn.silu(gate_lin) * up_lin


def rotate(values, cos_rows, sin_rows):
    row_total = values.shape[0]
    heads_view = values.reshape(row_total, -1, HEAD_DIM)
    half_dim = HEAD_DIM // 2
    first_half = heads_view[..., :half_dim]
    second_half = heads_view[..., half_dim:]
    cos_wide = cos_rows[:, None, :]
    sin_wide = sin_rows[:, None, :]
    turned = jnp.concatenate(
        [
            first_half * cos_wide - second_half * sin_wide,
            second_half * cos_wide + first_half * sin_wide,
        ],
        axis=-1,
    )
    return turned.reshape(row_total, -1)


def geometry(segments):
    row_total = segments.shape[0]
    seq_numbers = jnp.arange(SEGS, dtype=jnp.int32)
    starts = jnp.sum((segments[:, None] < seq_numbers[None, :]).astype(jnp.int32), axis=0)
    onehot = segments[:, None] == seq_numbers[None, :]
    offset = jnp.sum(jnp.where(onehot, starts[None, :], 0), axis=1)
    row_index = jnp.arange(row_total, dtype=jnp.int32)
    places = row_index - offset
    half_dim = HEAD_DIM // 2
    frequency = jnp.exp(
        -jnp.arange(half_dim, dtype=jnp.float32) * (2.0 * math.log(10000.0) / HEAD_DIM)
    )
    angles = places.astype(jnp.float32)[:, None] * frequency[None, :]
    visible = (segments[:, None] == segments[None, :]) & (row_index[None, :] <= row_index[:, None])
    return (jnp.cos(angles), jnp.sin(angles), visible)


def group_rows(values):
    return lax.all_gather(values, "tensor", axis=0, tiled=True)


def share_sum(values):
    return lax.psum_scatter(values, "tensor", scatter_dimension=0, tiled=True)


def on_device(
    tokens_in,
    cotangent,
    segment_ids,
    destination,
    source,
    w_query,
    w_key,
    w_value,
    w_out,
    w_gate,
    w_up,
    w_down,
):
    tok_rows = tokens_in.shape[0]
    devices = lax.axis_size(("dp", "tensor"))
    per_peer = tok_rows // devices
    row_index = jnp.arange(tok_rows, dtype=jnp.int32)
    peer_to = destination // tok_rows
    ahead_rows = (peer_to[None, :] == peer_to[:, None]) & (
        destination[None, :] < destination[:, None]
    )
    send_slot = peer_to * per_peer + jnp.sum(ahead_rows.astype(jnp.int32), axis=1)
    peer_from = source // tok_rows
    before = (peer_from[None, :] == peer_from[:, None]) & (row_index[None, :] < row_index[:, None])
    recv_slot = peer_from * per_peer + jnp.sum(before.astype(jnp.int32), axis=1)
    packed_in = jnp.zeros_like(tokens_in).at[send_slot].set(tokens_in)
    packed_grad = jnp.zeros_like(cotangent).at[send_slot].set(cotangent)
    arrived_in, arrived_grad = (
        lax.all_to_all(packed_in, ("dp", "tensor"), split_axis=0, concat_axis=0, tiled=True),
        lax.all_to_all(packed_grad, ("dp", "tensor"), split_axis=0, concat_axis=0, tiled=True),
    )
    inputs = arrived_in[recv_slot].astype(jnp.float32)
    upstream_low = arrived_grad[recv_slot]
    upstream = upstream_low.astype(jnp.float32)
    cos_rows, sin_rows, visible = geometry(segment_ids)
    score_scale = 1.0 / math.sqrt(HEAD_DIM)
    query_full, key_full, value_full, out_full = (
        lax.all_gather(w_query.astype(jnp.bfloat16), "dp", axis=0, tiled=True),
        lax.all_gather(w_key.astype(jnp.bfloat16), "dp", axis=0, tiled=True),
        lax.all_gather(w_value.astype(jnp.bfloat16), "dp", axis=0, tiled=True),
        lax.all_gather(w_out.astype(jnp.bfloat16), "dp", axis=1, tiled=True),
    )
    gate_full, up_full, down_full = (
        lax.all_gather(w_gate.astype(jnp.bfloat16), "dp", axis=0, tiled=True),
        lax.all_gather(w_up.astype(jnp.bfloat16), "dp", axis=0, tiled=True),
        lax.all_gather(w_down.astype(jnp.bfloat16), "dp", axis=1, tiled=True),
    )
    normed_one = layer_norm(inputs)
    seen_one = group_rows(normed_one.astype(jnp.bfloat16))
    group_total = seen_one.shape[0]
    query_lin = project(seen_one, query_full)
    key_lin = project(seen_one, key_full)
    queries = rotate(query_lin, cos_rows, sin_rows).astype(jnp.bfloat16)
    key_rows = rotate(key_lin, cos_rows, sin_rows).astype(jnp.bfloat16)
    value_rows = project(seen_one, value_full).astype(jnp.bfloat16)
    heads_local = queries.shape[1] // HEAD_DIM

    def by_head(values):
        return values.reshape(group_total, heads_local, HEAD_DIM).transpose(1, 0, 2)

    def from_heads(values):
        return values.transpose(1, 0, 2).reshape(group_total, heads_local * HEAD_DIM)

    def scores_of(query_head, key_head):
        raw_scores = project_t(query_head, key_head) * score_scale
        return jnp.where(visible, raw_scores, NEG_LARGE)

    def head_forward(operands):
        query_head, key_head, value_head = operands
        scores = scores_of(query_head, key_head)
        row_peak = jnp.max(scores, axis=1, keepdims=True)
        weights = jnp.exp(scores - row_peak)
        totals = jnp.sum(weights, axis=1, keepdims=True)
        soft_rows = (weights / totals).astype(jnp.bfloat16)
        mixed_rows = project(soft_rows, value_head).astype(jnp.bfloat16)
        return (mixed_rows, (row_peak + jnp.log(totals))[:, 0])

    heads_query = by_head(queries)
    heads_key = by_head(key_rows)
    heads_value = by_head(value_rows)
    mixed_heads, log_totals = lax.map(head_forward, (heads_query, heads_key, heads_value))
    attended = from_heads(mixed_heads)
    middle = inputs + share_sum(project(attended, out_full))
    seen_two = group_rows(layer_norm(middle).astype(jnp.bfloat16))
    gate_lin = project(seen_two, gate_full)
    up_lin = project(seen_two, up_full)
    hidden = swiglu(gate_lin, up_lin).astype(jnp.bfloat16)
    output = middle + share_sum(project(hidden, down_full))
    grad_two_all = group_rows(upstream_low)
    grad_hidden = project_t(grad_two_all, down_full)
    grad_down = outer_sum(hidden, grad_two_all)
    _, swiglu_back = jax.vjp(swiglu, gate_lin, up_lin)
    grad_gate_f, grad_up_f = swiglu_back(grad_hidden)
    grad_gate = grad_gate_f.astype(jnp.bfloat16)
    grad_upward = grad_up_f.astype(jnp.bfloat16)
    grad_gate_w = outer_sum(seen_two, grad_gate)
    grad_up_w = outer_sum(seen_two, grad_upward)
    grad_normed_two = share_sum(project_t(grad_gate, gate_full) + project_t(grad_upward, up_full))
    grad_middle = upstream + norm_back(middle, grad_normed_two)
    grad_one_all = group_rows(grad_middle.astype(jnp.bfloat16))
    grad_attended = project_t(grad_one_all, out_full).astype(jnp.bfloat16)
    grad_out_w = outer_sum(attended, grad_one_all)

    def head_backward(operands):
        query_head, key_head, value_head, grad_mixed, log_total = operands
        scores = scores_of(query_head, key_head)
        soft_rows = jnp.exp(scores - log_total[:, None])
        grad_soft = project_t(grad_mixed, value_head)
        inner_sum = jnp.sum(soft_rows * grad_soft, axis=1, keepdims=True)
        grad_scores = (soft_rows * (grad_soft - inner_sum)).astype(jnp.bfloat16)
        grad_query = project(grad_scores, key_head) * score_scale
        grad_key = outer_sum(grad_scores, query_head) * score_scale
        grad_value = outer_sum(soft_rows.astype(jnp.bfloat16), grad_mixed)
        return (grad_query, grad_key, grad_value)

    grad_query_heads, grad_key_heads, grad_value_heads = lax.map(
        head_backward, (heads_query, heads_key, heads_value, by_head(grad_attended), log_totals)
    )
    _, rotate_back = jax.vjp(lambda values: rotate(values, cos_rows, sin_rows), query_lin)
    grad_query_lin = rotate_back(from_heads(grad_query_heads))[0].astype(jnp.bfloat16)
    grad_key_lin = rotate_back(from_heads(grad_key_heads))[0].astype(jnp.bfloat16)
    grad_value_lin = from_heads(grad_value_heads).astype(jnp.bfloat16)
    grad_query_w = outer_sum(seen_one, grad_query_lin)
    grad_key_w = outer_sum(seen_one, grad_key_lin)
    grad_value_w = outer_sum(seen_one, grad_value_lin)
    grad_normed_one = share_sum(
        project_t(grad_query_lin, query_full)
        + project_t(grad_key_lin, key_full)
        + project_t(grad_value_lin, value_full)
    )
    grad_inputs = grad_middle + norm_back(inputs, grad_normed_one)
    summed_query, summed_key, summed_value, summed_out, summed_gate, summed_up, summed_down = (
        lax.psum_scatter(grad_query_w, "dp", scatter_dimension=0, tiled=True),
        lax.psum_scatter(grad_key_w, "dp", scatter_dimension=0, tiled=True),
        lax.psum_scatter(grad_value_w, "dp", scatter_dimension=0, tiled=True),
        lax.psum_scatter(grad_out_w, "dp", scatter_dimension=1, tiled=True),
        lax.psum_scatter(grad_gate_w, "dp", scatter_dimension=0, tiled=True),
        lax.psum_scatter(grad_up_w, "dp", scatter_dimension=0, tiled=True),
        lax.psum_scatter(grad_down, "dp", scatter_dimension=1, tiled=True),
    )
    packed_out = jnp.zeros_like(output).at[recv_slot].set(output)
    packed_back = jnp.zeros_like(grad_inputs).at[recv_slot].set(grad_inputs)
    returned_out, returned_grad = (
        lax.all_to_all(packed_out, ("dp", "tensor"), split_axis=0, concat_axis=0, tiled=True),
        lax.all_to_all(packed_back, ("dp", "tensor"), split_axis=0, concat_axis=0, tiled=True),
    )
    return (
        returned_out[send_slot],
        returned_grad[send_slot],
        summed_query,
        summed_key,
        summed_value,
        summed_out,
        summed_gate,
        summed_up,
        summed_down,
    )


def solution(mesh):
    in_specs = (
        P(("dp", "tensor"), None),
        P(("dp", "tensor"), None),
        P("dp"),
        P(("dp", "tensor")),
        P(("dp", "tensor")),
        P("dp", "tensor"),
        P("dp", "tensor"),
        P("dp", "tensor"),
        P("tensor", "dp"),
        P("dp", "tensor"),
        P("dp", "tensor"),
        P("tensor", "dp"),
    )
    out_specs = (
        P(("dp", "tensor"), None),
        P(("dp", "tensor"), None),
        P("dp", "tensor"),
        P("dp", "tensor"),
        P("dp", "tensor"),
        P("tensor", "dp"),
        P("dp", "tensor"),
        P("dp", "tensor"),
        P("tensor", "dp"),
    )
    return jax.shard_map(
        on_device, mesh=mesh, in_specs=in_specs, out_specs=out_specs, check_vma=False
    )
```

profile of v0, /device:TPU:0, one launch (start us, length us, event | category | flops | bytes accessed | tf_op | source)
XLA Modules:
  0.0 4124.4 jit_solution(4641292807812543355)
XLA Ops:
  13.4 7.3 all-to-all-start
  21.0 25.9 all-to-all-done
  55.8 5.4 all-gather.13.cloned.1.call-done
  61.2 80.6 %all-gather.17.cloned.1.call-done = bf16[2048,1024]{1,0:T(8,128)(2,1)} async-done(((bf16[128,1024]{1,0:T(8,128)(2,1)}), bf16[2048,1024]{1,0:T(8,128)(2,1)}) %all-gather.17.cloned.1.call-update) | async-done | bytes 4194320 | tf_op jit(solution)/shard_map/all_gather | solution.py:129
  141.8 5.2 fusion.79
  147.0 72.9 %all-gather.15.cloned.1.call-done = bf16[2048,1024]{1,0:T(8,128)(2,1)} async-done(((bf16[128,1024]{1,0:T(8,128)(2,1)}), bf16[2048,1024]{1,0:T(8,128)(2,1)}) %all-gather.15.cloned.1.call-update) | async-done | bytes 4194320 | tf_op jit(solution)/shard_map/all_gather | solution.py:128
  219.9 5.2 fusion.78
  228.6 69.2 %all-gather.19.cloned.1.call-done = bf16[2048,1024]{1,0:T(8,128)(2,1)} async-done(((bf16[128,1024]{1,0:T(8,128)(2,1)}), bf16[2048,1024]{1,0:T(8,128)(2,1)}) %all-gather.19.cloned.1.call-update) | async-done | bytes 4194320 | tf_op jit(solution)/shard_map/all_gather | solution.py:130
  297.8 5.2 fusion.60
  304.1 34.4 while.28
  338.5 50.3 %all-gather.21.cloned.1.call-done = bf16[1024,2048]{1,0:T(8,128)(2,1)} async-done(((bf16[1024,128]{1,0:T(8,128)(2,1)}), bf16[1024,2048]{1,0:T(8,128)(2,1)}) %all-gather.21.cloned.1.call-update) | async-done | bytes 4194320 | tf_op jit(solution)/shard_map/all_gather | solution.py:131
  388.8 6.5 fusion.80
  395.8 9.9 reduce-scatter.12.cloned.1.call-done
  414.9 3.8 scatter_custom_fusion.2
  418.7 49.5 %all_to_all.48 = bf16[32,8,2048]{2,1,0:T(8,128)(2,1)S(1)} all-to-all(bf16[32,8,2048]{2,1,0:T(8,128)(2,1)} %bitcast.174), channel_id=1, replica_groups=mesh['dp'=16,'tensor'=2] {'dp','tensor'}, dimensions={0} | all-to-all | bytes 2097152 | tf_op jit(solution)/shard_map/all_to_all | solution.py:120
  473.3 155.9 %all-gather.25.cloned.1.call-done = bf16[2048,4096]{1,0:T(8,128)(2,1)} async-done(((bf16[128,4096]{1,0:T(8,128)(2,1)}), bf16[2048,4096]{1,0:T(8,128)(2,1)}) %all-gather.25.cloned.1.call-update) | async-done | bytes 16777232 | tf_op jit(solution)/shard_map/all_gather | solution.py:134
  629.3 15.0 fusion.81
  644.2 178.6 %all-gather.27.cloned.1.call-done = bf16[2048,4096]{1,0:T(8,128)(2,1)} async-done(((bf16[128,4096]{1,0:T(8,128)(2,1)}), bf16[2048,4096]{1,0:T(8,128)(2,1)}) %all-gather.27.cloned.1.call-update) | async-done | bytes 16777232 | tf_op jit(solution)/shard_map/all_gather | solution.py:135
  822.9 14.9 fusion.82
  837.8 249.2 %all-gather.29.cloned.1.call-done = bf16[4096,2048]{1,0:T(8,128)(2,1)} async-done(((bf16[4096,128]{1,0:T(8,128)(2,1)}), bf16[4096,2048]{1,0:T(8,128)(2,1)}) %all-gather.29.cloned.1.call-update) | async-done | bytes 16777232 | tf_op jit(solution)/shard_map/all_gather | solution.py:136
  1087.0 20.4 multiply_convert_fusion.1
  1107.4 16.5 fusion.84
  1123.9 14.4 convolution_add_fusion
  1138.4 10.3 reduce-scatter.16.cloned.1.call-done
  1154.2 14.9 fusion.83
  1169.2 5.2 fusion.61
  1175.1 65.5 %while.29 = (s32[]{:T(128)}, f32[8,512,128]{1,2,0:T(8,128)}, f32[8,512,128]{1,2,0:T(8,128)}, bf16[8,512,128]{1,2,0:T(8,128)(2,1)}, bf16[8,512,128]{2,1,0:T(8,128...) while((s32[]{:T(128)}, f32[8,512,128]{1,2,0:T(8,128)}, ...), condition=%wide.region_22.23_spmd.clone, body=%wide.region_20.22_spmd.clone.sunk | while | flops 338820608 | bytes 11682949 | solution.py:206
  1250.8 4.4 add_add_fusion
  1255.7 7.5 fusion.87
  1264.7 5.6 fusion.88
  1271.6 5.7 fusion.89
  1279.6 5.6 fusion.90
  1286.7 17.7 fusion.91
  1304.5 17.7 fusion.92
  1323.8 17.6 fusion.93
  1342.9 4.5 scatter_custom_fusion.1
  1347.5 5.9 all-to-all-start.1
  1356.4 6.1 scatter_custom_fusion.3
  1362.5 58.4 %all-to-all-done.1 = f32[32,8,2048]{2,1,0:T(8,128)S(1)} async-done(((f32[32,8,2048]{2,1,0:T(8,128)}), f32[32,8,2048]{2,1,0:T(8,128)S(1)}, u32[]{:S(2)}, u32[]{:S(2)}) %all-to-all-start.1) | async-done | bytes 2097184 | tf_op jit(solution)/shard_map/all_to_all | solution.py:234
  1420.9 8.0 all-to-all-start.3
  1431.7 64.5 %all-to-all-done.3 = f32[32,8,2048]{2,1,0:T(8,128)} async-done(((f32[32,8,2048]{2,1,0:T(8,128)}), f32[32,8,2048]{2,1,0:T(8,128)}, u32[]{:S(2)}, u32[]{:S(2)}) %all-to-all-start.3) | async-done | bytes 2097184 | tf_op jit(solution)/shard_map/all_to_all | solution.py:235
  1496.2 5.2 gather_fusion.3
  1501.4 177.1 %reduce-scatter.22.cloned.1.call-done = f32[128,1024]{1,0:T(8,128)} async-done(((f32[2048,1024]{1,0:T(8,128)}), f32[128,1024]{1,0:T(8,128)}) %reduce-scatter.22.cloned.1.call-update) | async-done | bytes 524304 | tf_op jit(solution)/shard_map/reduce_scatter | solution.py:224
  1678.5 183.0 %reduce-scatter.24.cloned.1.call-done = f32[128,1024]{1,0:T(8,128)} async-done(((f32[2048,1024]{1,0:T(8,128)}), f32[128,1024]{1,0:T(8,128)}) %reduce-scatter.24.cloned.1.call-update) | async-done | bytes 524304 | tf_op jit(solution)/shard_map/reduce_scatter | solution.py:225
  1861.5 183.1 %reduce-scatter.26.cloned.1.call-done = f32[1024,128]{1,0:T(8,128)} async-done(((f32[1024,2048]{1,0:T(8,128)}), f32[1024,128]{1,0:T(8,128)}) %reduce-scatter.26.cloned.1.call-update) | async-done | bytes 524304 | tf_op jit(solution)/shard_map/reduce_scatter | solution.py:226
  2044.6 688.6 %reduce-scatter.28.cloned.1.call-done = f32[128,4096]{1,0:T(8,128)} async-done(((f32[2048,4096]{1,0:T(8,128)}), f32[128,4096]{1,0:T(8,128)}) %reduce-scatter.28.cloned.1.call-update) | async-done | bytes 2097168 | tf_op jit(solution)/shard_map/reduce_scatter | solution.py:227
  2733.2 692.0 %reduce-scatter.30.cloned.1.call-done = f32[128,4096]{1,0:T(8,128)} async-done(((f32[2048,4096]{1,0:T(8,128)}), f32[128,4096]{1,0:T(8,128)}) %reduce-scatter.30.cloned.1.call-update) | async-done | bytes 2097168 | tf_op jit(solution)/shard_map/reduce_scatter | solution.py:228
  3425.3 692.0 %reduce-scatter.32.cloned.1.call-done = f32[4096,128]{1,0:T(8,128)} async-done(((f32[4096,2048]{1,0:T(8,128)}), f32[4096,128]{1,0:T(8,128)}) %reduce-scatter.32.cloned.1.call-update) | async-done | bytes 2097168 | tf_op jit(solution)/shard_map/reduce_scatter | solution.py:229
  (331 shorter events, 165.7 us)
Async XLA Ops:
  7.2 13.5 copy-start.32
  9.5 405.4 %copy-start.29 = (s32[256]{0:T(256)}, s32[256]{0:T(256)S(1)}, u32[]{:S(2)}) copy-start(s32[256]{0:T(256)S(1)} %compare_select_fusion) | copy-start | bytes 3076
  13.4 33.5 all-to-all-start
  20.7 40.5 all-gather.13.cloned.1.call-start
  20.9 27.3 copy-start.31
  48.3 3.1 copy-start.2
  48.5 3.0 copy-start.15
  51.4 2.6 copy-start.18
  51.4 3.6 copy-start.27
  51.5 90.4 %all-gather.17.cloned.1.call-start = ((), (), s32[]{:S(2)}) async-start(), calls=%async_computation.17 | async-start | bytes 4456448 | tf_op jit(solution)/shard_map/all_gather | solution.py:129
  52.3 167.6 %all-gather.15.cloned.1.call-start = ((), (), s32[]{:S(2)}) async-start(), calls=%async_computation.16 | async-start | bytes 4456448 | tf_op jit(solution)/shard_map/all_gather | solution.py:128
  53.1 244.7 %all-gather.19.cloned.1.call-start = ((), (), s32[]{:S(2)}) async-start(), calls=%async_computation.18 | async-start | bytes 4456448 | tf_op jit(solution)/shard_map/all_gather | solution.py:130
  53.9 334.9 %all-gather.21.cloned.1.call-start = ((), (), s32[]{:S(2)}) async-start(), calls=%async_computation.19 | async-start | bytes 4456448 | tf_op jit(solution)/shard_map/all_gather | solution.py:131
  54.7 351.0 %reduce-scatter.12.cloned.1.call-start = ((), (), s32[]{:S(2)}) async-start(), calls=%async_computation.20 | async-start | bytes 6291456 | tf_op jit(solution)/shard_map/reduce_scatter | solution.py:87
  55.8 169.3 %copy-start.11 = (f32[512,64]{0,1:T(8,128)}, f32[512,64]{0,1:T(8,128)S(1)}, u32[]{:S(2)}) copy-start(f32[512,64]{0,1:T(8,128)S(1)} %get-tuple-element.239) | copy-start | bytes 393220
  55.8 169.3 %copy-start.13 = (f32[512,64]{0,1:T(8,128)}, f32[512,64]{0,1:T(8,128)S(1)}, u32[]{:S(2)}) copy-start(f32[512,64]{0,1:T(8,128)S(1)} %get-tuple-element.240) | copy-start | bytes 393220
  338.5 56.8 %copy-start.9 = (bf16[8,512,128]{1,2,0:T(8,128)(2,1)}, bf16[8,512,128]{1,2,0:T(8,128)(2,1)S(1)}, u32[]{:S(2)}) copy-start(bf16[8,512,128]{1,2,0:T(8,128)(2,1)S(1)} %get-tuple-element.101) | copy-start | bytes 3145732
  395.3 10.4 copy-start.3
  395.4 78.0 %all-gather.23.cloned.1.call-start = ((), (), s32[]{:S(2)}) async-start(), calls=%async_computation.21 | async-start | bytes 3145728 | tf_op jit(solution)/shard_map/all_gather | solution.py:83
  407.6 743.2 %copy-start = (f32[256,2048]{1,0:T(8,128)}, f32[256,2048]{1,0:T(8,128)S(1)}, u32[]{:S(2)}) copy-start(f32[256,2048]{1,0:T(8,128)S(1)} %get-tuple-element.217) | copy-start | bytes 6291460
  409.3 220.0 %all-gather.25.cloned.1.call-start = ((), (), s32[]{:S(2)}) async-start(), calls=%async_computation.22 | async-start | bytes 17825792 | tf_op jit(solution)/shard_map/all_gather | solution.py:134
  412.1 410.8 %all-gather.27.cloned.1.call-start = ((), (), s32[]{:S(2)}) async-start(), calls=%async_computation.23 | async-start | bytes 17825792 | tf_op jit(solution)/shard_map/all_gather | solution.py:135
  414.8 422.9 %all-gather.33.cloned.1.call-start = ((), (), s32[]{:S(2)}) async-start(), calls=%async_computation.36 | async-start | bytes 3145728 | tf_op jit(solution)/shard_map/all_gather | solution.py:83
  470.5 616.5 %all-gather.29.cloned.1.call-start = ((), (), s32[]{:S(2)}) async-start(), calls=%async_computation.24 | async-start | bytes 17825792 | tf_op jit(solution)/shard_map/all_gather | solution.py:136
  473.3 675.4 %reduce-scatter.16.cloned.1.call-start = ((), (), s32[]{:S(2)}) async-start(), calls=%async_computation.26 | async-start | bytes 6291456 | tf_op jit(solution)/shard_map/reduce_scatter | solution.py:87
  1107.4 16.5 copy-start.42
  1138.3 30.9 all-gather.31.cloned.1.call-start
  1154.1 187.3 %reduce-scatter.14.cloned.1.call-start = ((), (), s32[]{:S(2)}) async-start(), calls=%async_computation.25 | async-start | bytes 6291456 | tf_op jit(solution)/shard_map/reduce_scatter | solution.py:87
  1169.1 184.3 %reduce-scatter.18.cloned.1.call-start = ((), (), s32[]{:S(2)}) async-start(), calls=%async_computation.28 | async-start | bytes 6291456 | tf_op jit(solution)/shard_map/reduce_scatter | solution.py:87
  1175.1 65.5 %copy-start.12 = (f32[512,64]{0,1:T(8,128)S(1)}, f32[512,64]{0,1:T(8,128)}, u32[]{:S(2)}) copy-start(f32[512,64]{0,1:T(8,128)} %copy-done.11) | copy-start | bytes 393220
  1175.1 65.5 %copy-start.14 = (f32[512,64]{0,1:T(8,128)S(1)}, f32[512,64]{0,1:T(8,128)}, u32[]{:S(2)}) copy-start(f32[512,64]{0,1:T(8,128)} %copy-done.13) | copy-start | bytes 393220
  1245.9 2.4 copy-start.33
  1248.3 2.4 copy-start.35
  1248.3 2.5 copy-start.40
  1255.2 246.1 %reduce-scatter.20.cloned.1.call-start = ((), (), s32[]{:S(2)}) async-start(), calls=%async_computation.29 | async-start | bytes 8912896 | tf_op jit(solution)/shard_map/reduce_scatter | solution.py:223
  1263.2 415.3 %reduce-scatter.22.cloned.1.call-start = ((), (), s32[]{:S(2)}) async-start(), calls=%async_computation.30 | async-start | bytes 8912896 | tf_op jit(solution)/shard_map/reduce_scatter | solution.py:224
  1270.4 591.0 %reduce-scatter.24.cloned.1.call-start = ((), (), s32[]{:S(2)}) async-start(), calls=%async_computation.31 | async-start | bytes 8912896 | tf_op jit(solution)/shard_map/reduce_scatter | solution.py:225
  1277.3 767.2 %reduce-scatter.26.cloned.1.call-start = ((), (), s32[]{:S(2)}) async-start(), calls=%async_computation.32 | async-start | bytes 8912896 | tf_op jit(solution)/shard_map/reduce_scatter | solution.py:226
  1285.2 1448.1 %reduce-scatter.28.cloned.1.call-start = ((), (), s32[]{:S(2)}) async-start(), calls=%async_computation.33 | async-start | bytes 35651584 | tf_op jit(solution)/shard_map/reduce_scatter | solution.py:227
  1304.4 2120.8 %reduce-scatter.30.cloned.1.call-start = ((), (), s32[]{:S(2)}) async-start(), calls=%async_computation.34 | async-start | bytes 35651584 | tf_op jit(solution)/shard_map/reduce_scatter | solution.py:228
  1322.2 2795.1 %reduce-scatter.32.cloned.1.call-start = ((), (), s32[]{:S(2)}) async-start(), calls=%async_computation.35 | async-start | bytes 35651584 | tf_op jit(solution)/shard_map/reduce_scatter | solution.py:229
  1347.5 6.0 copy-start.4
  1347.5 6.0 copy-start.20
  1347.5 73.5 %all-to-all-start.1 = ((f32[32,8,2048]{2,1,0:T(8,128)}), f32[32,8,2048]{2,1,0:T(8,128)S(1)}, u32[]{:S(2)}, u32[]{:S(2)}) async-start(f32[32,8,2048]{2,1,0:T(8,128)} %bitcast.171), calls=%async_computation.3 | async-start | bytes 4194304 | tf_op jit(solution)/shard_map/all_to_all | solution.py:234
  1353.4 2.3 copy-start.26
  1353.4 2.3 copy-start.22
  1420.9 8.0 copy-start.30
  1420.9 75.2 %all-to-all-start.3 = ((f32[32,8,2048]{2,1,0:T(8,128)}), f32[32,8,2048]{2,1,0:T(8,128)}, u32[]{:S(2)}, u32[]{:S(2)}) async-start(f32[32,8,2048]{2,1,0:T(8,128)} %bitcast.172), calls=%async_computation.7 | async-start | bytes 4194304 | tf_op jit(solution)/shard_map/all_to_all | solution.py:235
  (20 other events, 29.9 us)
Sparse Core Ops, SparseCore 0:
  51.6 9.5 all-gather.12
  64.5 77.2 all-gather.16
  145.2 74.6 all-gather.14
  223.1 74.6 all-gather.18
  300.9 87.8 all-gather.20
  395.5 10.2 reduce-scatter.11
  409.4 11.8 all-gather.22
  425.1 204.1 all-gather.24
  633.0 189.7 all-gather.26
  824.3 8.7 all-gather.32
  836.2 250.7 all-gather.28
  1138.4 10.2 reduce-scatter.15
  1154.3 11.8 all-gather.30
  1169.3 13.3 reduce-scatter.13
  1255.3 13.2 reduce-scatter.17
  1271.4 224.4 reduce-scatter.19
  1498.6 179.8 reduce-scatter.21
  1681.2 180.2 reduce-scatter.23
  1864.3 180.2 reduce-scatter.25
  2047.4 685.8 reduce-scatter.27
  2736.2 689.0 reduce-scatter.29
  3428.2 689.0 reduce-scatter.31
where the time goes:
time: 4140 us; the launch traced here: 4120 us
  waiting for transfers between devices  3650 us (88%)
  matrix products  279 us (7%)
  local copies, waits for them, and re-layouts  63.7 us (2%)
  blocking collectives  49.5 us (1%)
  other arithmetic  45.1 us (1%)
    reduce_scatter x1, waiting for transfers between devices, on_device(): lax.psum_scatter(grad_up_w, 'dp', scatter_dimension=0, tiled=True)  692 us
    reduce_scatter x1, waiting for transfers between devices, on_device(): lax.psum_scatter(grad_down, 'dp', scatter_dimension=1, tiled=True)  692 us
    reduce_scatter x1, waiting for transfers between devices, on_device(): lax.psum_scatter(grad_gate_w, 'dp', scatter_dimension=0, tiled=True)  689 us
    all_gather x1, waiting for transfers between devices, on_device(): lax.all_gather(w_down.astype(jnp.bfloat16), 'dp', axis=1, tiled=True)  249 us
    reduce_scatter x1, waiting for transfers between devices, on_device(): lax.psum_scatter(grad_out_w, 'dp', scatter_dimension=1, tiled=True)  183 us
    reduce_scatter x1, waiting for transfers between devices, on_device(): lax.psum_scatter(grad_value_w, 'dp', scatter_dimension=0, tiled=True)  183 us
    all_gather x1, waiting for transfers between devices, on_device(): lax.all_gather(w_up.astype(jnp.bfloat16), 'dp', axis=0, tiled=True)  179 us
    reduce_scatter x1, waiting for transfers between devices, on_device(): lax.psum_scatter(grad_key_w, 'dp', scatter_dimension=0, tiled=True)  177 us
  transfers between devices with their start and end apart: 25, of which 19 were waited for; matrix products, arithmetic and copies ran while one was open for 7% of the time, Pallas kernels for 0%

commit v1 on v0

v1 whole, which is shorter than its diff:
```python
import math

import jax
import jax.numpy as jnp
from jax import lax
from jax.experimental import pallas as pl
from jax.experimental.pallas import tpu as pltpu
from jax.sharding import Mesh
from jax.sharding import PartitionSpec as P

HEAD_DIM = 128
SEGS = 4
EPSILON = 1e-05
NEG_LARGE = -1e30
F32 = jnp.float32
BF16 = jnp.bfloat16
FLIP = ((0, 1), (1, 0))


def project(left, right):
    return jnp.dot(left, right, preferred_element_type=F32)


def project_t(left, right):
    return lax.dot_general(left, right, (((1,), (1,)), ((), ())), preferred_element_type=F32)


def outer_sum(left, right):
    return lax.dot_general(left, right, (((0,), (0,)), ((), ())), preferred_element_type=F32)


def norm_parts(values):
    center = values - jnp.mean(values, axis=-1, keepdims=True)
    spread = jnp.mean(center * center, axis=-1, keepdims=True)
    scale = lax.rsqrt(spread + EPSILON)
    return center * scale, scale


def norm_back(normed, scale, gradient):
    mean_grad = jnp.mean(gradient, axis=-1, keepdims=True)
    mean_both = jnp.mean(gradient * normed, axis=-1, keepdims=True)
    return (gradient - mean_grad - normed * mean_both) * scale


def to_x(values):
    return lax.ppermute(values, "x", FLIP)


def to_y(values):
    return lax.ppermute(values, "y", FLIP)


def to_core(values):
    return lax.ppermute(values, "c", FLIP)


def plane_gather(rows):
    half = rows.shape[0] // 2
    first, second = rows[:half], rows[half:]
    first_x = to_x(first)
    second_y = to_y(second)
    first_far = to_y(jnp.concatenate([first, first_x]))
    second_far = to_x(jnp.concatenate([second, second_y]))
    mine = jnp.concatenate(
        [
            first,
            second,
            first_x,
            second_far[:half],
            first_far[:half],
            second_y,
            first_far[half:],
            second_far[half:],
        ]
    )
    return jnp.concatenate([mine, to_core(mine)])


def plane_scatter(far, near):
    block = near.shape[0] // 4
    half = block // 2
    got = to_core(far.astype(BF16))
    paired = (near + got.astype(F32)).astype(BF16).reshape(4, 2, half, -1)
    by_y = to_y(jnp.concatenate([paired[2, 0], paired[3, 0]])).astype(F32)
    by_x = to_x(jnp.concatenate([paired[1, 1], paired[3, 1]])).astype(F32)
    own_first = paired[0, 0].astype(F32) + by_y[:half]
    own_second = paired[0, 1].astype(F32) + by_x[:half]
    x_first = (paired[1, 0].astype(F32) + by_y[half:]).astype(BF16)
    y_second = (paired[2, 1].astype(F32) + by_x[half:]).astype(BF16)
    return jnp.concatenate(
        [own_first + to_x(x_first).astype(F32), own_second + to_y(y_second).astype(F32)]
    )


def ring_next(values):
    total = lax.axis_size("z")
    return lax.ppermute(values, "z", [(i, (i + 1) % total) for i in range(total)])


def ring_gather(block):
    total = lax.axis_size("z")
    place = lax.axis_index("z")
    rows = block.shape[0]
    whole = jnp.zeros((total * rows, block.shape[1]), block.dtype)
    current = block
    whole = lax.dynamic_update_slice(whole, current, (place * rows, 0))
    for step in range(1, total):
        current = ring_next(current)
        owner = lax.rem(place - step + total, total)
        whole = lax.dynamic_update_slice(whole, current, (owner * rows, 0))
    return whole, current


def ring_outer(left, right):
    total = lax.axis_size("z")
    place = lax.axis_index("z")
    columns = left.shape[1] // total
    running = None
    for step in range(total):
        owner = lax.rem(place + 2 * total - 1 - step, total)
        piece = lax.dynamic_slice(left, (0, owner * columns), (left.shape[0], columns))
        term = outer_sum(piece, right)
        if running is not None:
            term = term + ring_next(running).astype(F32)
        running = term.astype(BF16)
    return running


def to_plane(values):
    pieces = values.reshape(-1, values.shape[2])
    return lax.all_to_all(pieces, ("y", "x"), split_axis=0, concat_axis=0, tiled=True)


def spread(weight):
    rows, columns = weight.shape
    return weight.reshape(rows, 4, columns // 4).transpose(1, 0, 2).astype(BF16)


def from_plane(block):
    rows = block.shape[0] // 4
    got = lax.all_to_all(block, ("y", "x"), split_axis=0, concat_axis=0, tiled=True)
    return got.reshape(4, rows, block.shape[1])


def gathered(block):
    return block.transpose(1, 0, 2).reshape(block.shape[1], -1).astype(F32)


def turn(values, cos_rows, sin_rows):
    return values * cos_rows + pltpu.roll(values, HEAD_DIM // 2, 1) * sin_rows


def visible_of(places):
    size = places.shape[0]
    row = lax.broadcasted_iota(jnp.int32, (size, size), 0)
    column = lax.broadcasted_iota(jnp.int32, (size, size), 1)
    return (column <= row) & (row - column <= places)


def soft_of(queries, keys, visible):
    scores = project_t(queries, keys) * (1.0 / math.sqrt(HEAD_DIM))
    scores = jnp.where(visible, scores, NEG_LARGE)
    weights = jnp.exp(scores - jnp.max(scores, axis=1, keepdims=True))
    return weights / jnp.sum(weights, axis=1, keepdims=True)


def attend_kernel(lin_ref, cos_ref, sin_ref, place_ref, low_ref, out_ref):
    width = out_ref.shape[1]
    cos_rows, sin_rows = cos_ref[...], sin_ref[...]
    visible = visible_of(place_ref[...])
    for start in range(0, width, HEAD_DIM):
        here = slice(start, start + HEAD_DIM)
        key_at = slice(width + start, width + start + HEAD_DIM)
        value_at = slice(2 * width + start, 2 * width + start + HEAD_DIM)
        queries = turn(lin_ref[:, here], cos_rows, sin_rows).astype(BF16)
        keys = turn(lin_ref[:, key_at], cos_rows, sin_rows).astype(BF16)
        values = lin_ref[:, value_at].astype(BF16)
        low_ref[:, here] = queries
        low_ref[:, key_at] = keys
        low_ref[:, value_at] = values
        soft = soft_of(queries, keys, visible).astype(BF16)
        out_ref[:, here] = project(soft, values).astype(BF16)


def attend_back_kernel(low_ref, grad_ref, cos_ref, sin_ref, place_ref, out_ref):
    width = grad_ref.shape[1]
    cos_rows, sin_rows = cos_ref[...], -sin_ref[...]
    visible = visible_of(place_ref[...])
    scale = 1.0 / math.sqrt(HEAD_DIM)
    for start in range(0, width, HEAD_DIM):
        here = slice(start, start + HEAD_DIM)
        key_at = slice(width + start, width + start + HEAD_DIM)
        value_at = slice(2 * width + start, 2 * width + start + HEAD_DIM)
        queries, keys, values = low_ref[:, here], low_ref[:, key_at], low_ref[:, value_at]
        grad = grad_ref[:, here]
        soft = soft_of(queries, keys, visible)
        grad_soft = project_t(grad, values)
        inner = jnp.sum(soft * grad_soft, axis=1, keepdims=True)
        grad_scores = (soft * (grad_soft - inner)).astype(BF16)
        grad_query = project(grad_scores, keys) * scale
        grad_key = outer_sum(grad_scores, queries) * scale
        out_ref[:, here] = turn(grad_query, cos_rows, sin_rows).astype(BF16)
        out_ref[:, key_at] = turn(grad_key, cos_rows, sin_rows).astype(BF16)
        out_ref[:, value_at] = outer_sum(soft.astype(BF16), grad).astype(BF16)


def row_spec(rows, columns):
    return pl.BlockSpec((rows, columns), lambda i: (i, 0))


def attend(lin, cos_rows, sin_rows, places, block):
    rows, width = lin.shape[0], lin.shape[1] // 3
    return pl.pallas_call(
        attend_kernel,
        grid=(rows // block,),
        in_specs=[
            row_spec(block, 3 * width),
            row_spec(block, HEAD_DIM),
            row_spec(block, HEAD_DIM),
            row_spec(block, 1),
        ],
        out_specs=[row_spec(block, 3 * width), row_spec(block, width)],
        out_shape=[
            jax.ShapeDtypeStruct((rows, 3 * width), BF16),
            jax.ShapeDtypeStruct((rows, width), BF16),
        ],
        cost_estimate=pl.CostEstimate(
            flops=4 * rows * block * width,
            bytes_accessed=rows * (20 * width + 1024),
            transcendentals=rows * block * width // HEAD_DIM,
        ),
        name="attend",
    )(lin, cos_rows, sin_rows, places)


def attend_back(low, grad, cos_rows, sin_rows, places, block):
    rows, width = grad.shape
    return pl.pallas_call(
        attend_back_kernel,
        grid=(rows // block,),
        in_specs=[
            row_spec(block, 3 * width),
            row_spec(block, width),
            row_spec(block, HEAD_DIM),
            row_spec(block, HEAD_DIM),
            row_spec(block, 1),
        ],
        out_specs=row_spec(block, 3 * width),
        out_shape=jax.ShapeDtypeStruct((rows, 3 * width), BF16),
        cost_estimate=pl.CostEstimate(
            flops=10 * rows * block * width,
            bytes_accessed=rows * (14 * width + 1024),
            transcendentals=rows * block * width // HEAD_DIM,
        ),
        name="attend_back",
    )(low, grad, cos_rows, sin_rows, places)


def plane_places(segment_ids):
    segments = lax.all_gather(segment_ids, ("y", "x"), axis=0)
    groups, size = segments.shape
    numbers = jnp.arange(SEGS, dtype=jnp.int32)
    starts = jnp.sum((segments[:, :, None] < numbers).astype(jnp.int32), axis=1)
    onehot = segments[:, :, None] == numbers
    offset = jnp.sum(jnp.where(onehot, starts[:, None, :], 0), axis=2)
    places = jnp.arange(size, dtype=jnp.int32)[None, :] - offset
    places = places.reshape(2, 2, 2, size // 2)
    places = jnp.where(lax.axis_index("y") == 1, places[::-1], places)
    places = jnp.where(lax.axis_index("x") == 1, places[:, ::-1], places)
    places = jnp.where(lax.axis_index("c") == 1, places[:, :, ::-1], places)
    return places.transpose(2, 0, 1, 3).reshape(-1, 1)


def after(values, *gates):
    return lax.optimization_barrier((values,) + gates)[0]


EVERY = ("z", "y", "x", "c")


def exchange(rows):
    return lax.all_to_all(rows, EVERY, split_axis=0, concat_axis=0, tiled=True)


def on_device(
    tokens_in,
    cotangent,
    segment_ids,
    destination,
    source,
    w_query,
    w_key,
    w_value,
    w_out,
    w_gate,
    w_up,
    w_down,
):
    tok_rows = tokens_in.shape[0]
    devices = lax.axis_size(EVERY)
    per_peer = tok_rows // devices
    row_index = jnp.arange(tok_rows, dtype=jnp.int32)
    peer_to = destination // tok_rows
    ahead_rows = (peer_to[None, :] == peer_to[:, None]) & (
        destination[None, :] < destination[:, None]
    )
    send_slot = peer_to * per_peer + jnp.sum(ahead_rows.astype(jnp.int32), axis=1)
    peer_from = source // tok_rows
    before = (peer_from[None, :] == peer_from[:, None]) & (row_index[None, :] < row_index[:, None])
    recv_slot = peer_from * per_peer + jnp.sum(before.astype(jnp.int32), axis=1)
    send_pick = (send_slot[:, None] == row_index[None, :]).astype(BF16)
    recv_pick = (recv_slot[:, None] == row_index[None, :]).astype(BF16)

    arrived = project(recv_pick, exchange(outer_sum(send_pick, tokens_in).astype(BF16)))
    upstream_low = project(
        recv_pick, exchange(outer_sum(send_pick, cotangent).astype(BF16))
    ).astype(BF16)
    upstream = upstream_low.astype(F32)

    attention_block = to_plane(
        jnp.concatenate([spread(w_query), spread(w_key), spread(w_value), spread(w_out.T)], axis=2)
    )
    forward_block = to_plane(jnp.concatenate([spread(w_gate), spread(w_up)], axis=2))
    down_block = to_plane(spread(w_down.T))
    attention_w, attention_last = ring_gather(attention_block)
    forward_w, forward_last = ring_gather(after(forward_block, attention_last))
    down_w, _ = ring_gather(after(down_block, forward_last))
    head_width = attention_w.shape[1] // 4
    hidden_width = down_w.shape[1]
    qkv_w = attention_w[:, : 3 * head_width]
    out_w = attention_w[:, 3 * head_width :]

    places = plane_places(segment_ids)
    half_dim = HEAD_DIM // 2
    frequency = jnp.exp(
        -jnp.arange(half_dim, dtype=F32) * (2.0 * math.log(10000.0) / HEAD_DIM)
    )
    angles = places.astype(F32) * frequency[None, :]
    cos_half, sin_half = jnp.cos(angles), jnp.sin(angles)
    cos_rows = jnp.concatenate([cos_half, cos_half], axis=1)
    sin_rows = jnp.concatenate([-sin_half, sin_half], axis=1)

    normed_one, scale_one = norm_parts(arrived)
    seen_one = plane_gather(normed_one.astype(BF16))
    total_rows = seen_one.shape[0]
    middle_row = total_rows // 2
    qkv_lin = project(seen_one, qkv_w)
    qkv_low, attended = attend(qkv_lin, cos_rows, sin_rows, places, tok_rows)
    middle = arrived + plane_scatter(
        project_t(attended[middle_row:], out_w), project_t(attended[:middle_row], out_w)
    )
    normed_two, scale_two = norm_parts(middle)
    seen_two = plane_gather(normed_two.astype(BF16))
    grad_two_all = plane_gather(upstream_low)

    gate_lin = project(seen_two, forward_w[:, :hidden_width])
    up_lin = project(seen_two, forward_w[:, hidden_width:])
    sigmoid = jax.nn.sigmoid(gate_lin)
    hidden = (gate_lin * sigmoid * up_lin).astype(BF16)
    summed_down = from_plane(ring_outer(grad_two_all, hidden))
    output = middle + plane_scatter(
        project_t(hidden[middle_row:], down_w), project_t(hidden[:middle_row], down_w)
    )
    grad_hidden = project(grad_two_all, down_w)
    grad_gate = grad_hidden * up_lin * (sigmoid * (1.0 + gate_lin * (1.0 - sigmoid)))
    grad_up = grad_hidden * (gate_lin * sigmoid)
    grad_both = jnp.concatenate([grad_gate.astype(BF16), grad_up.astype(BF16)], axis=1)
    grad_normed_two = plane_scatter(
        project_t(grad_both[middle_row:], forward_w), project_t(grad_both[:middle_row], forward_w)
    )
    summed_forward = from_plane(ring_outer(seen_two, grad_both))
    grad_middle = upstream + norm_back(normed_two, scale_two, grad_normed_two)
    grad_one_all = plane_gather(grad_middle.astype(BF16))
    grad_attended = project(grad_one_all, out_w).astype(BF16)
    grad_qkv = attend_back(qkv_low, grad_attended, cos_rows, sin_rows, places, tok_rows)
    grad_normed_one = plane_scatter(
        project_t(grad_qkv[middle_row:], qkv_w), project_t(grad_qkv[:middle_row], qkv_w)
    )
    grad_inputs = grad_middle + norm_back(normed_one, scale_one, grad_normed_one)
    summed_out = from_plane(ring_outer(grad_one_all, attended))
    summed_qkv = from_plane(ring_outer(seen_one, grad_qkv))

    def give_back(rows):
        packed = outer_sum(recv_pick, rows.astype(BF16)).astype(BF16)
        return project(send_pick, exchange(packed))

    return (
        give_back(output),
        give_back(grad_inputs),
        gathered(summed_qkv[:, :, :head_width]),
        gathered(summed_qkv[:, :, head_width : 2 * head_width]),
        gathered(summed_qkv[:, :, 2 * head_width :]),
        gathered(summed_out).T,
        gathered(summed_forward[:, :, :hidden_width]),
        gathered(summed_forward[:, :, hidden_width:]),
        gathered(summed_down).T,
    )


def solution(mesh):
    groups, cores = mesh.shape["dp"], mesh.shape["tensor"]
    whole = Mesh(mesh.devices.reshape(groups // 4, 2, 2, cores), EVERY)
    rows = P(EVERY, None)
    tall = P(("z", "y", "x"), "c")
    wide = P("c", ("z", "y", "x"))
    in_specs = (
        rows,
        rows,
        P(("z", "y", "x")),
        P(EVERY),
        P(EVERY),
        tall,
        tall,
        tall,
        wide,
        tall,
        tall,
        wide,
    )
    out_specs = (rows, rows, tall, tall, tall, wide, tall, tall, wide)
    return jax.shard_map(
        on_device, mesh=whole, in_specs=in_specs, out_specs=out_specs, check_vma=False
    )
```

time: 4140 us -> 1030 us (0.25)
  waiting for transfers between devices: 3650 us -> 468 us
  starting transfers between devices: 23.5 us -> 104 us
  local copies, waits for them, and re-layouts: 63.7 us -> 107 us
    reduce_scatter x11 -> x0, waiting for transfers between devices: 2640 us -> none  [the longest x1 692 us: on_device(): lax.psum_scatter(grad_up_w, 'dp', scatter_dimension=0, tiled=True)]
    all_gather x11 -> x0, waiting for transfers between devices: 862 us -> none  [the longest x1 249 us: on_device(): lax.all_gather(w_down.astype(jnp.bfloat16), 'dp', axis=1, tiled=True)]
    ppermute x0 -> x61, waiting for transfers between devices: none -> 403 us  [the longest x21 236 us: ring_next(): lax.ppermute(values, 'z', [(i, (i + 1) % total) for i in range(total)])]
    all_to_all x3 -> x11, waiting for transfers between devices: 149 us -> 64.4 us  [the longest x4 54.9 us: exchange(): return lax.all_to_all(rows, EVERY, split_axis=0, concat_axis=0, tiled=True)]
    ppermute x0 -> x61, starting transfers between devices: none -> 52.1 us  [the longest x16 23.6 us: to_x(): return lax.ppermute(values, 'x', FLIP)]
    all_to_all x1 -> x0, blocking collectives: 49.5 us -> none  [on_device(): lax.all_to_all(packed_grad, ('dp', 'tensor'), split_axis=0, concat_axis=0...]
    dot_general x31 -> x8, matrix products: 97.2 us -> 66.1 us  [project_t(): lax.dot_general(left, right, (((1,), (1,)), ((), ())), preferred_element_...]
    dot_general x23 -> x20, matrix products: 94.7 us -> 98.4 us  [outer_sum(): lax.dot_general(left, right, (((0,), (0,)), ((), ())), preferred_element_...]
  transfers between devices with their start and end apart: 25 -> 72, of which waited for: 19 -> 36; matrix products, arithmetic and copies ran while one was open for 7% -> 31% of each run, Pallas kernels for 0% -> 2%
where the time goes in v1:
time: 1030 us; the launch traced here: 1020 us
  waiting for transfers between devices  468 us (45%)
  matrix products  238 us (23%)
  local copies, waits for them, and re-layouts  107 us (10%)
  starting transfers between devices  104 us (10%)
  other arithmetic  59.8 us (6%)
  Pallas kernels  24.4 us (2%)
  blocking collectives  16.4 us (2%)
    ppermute x21, waiting for transfers between devices, ring_next(): lax.ppermute(values, 'z', [(i, (i + 1) % total) for i in range(total)])  236 us
    ppermute x16, waiting for transfers between devices, to_x(): return lax.ppermute(values, 'x', FLIP)  118 us
    dot_general x20, matrix products, outer_sum(): lax.dot_general(left, right, (((0,), (0,)), ((), ())), preferred_element_...  98.4 us
    dot_general x9, matrix products, project(): return jnp.dot(left, right, preferred_element_type=F32)  73.8 us
    dot_general x8, matrix products, project_t(): lax.dot_general(left, right, (((1,), (1,)), ((), ())), preferred_element_...  66.1 us
    all_to_all x4, waiting for transfers between devices, exchange(): return lax.all_to_all(rows, EVERY, split_axis=0, concat_axis=0, tiled=True)  54.9 us
    unnamed x194, local copies, waits for them, and re-layouts  53.5 us
    ppermute x16, waiting for transfers between devices, to_y(): return lax.ppermute(values, 'y', FLIP)  47.9 us
  transfers between devices with their start and end apart: 72, of which 36 were waited for; matrix products, arithmetic and copies ran while one was open for 31% of the time, Pallas kernels for 2%

profile of v1, /device:TPU:0, one launch (start us, length us, event | category | flops | bytes accessed | tf_op | source)
XLA Modules:
  0.0 1020.5 jit_solution(12779644565171720754)
XLA Ops:
  4.6 7.3 all-to-all-start
  12.2 26.0 %all-to-all-done = bf16[32,8,2048]{2,1,0:T(8,128)(2,1)S(1)} async-done(((bf16[32,8,2048]{2,1,0:T(8,128)(2,1)}), bf16[32,8,2048]{2,1,0:T(8,128)(2,1)S(1)}, u32[]{:S(2)}, u32[]{:S(2)}) %all-to-all-start) | async-done | bytes 1048608 | tf_op jit(solution)/shard_map/all_to_all | solution.py:282
  55.2 16.4 %all-gather.1 = s32[4,1,512]{2,1,0:T(1,128)S(1)} all-gather(s32[1,1,512]{2,1,0:T(1,128)S(1)} %bitcast.279), channel_id=2, replica_groups=mesh['z'=4,'y'=2,'x'=2,'c'=2] {'y','x'}, dimensions={0}, use_global_device_ids=true | all-gather | bytes 10240 | tf_op jit(solution)/shard_map/all_gather | solution.py:260
  83.1 8.7 collective-permute-done
  94.9 15.7 %collective-permute-done.2 = bf16[256,2048]{1,0:T(8,128)(2,1)S(1)} collective-permute-done((bf16[256,2048]{1,0:T(8,128)(2,1)S(1)}, bf16[256,2048]{1,0:T(8,128)(2,1)S(1)}, u32[]{:S(2)}, u32[]{:S(2)}) %collective-permute-start.2) | collective-permute-done | bytes 1048608 | tf_op jit(solution)/shard_map/ppermute | solution.py:46
  124.8 25.2 %collective-permute-done.5 = bf16[512,1024]{1,0:T(8,128)(2,1)} collective-permute-done((bf16[512,1024]{1,0:T(8,128)(2,1)S(1)}, bf16[512,1024]{1,0:T(8,128)(2,1)}, u32[]{:S(2)}, u32[]{:S(2)}) %collective-permute-start.5) | collective-permute-done | bytes 1048608 | tf_op jit(solution)/shard_map/ppermute | solution.py:97
  158.0 18.7 %collective-permute-done.6 = bf16[512,1024]{1,0:T(8,128)(2,1)S(1)} collective-permute-done((bf16[512,1024]{1,0:T(8,128)(2,1)}, bf16[512,1024]{1,0:T(8,128)(2,1)S(1)}, u32[]{:S(2)}, u32[]{:S(2)}) %collective-permute-start.6) | collective-permute-done | bytes 1048608 | tf_op jit(solution)/shard_map/ppermute | solution.py:97
  178.6 24.3 %collective-permute-done.7 = bf16[512,1024]{1,0:T(8,128)(2,1)S(1)} collective-permute-done((bf16[512,1024]{1,0:T(8,128)(2,1)S(1)}, bf16[512,1024]{1,0:T(8,128)(2,1)S(1)}, u32[]{:S(2)}, u32[]{:S(2)}) %collective-permute-start.7) | collective-permute-done | bytes 1048608 | tf_op jit(solution)/shard_map/ppermute | solution.py:97
  207.1 8.7 fusion.22.lin_ref
  215.7 11.5 %attend.1 = (bf16[2048,768]{1,0:T(8,128)(2,1)}, bf16[2048,256]{1,0:T(8,128)(2,1)}) custom-call(f32[2048,768]{1,0:T(8,128)} %fusion.22.lin_ref, f32[2048,128]{1,0:T(8,128)} %get-tuple-element.96.cos_ref, f32[2048,128]{1,0:T(8,128)} %get-tuple-element.97.sin_ref, s32[2048,1]{1,0:T(8,128)} %reshape.243.place_ref), custom_call_target="tpu_custom_call" | custom-call | flops 536870912 | bytes 12582912 | tf_op jit(solution)/shard_map/attend/pallas_call | solution.py:213
  242.8 19.6 %all-to-all-done.5 = bf16[32,8,2048]{2,1,0:T(8,128)(2,1)S(1)} async-done(((bf16[32,8,2048]{2,1,0:T(8,128)(2,1)}), bf16[32,8,2048]{2,1,0:T(8,128)(2,1)S(1)}, u32[]{:S(2)}, u32[]{:S(2)}) %all-to-all-start.5) | async-done | bytes 1048608 | tf_op jit(solution)/shard_map/all_to_all | solution.py:282
  286.9 6.6 collective-permute-done.30
  300.0 19.8 %collective-permute-done.18 = bf16[512,2048]{1,0:T(8,128)(2,1)} collective-permute-done((bf16[512,2048]{1,0:T(8,128)(2,1)}, bf16[512,2048]{1,0:T(8,128)(2,1)}, u32[]{:S(2)}, u32[]{:S(2)}) %collective-permute-start.18) | collective-permute-done | bytes 2097184 | tf_op jit(solution)/shard_map/ppermute | solution.py:97
  325.6 20.5 %collective-permute-done.11 = bf16[256,2048]{1,0:T(8,128)(2,1)S(1)} collective-permute-done((bf16[256,2048]{1,0:T(8,128)(2,1)S(1)}, bf16[256,2048]{1,0:T(8,128)(2,1)S(1)}, u32[]{:S(2)}, u32[]{:S(2)}) %collective-permute-start.11) | collective-permute-done | bytes 1048608 | tf_op jit(solution)/shard_map/ppermute | solution.py:46
  346.3 8.9 collective-permute-done.10
  359.7 8.1 collective-permute-done.19
  374.3 40.5 %collective-permute-done.20 = bf16[512,2048]{1,0:T(8,128)(2,1)S(1)} collective-permute-done((bf16[512,2048]{1,0:T(8,128)(2,1)S(1)}, bf16[512,2048]{1,0:T(8,128)(2,1)S(1)}, u32[]{:S(2)}, u32[]{:S(2)}) %collective-permute-start.20) | collective-permute-done | bytes 2097184 | tf_op jit(solution)/shard_map/ppermute | solution.py:97
  417.9 11.8 %collective-permute-done.13 = bf16[128,2048]{1,0:T(8,128)(2,1)S(1)} collective-permute-done((bf16[128,2048]{1,0:T(8,128)(2,1)S(1)}, bf16[128,2048]{1,0:T(8,128)(2,1)S(1)}, u32[]{:S(2)}, u32[]{:S(2)}) %collective-permute-start.13) | collective-permute-done | bytes 524320 | tf_op jit(solution)/shard_map/ppermute | solution.py:46
  440.6 7.3 collective-permute-done.15
  470.0 16.5 %collective-permute-done.23 = bf16[512,1024]{1,0:T(8,128)(2,1)S(1)} collective-permute-done((bf16[512,1024]{1,0:T(8,128)(2,1)}, bf16[512,1024]{1,0:T(8,128)(2,1)S(1)}, u32[]{:S(2)}, u32[]{:S(2)}) %collective-permute-start.23) | collective-permute-done | bytes 1048608 | tf_op jit(solution)/shard_map/ppermute | solution.py:97
  492.9 13.6 %fusion.7 = f32[2048,1024]{0,1:T(8,128)} fusion(bf16[2048,2048]{1,0:T(8,128)(2,1)} %constant_dynamic-update-slice_fusion.10, bf16[2048,2048]{1,0:T(8,128)(2,1)S(1)} %constant_dynamic-update-slice_fusion.32), kind=kOutput, calls=%fused_computation.18 | convolution fusion | flops 8589934592 | bytes 20971520 | tf_op jit(solution)/shard_map/dot_general | solution.py:21
  506.5 13.7 %fusion.9 = f32[2048,1024]{0,1:T(8,128)} fusion(bf16[2048,2048]{1,0:T(8,128)(2,1)} %constant_dynamic-update-slice_fusion.10, bf16[2048,2048]{1,0:T(8,128)(2,1)S(1)} %constant_dynamic-update-slice_fusion.32), kind=kOutput, calls=%fused_computation.20 | convolution fusion | flops 8589934592 | bytes 20971520 | tf_op jit(solution)/shard_map/dot_general | solution.py:21
  520.2 22.7 %multiply_convert_fusion = (bf16[2048,1024]{0,1:T(8,128)(2,1)}, bf16[2048,1024]{0,1:T(8,128)(2,1)}, bf16[2048,1024]{0,1:T(8,128)(2,1)}) fusion(f32[2048,1024]{0,1:T(8,128)} %fusion.9, f32[2048,1024]{0,1:T(8,128)} %fusion.7, bf16[2048,2048]{1,0:T(8,128)(2,1)} %constant_dynamic-update-slice_fusion.17, bf16[2048,1024]{1,0:T(8,128)(2,1)} %copy-done.30), kind=kOutput, calls=%fused_computation.7 | convolution fusion | flops 8621391872 | bytes 41943040 | tf_op jit(solution)/shard_map/dot_general | solution.py:21
  542.9 14.6 %fusion.11 = bf16[1024,2048]{1,0:T(8,128)(2,1)} fusion(bf16[2048,2048]{1,0:T(8,128)(2,1)} %copy-done.21, bf16[2048,1024]{0,1:T(8,128)(2,1)} %get-tuple-element.33, bf16[2048,1024]{0,1:T(8,128)(2,1)} %get-tuple-element.32), kind=kOutput, calls=%fused_computation.28 | convolution fusion | flops 8600420352 | bytes 20971520 | tf_op jit(solution)/shard_map/dot_general | solution.py:25
  557.7 6.3 fusion.59
  565.1 13.0 %add_convert_fusion.1 = bf16[1024,2048]{1,0:T(8,128)(2,1)} fusion(bf16[1024,2048]{1,0:T(8,128)(2,1)} %collective-permute-done.34, bf16[2048,2048]{1,0:T(8,128)(2,1)S(1)} %copy-done.22, bf16[2048,1024]{0,1:T(8,128)(2,1)} %get-tuple-element.33, bf16[2048,1024]{0,1:T(8,128)(2,1)} %get-tuple-element.32), kind=kOutput, calls=%fused_computation.6 | convolution fusion | flops 8604614656 | bytes 25165824 | tf_op jit(solution)/shard_map/dot_general | solution.py:25
  581.0 8.1 convolution_convert_fusion.2
  591.0 14.4 %collective-permute-done.35 = bf16[256,2048]{1,0:T(8,128)(2,1)S(1)} collective-permute-done((bf16[256,2048]{1,0:T(8,128)(2,1)S(1)}, bf16[256,2048]{1,0:T(8,128)(2,1)S(1)}, u32[]{:S(2)}, u32[]{:S(2)}) %collective-permute-start.35) | collective-permute-done | bytes 1048608 | tf_op jit(solution)/shard_map/ppermute | solution.py:50
  607.5 8.8 convolution_convert_fusion.3
  616.6 9.1 collective-permute-done.36
  631.8 7.6 collective-permute-done.38
  645.1 21.9 %collective-permute-done.55 = bf16[512,2048]{1,0:T(8,128)(2,1)} collective-permute-done((bf16[512,2048]{1,0:T(8,128)(2,1)}, bf16[512,2048]{1,0:T(8,128)(2,1)}, u32[]{:S(2)}, u32[]{:S(2)}) %collective-permute-start.55) | collective-permute-done | bytes 2097184 | tf_op jit(solution)/shard_map/ppermute | solution.py:97
  667.0 10.7 %add_convert_fusion.6 = bf16[512,2048]{1,0:T(8,128)(2,1)} fusion(bf16[512,2048]{1,0:T(8,128)(2,1)} %collective-permute-done.55, bf16[2048,2048]{1,0:T(8,128)(2,1)} %constant_dynamic-update-slice_fusion.10, s32[]{:T(128)S(6)} %select_n.91, bf16[2048,1024]{0,1:T(8,128)(2,1)} %get-tuple-element.32, bf16[2048,1024]{0,1:T(8,128)(2,1)} %get-tuple-element.33), kind=kOutput, calls=%fused_computation.24 | convolution fusion | flops 4314890240 | bytes 14680068 | tf_op jit(solution)/shard_map/dot_general | solution.py:29
  679.7 9.6 collective-permute-done.59
  704.3 30.1 %collective-permute-done.56 = bf16[512,2048]{1,0:T(8,128)(2,1)} collective-permute-done((bf16[512,2048]{1,0:T(8,128)(2,1)}, bf16[512,2048]{1,0:T(8,128)(2,1)}, u32[]{:S(2)}, u32[]{:S(2)}) %collective-permute-start.56) | collective-permute-done | bytes 2097184 | tf_op jit(solution)/shard_map/ppermute | solution.py:97
  734.4 10.5 %add_convert_fusion.5 = bf16[512,2048]{1,0:T(8,128)(2,1)} fusion(bf16[512,2048]{1,0:T(8,128)(2,1)} %collective-permute-done.56, bf16[2048,2048]{1,0:T(8,128)(2,1)} %constant_dynamic-update-slice_fusion.10, s32[]{:T(128)S(6)} %select_n.90, bf16[2048,1024]{0,1:T(8,128)(2,1)} %get-tuple-element.32, bf16[2048,1024]{0,1:T(8,128)(2,1)} %get-tuple-element.33), kind=kOutput, calls=%fused_computation.23 | convolution fusion | flops 4314890240 | bytes 14680068 | tf_op jit(solution)/shard_map/dot_general | solution.py:29
  745.1 8.6 add_convert_fusion.2
  764.1 13.0 %attend_back.1 = bf16[2048,768]{1,0:T(8,128)(2,1)} custom-call(bf16[2048,768]{1,0:T(8,128)(2,1)} %get-tuple-element.16.low_ref, bf16[2048,256]{1,0:T(8,128)(2,1)} %convolution_convert_fusion.9.grad_ref, f32[2048,128]{1,0:T(8,128)} %get-tuple-element.96.cos_ref, f32[2048,128]{1,0:T(8,128)} %get-tuple-element.97.sin_ref, s32[2048,1]{1,0:T(8,128)} %reshape.243.place_ref), custom_call_target="tpu_custom_call" | custom-call | flops 1342177280 | bytes 9437184 | tf_op jit(solution)/shard_map/attend_back/pallas_call | solution.py:238
  777.1 7.8 convolution_convert_fusion.1
  802.7 9.4 collective-permute-done.27
  812.4 11.1 %collective-permute-done.26 = bf16[128,2048]{1,0:T(8,128)(2,1)} collective-permute-done((bf16[128,2048]{1,0:T(8,128)(2,1)}, bf16[128,2048]{1,0:T(8,128)(2,1)}, u32[]{:S(2)}, u32[]{:S(2)}) %collective-permute-start.26) | collective-permute-done | bytes 524320 | tf_op jit(solution)/shard_map/ppermute | solution.py:46
  826.9 9.4 add_convert_fusion.4
  862.5 6.1 all-to-all-start.9
  882.9 15.0 %collective-permute-done.45 = bf16[256,2048]{1,0:T(8,128)(2,1)} collective-permute-done((bf16[256,2048]{1,0:T(8,128)(2,1)}, bf16[256,2048]{1,0:T(8,128)(2,1)}, u32[]{:S(2)}, u32[]{:S(2)}) %collective-permute-start.45) | collective-permute-done | bytes 1048608 | tf_op jit(solution)/shard_map/ppermute | solution.py:50
  923.9 10.5 %collective-permute-done.46 = bf16[128,2048]{1,0:T(8,128)(2,1)} collective-permute-done((bf16[128,2048]{1,0:T(8,128)(2,1)}, bf16[128,2048]{1,0:T(8,128)(2,1)}, u32[]{:S(2)}, u32[]{:S(2)}) %collective-permute-start.46) | collective-permute-done | bytes 524320 | tf_op jit(solution)/shard_map/ppermute | solution.py:46
  940.2 14.1 %collective-permute-done.51 = bf16[512,768]{1,0:T(8,128)(2,1)S(1)} collective-permute-done((bf16[512,768]{1,0:T(8,128)(2,1)S(1)}, bf16[512,768]{1,0:T(8,128)(2,1)S(1)}, u32[]{:S(2)}, u32[]{:S(2)}) %collective-permute-start.51) | collective-permute-done | bytes 786464 | tf_op jit(solution)/shard_map/ppermute | solution.py:97
  983.9 7.1 all-to-all-start.6
  1008.0 9.3 all-to-all-done.6
  (453 shorter events, 360.0 us)
Async XLA Ops:
  4.6 33.5 %all-to-all-start = ((bf16[32,8,2048]{2,1,0:T(8,128)(2,1)}), bf16[32,8,2048]{2,1,0:T(8,128)(2,1)S(1)}, u32[]{:S(2)}, u32[]{:S(2)}) async-start(bf16[32,8,2048]{2,1,0:T(8,128)(2,1)} %fusion.16), calls=%async_computation | async-start | bytes 2097152 | tf_op jit(solution)/shard_map/all_to_all | solution.py:282
  41.6 35.7 %collective-permute-start.1 = (bf16[128,2048]{1,0:T(8,128)(2,1)}, bf16[128,2048]{1,0:T(8,128)(2,1)}, u32[]{:S(2)}, u32[]{:S(2)}) collective-permute-start(bf16[128,2048]{1,0:T(8,128)(2,1)} %get-tuple-element.77), channel_id=1, source_target_pairs={{0,4},{4,0},{1,5},{5,1},{2,6},{6,2},{3,7},{7,3},{8,12},{12,8},{9,1... | collective-permute-start | bytes 1572872 | tf_op jit(solution)/shard_map/ppermute | solution.py:50
  50.9 65.5 %all-to-all-start.1 = ((bf16[4,128,1024]{1,2,0:T(8,128)(2,1)}), bf16[4,128,1024]{1,2,0:T(8,128)(2,1)}, u32[]{:S(2)}, u32[]{:S(2)}) async-start(bf16[4,128,1024]{1,2,0:T(8,128)(2,1)} %pad_maximum_fusion.6), calls=%async_computation.1 | async-start | bytes 2097152 | tf_op jit(solution)/shard_map/all_to_all | solution.py:131
  78.6 32.0 %collective-permute-start.2 = (bf16[256,2048]{1,0:T(8,128)(2,1)S(1)}, bf16[256,2048]{1,0:T(8,128)(2,1)S(1)}, u32[]{:S(2)}, u32[]{:S(2)}) collective-permute-start(bf16[256,2048]{1,0:T(8,128)(2,1)S(1)} %pad_maximum_fusion.4), channel_id=1, source_target_pairs={{0,2},{2,0},{1,3},{3,1},{4,6},{6,4},{5,7},{7,5},{8,10},{10,8},{9,1... | collective-permute-start | bytes 3145736 | tf_op jit(solution)/shard_map/ppermute | solution.py:46
  116.3 86.7 %collective-permute-start.4 = (bf16[1024,2048]{1,0:T(8,128)(2,1)}, bf16[1024,2048]{1,0:T(8,128)(2,1)}, u32[]{:S(2)}, u32[]{:S(2)}) collective-permute-start(bf16[1024,2048]{1,0:T(8,128)(2,1)} %get-tuple-element.75), channel_id=1, source_target_pairs={{0,1},{1,0},{2,3},{3,2},{4,5},{5,4},{6,7},{7,6},{8,9},{9,8},{10,11... | collective-permute-start | bytes 12582920 | tf_op jit(solution)/shard_map/ppermute | solution.py:54
  116.4 117.1 %all-to-all-start.2 = ((bf16[4,128,2048]{1,2,0:T(8,128)(2,1)}), bf16[4,128,2048]{1,2,0:T(8,128)(2,1)}, u32[]{:S(2)}, u32[]{:S(2)}) async-start(bf16[4,128,2048]{1,2,0:T(8,128)(2,1)} %pad_maximum_fusion.1), calls=%async_computation.2 | async-start | bytes 4194304 | tf_op jit(solution)/shard_map/all_to_all | solution.py:131
  122.4 27.5 %collective-permute-start.5 = (bf16[512,1024]{1,0:T(8,128)(2,1)S(1)}, bf16[512,1024]{1,0:T(8,128)(2,1)}, u32[]{:S(2)}, u32[]{:S(2)}) collective-permute-start(bf16[512,1024]{1,0:T(8,128)(2,1)S(1)} %bitcast.242), channel_id=1, source_target_pairs={{0,8},{8,16},{16,24},{24,0},{1,9},{9,17},{17,25},{25,1},{2,10},{10... | collective-permute-start | bytes 3145736 | tf_op jit(solution)/shard_map/ppermute | solution.py:97
  150.0 26.8 %collective-permute-start.6 = (bf16[512,1024]{1,0:T(8,128)(2,1)}, bf16[512,1024]{1,0:T(8,128)(2,1)S(1)}, u32[]{:S(2)}, u32[]{:S(2)}) collective-permute-start(bf16[512,1024]{1,0:T(8,128)(2,1)} %collective-permute-done.5), channel_id=1, source_target_pairs={{0,8},{8,16},{16,24},{24,0},{1,9},{9,17},{17,25},{25,1},{2,10},{10... | collective-permute-start | bytes 3145736 | tf_op jit(solution)/shard_map/ppermute | solution.py:97
  232.0 42.7 %collective-permute-start.8 = (bf16[1024,2048]{1,0:T(8,128)(2,1)}, bf16[1024,2048]{1,0:T(8,128)(2,1)}, u32[]{:S(2)}, u32[]{:S(2)}) collective-permute-start(bf16[1024,2048]{1,0:T(8,128)(2,1)} %convolution_convert_fusion), channel_id=1, source_target_pairs={{0,1},{1,0},{2,3},{3,2},{4,5},{5,4},{6,7},{7,6},{8,9},{9,8},{10,11... | collective-permute-start | bytes 12582920 | tf_op jit(solution)/shard_map/ppermute | solution.py:54
  233.6 28.9 %all-to-all-start.5 = ((bf16[32,8,2048]{2,1,0:T(8,128)(2,1)}), bf16[32,8,2048]{2,1,0:T(8,128)(2,1)S(1)}, u32[]{:S(2)}, u32[]{:S(2)}) async-start(bf16[32,8,2048]{2,1,0:T(8,128)(2,1)} %fusion.18), calls=%async_computation.5 | async-start | bytes 2097152 | tf_op jit(solution)/shard_map/all_to_all | solution.py:282
  270.8 49.0 %collective-permute-start.18 = (bf16[512,2048]{1,0:T(8,128)(2,1)}, bf16[512,2048]{1,0:T(8,128)(2,1)}, u32[]{:S(2)}, u32[]{:S(2)}) collective-permute-start(bf16[512,2048]{1,0:T(8,128)(2,1)} %bitcast.27), channel_id=1, source_target_pairs={{0,8},{8,16},{16,24},{24,0},{1,9},{9,17},{17,25},{25,1},{2,10},{10... | collective-permute-start | bytes 6291464 | tf_op jit(solution)/shard_map/ppermute | solution.py:97
  282.6 39.3 %collective-permute-start.9 = (bf16[256,2048]{1,0:T(8,128)(2,1)}, bf16[256,2048]{1,0:T(8,128)(2,1)}, u32[]{:S(2)}, u32[]{:S(2)}) collective-permute-start(bf16[256,2048]{1,0:T(8,128)(2,1)} %pad_maximum_fusion.9), channel_id=1, source_target_pairs={{0,4},{4,0},{1,5},{5,1},{2,6},{6,2},{3,7},{7,3},{8,12},{12,8},{9,1... | collective-permute-start | bytes 3145736 | tf_op jit(solution)/shard_map/ppermute | solution.py:50
  294.8 29.9 %collective-permute-start.31 = (bf16[256,2048]{1,0:T(8,128)(2,1)S(1)}, bf16[256,2048]{1,0:T(8,128)(2,1)S(1)}, u32[]{:S(2)}, u32[]{:S(2)}) collective-permute-start(bf16[256,2048]{1,0:T(8,128)(2,1)S(1)} %pad_maximum_fusion.15), channel_id=1, source_target_pairs={{0,2},{2,0},{1,3},{3,1},{4,6},{6,4},{5,7},{7,5},{8,10},{10,8},{9,1... | collective-permute-start | bytes 3145736 | tf_op jit(solution)/shard_map/ppermute | solution.py:46
  297.6 59.4 %collective-permute-start.32 = (bf16[256,2048]{1,0:T(8,128)(2,1)S(1)}, bf16[256,2048]{1,0:T(8,128)(2,1)S(1)}, u32[]{:S(2)}, u32[]{:S(2)}) collective-permute-start(bf16[256,2048]{1,0:T(8,128)(2,1)S(1)} %pad_maximum_fusion.16), channel_id=1, source_target_pairs={{0,4},{4,0},{1,5},{5,1},{2,6},{6,2},{3,7},{7,3},{8,12},{12,8},{9,1... | collective-permute-start | bytes 3145736 | tf_op jit(solution)/shard_map/ppermute | solution.py:50
  319.8 48.0 %collective-permute-start.19 = (bf16[512,2048]{1,0:T(8,128)(2,1)}, bf16[512,2048]{1,0:T(8,128)(2,1)S(1)}, u32[]{:S(2)}, u32[]{:S(2)}) collective-permute-start(bf16[512,2048]{1,0:T(8,128)(2,1)} %collective-permute-done.18), channel_id=1, source_target_pairs={{0,8},{8,16},{16,24},{24,0},{1,9},{9,17},{17,25},{25,1},{2,10},{10... | collective-permute-start | bytes 6291464 | tf_op jit(solution)/shard_map/ppermute | solution.py:97
  319.9 26.2 %collective-permute-start.11 = (bf16[256,2048]{1,0:T(8,128)(2,1)S(1)}, bf16[256,2048]{1,0:T(8,128)(2,1)S(1)}, u32[]{:S(2)}, u32[]{:S(2)}) collective-permute-start(bf16[256,2048]{1,0:T(8,128)(2,1)S(1)} %pad_maximum_fusion.10), channel_id=1, source_target_pairs={{0,2},{2,0},{1,3},{3,1},{4,6},{6,4},{5,7},{7,5},{8,10},{10,8},{9,1... | collective-permute-start | bytes 3145736 | tf_op jit(solution)/shard_map/ppermute | solution.py:46
  323.5 31.7 %collective-permute-start.10 = (bf16[128,2048]{1,0:T(8,128)(2,1)S(1)}, bf16[128,2048]{1,0:T(8,128)(2,1)S(1)}, u32[]{:S(2)}, u32[]{:S(2)}) collective-permute-start(bf16[128,2048]{1,0:T(8,128)(2,1)S(1)} %fusion.115), channel_id=1, source_target_pairs={{0,2},{2,0},{1,3},{3,1},{4,6},{6,4},{5,7},{7,5},{8,10},{10,8},{9,1... | collective-permute-start | bytes 1572872 | tf_op jit(solution)/shard_map/ppermute | solution.py:46
  367.8 47.0 %collective-permute-start.20 = (bf16[512,2048]{1,0:T(8,128)(2,1)S(1)}, bf16[512,2048]{1,0:T(8,128)(2,1)S(1)}, u32[]{:S(2)}, u32[]{:S(2)}) collective-permute-start(bf16[512,2048]{1,0:T(8,128)(2,1)S(1)} %collective-permute-done.19), channel_id=1, source_target_pairs={{0,8},{8,16},{16,24},{24,0},{1,9},{9,17},{17,25},{25,1},{2,10},{10... | collective-permute-start | bytes 6291464 | tf_op jit(solution)/shard_map/ppermute | solution.py:97
  370.9 45.9 %collective-permute-start.14 = (bf16[128,2048]{1,0:T(8,128)(2,1)S(1)}, bf16[128,2048]{1,0:T(8,128)(2,1)S(1)}, u32[]{:S(2)}, u32[]{:S(2)}) collective-permute-start(bf16[128,2048]{1,0:T(8,128)(2,1)S(1)} %get-tuple-element.73), channel_id=1, source_target_pairs={{0,4},{4,0},{1,5},{5,1},{2,6},{6,2},{3,7},{7,3},{8,12},{12,8},{9,1... | collective-permute-start | bytes 1572872 | tf_op jit(solution)/shard_map/ppermute | solution.py:50
  374.3 86.9 %collective-permute-start.33 = (bf16[1024,2048]{1,0:T(8,128)(2,1)}, bf16[1024,2048]{1,0:T(8,128)(2,1)S(1)}, u32[]{:S(2)}, u32[]{:S(2)}) collective-permute-start(bf16[1024,2048]{1,0:T(8,128)(2,1)} %get-tuple-element.65), channel_id=1, source_target_pairs={{0,1},{1,0},{2,3},{3,2},{4,5},{5,4},{6,7},{7,6},{8,9},{9,8},{10,11... | collective-permute-start | bytes 12582920 | tf_op jit(solution)/shard_map/ppermute | solution.py:54
  416.9 31.0 %collective-permute-start.15 = (bf16[256,2048]{1,0:T(8,128)(2,1)S(1)}, bf16[256,2048]{1,0:T(8,128)(2,1)S(1)}, u32[]{:S(2)}, u32[]{:S(2)}) collective-permute-start(bf16[256,2048]{1,0:T(8,128)(2,1)S(1)} %pad_maximum_fusion.11), channel_id=1, source_target_pairs={{0,2},{2,0},{1,3},{3,1},{4,6},{6,4},{5,7},{7,5},{8,10},{10,8},{9,1... | collective-permute-start | bytes 3145736 | tf_op jit(solution)/shard_map/ppermute | solution.py:46
  452.4 38.2 %collective-permute-start.17 = (bf16[1024,2048]{1,0:T(8,128)(2,1)}, bf16[1024,2048]{1,0:T(8,128)(2,1)S(1)}, u32[]{:S(2)}, u32[]{:S(2)}) collective-permute-start(bf16[1024,2048]{1,0:T(8,128)(2,1)} %get-tuple-element.71), channel_id=1, source_target_pairs={{0,1},{1,0},{2,3},{3,2},{4,5},{5,4},{6,7},{7,6},{8,9},{9,8},{10,11... | collective-permute-start | bytes 12582920 | tf_op jit(solution)/shard_map/ppermute | solution.py:54
  564.0 63.1 %collective-permute-start.58 = (bf16[512,1024]{1,0:T(8,128)(2,1)}, bf16[512,1024]{1,0:T(8,128)(2,1)}, u32[]{:S(2)}, u32[]{:S(2)}) collective-permute-start(bf16[512,1024]{1,0:T(8,128)(2,1)} %fusion.59), channel_id=1, source_target_pairs={{0,8},{8,16},{16,24},{24,0},{1,9},{9,17},{17,25},{25,1},{2,10},{10... | collective-permute-start | bytes 3145736 | tf_op jit(solution)/shard_map/ppermute | solution.py:97
  589.2 27.1 %collective-permute-start.37 = (bf16[256,2048]{1,0:T(8,128)(2,1)S(1)}, bf16[256,2048]{1,0:T(8,128)(2,1)S(1)}, u32[]{:S(2)}, u32[]{:S(2)}) collective-permute-start(bf16[256,2048]{1,0:T(8,128)(2,1)S(1)} %pad_maximum_fusion.18), channel_id=1, source_target_pairs={{0,2},{2,0},{1,3},{3,1},{4,6},{6,4},{5,7},{7,5},{8,10},{10,8},{9,1... | collective-permute-start | bytes 3145736 | tf_op jit(solution)/shard_map/ppermute | solution.py:46
  616.3 50.7 %collective-permute-start.55 = (bf16[512,2048]{1,0:T(8,128)(2,1)}, bf16[512,2048]{1,0:T(8,128)(2,1)}, u32[]{:S(2)}, u32[]{:S(2)}) collective-permute-start(bf16[512,2048]{1,0:T(8,128)(2,1)} %convolution_convert_fusion.3), channel_id=1, source_target_pairs={{0,8},{8,16},{16,24},{24,0},{1,9},{9,17},{17,25},{25,1},{2,10},{10... | collective-permute-start | bytes 6291464 | tf_op jit(solution)/shard_map/ppermute | solution.py:97
  616.3 128.8 %collective-permute-start.24 = (bf16[1024,2048]{1,0:T(8,128)(2,1)}, bf16[1024,2048]{1,0:T(8,128)(2,1)}, u32[]{:S(2)}, u32[]{:S(2)}) collective-permute-start(bf16[1024,2048]{1,0:T(8,128)(2,1)} %convolution_convert_fusion.2), channel_id=1, source_target_pairs={{0,1},{1,0},{2,3},{3,2},{4,5},{5,4},{6,7},{7,6},{8,9},{9,8},{10,11... | collective-permute-start | bytes 12582920 | tf_op jit(solution)/shard_map/ppermute | solution.py:54
  631.4 57.9 %collective-permute-start.59 = (bf16[512,1024]{1,0:T(8,128)(2,1)S(1)}, bf16[512,1024]{1,0:T(8,128)(2,1)S(1)}, u32[]{:S(2)}, u32[]{:S(2)}) collective-permute-start(bf16[512,1024]{1,0:T(8,128)(2,1)S(1)} %add_convert_fusion.9), channel_id=1, source_target_pairs={{0,8},{8,16},{16,24},{24,0},{1,9},{9,17},{17,25},{25,1},{2,10},{10... | collective-permute-start | bytes 3145736 | tf_op jit(solution)/shard_map/ppermute | solution.py:97
  642.7 35.0 %collective-permute-start.39 = (bf16[128,2048]{1,0:T(8,128)(2,1)S(1)}, bf16[128,2048]{1,0:T(8,128)(2,1)S(1)}, u32[]{:S(2)}, u32[]{:S(2)}) collective-permute-start(bf16[128,2048]{1,0:T(8,128)(2,1)S(1)} %get-tuple-element.64), channel_id=1, source_target_pairs={{0,2},{2,0},{1,3},{3,1},{4,6},{6,4},{5,7},{7,5},{8,10},{10,8},{9,1... | collective-permute-start | bytes 1572872 | tf_op jit(solution)/shard_map/ppermute | solution.py:46
  644.5 34.5 %collective-permute-start.40 = (bf16[128,2048]{1,0:T(8,128)(2,1)S(1)}, bf16[128,2048]{1,0:T(8,128)(2,1)S(1)}, u32[]{:S(2)}, u32[]{:S(2)}) collective-permute-start(bf16[128,2048]{1,0:T(8,128)(2,1)S(1)} %get-tuple-element.63), channel_id=1, source_target_pairs={{0,4},{4,0},{1,5},{5,1},{2,6},{6,2},{3,7},{7,3},{8,12},{12,8},{9,1... | collective-permute-start | bytes 1572872 | tf_op jit(solution)/shard_map/ppermute | solution.py:50
  677.7 56.7 %collective-permute-start.56 = (bf16[512,2048]{1,0:T(8,128)(2,1)}, bf16[512,2048]{1,0:T(8,128)(2,1)}, u32[]{:S(2)}, u32[]{:S(2)}) collective-permute-start(bf16[512,2048]{1,0:T(8,128)(2,1)} %add_convert_fusion.6), channel_id=1, source_target_pairs={{0,8},{8,16},{16,24},{24,0},{1,9},{9,17},{17,25},{25,1},{2,10},{10... | collective-permute-start | bytes 6291464 | tf_op jit(solution)/shard_map/ppermute | solution.py:97
  694.3 98.4 %collective-permute-start.60 = (bf16[512,1024]{1,0:T(8,128)(2,1)}, bf16[512,1024]{1,0:T(8,128)(2,1)}, u32[]{:S(2)}, u32[]{:S(2)}) collective-permute-start(bf16[512,1024]{1,0:T(8,128)(2,1)} %add_convert_fusion.8), channel_id=1, source_target_pairs={{0,8},{8,16},{16,24},{24,0},{1,9},{9,17},{17,25},{25,1},{2,10},{10... | collective-permute-start | bytes 3145736 | tf_op jit(solution)/shard_map/ppermute | solution.py:97
  704.3 51.9 %collective-permute-start.43 = (bf16[1024,2048]{1,0:T(8,128)(2,1)}, bf16[1024,2048]{1,0:T(8,128)(2,1)}, u32[]{:S(2)}, u32[]{:S(2)}) collective-permute-start(bf16[1024,2048]{1,0:T(8,128)(2,1)} %get-tuple-element.61), channel_id=1, source_target_pairs={{0,1},{1,0},{2,3},{3,2},{4,5},{5,4},{6,7},{7,6},{8,9},{9,8},{10,11... | collective-permute-start | bytes 12582920 | tf_op jit(solution)/shard_map/ppermute | solution.py:54
  744.9 81.9 %collective-permute-start.57 = (bf16[512,2048]{1,0:T(8,128)(2,1)}, bf16[512,2048]{1,0:T(8,128)(2,1)}, u32[]{:S(2)}, u32[]{:S(2)}) collective-permute-start(bf16[512,2048]{1,0:T(8,128)(2,1)} %add_convert_fusion.5), channel_id=1, source_target_pairs={{0,8},{8,16},{16,24},{24,0},{1,9},{9,17},{17,25},{25,1},{2,10},{10... | collective-permute-start | bytes 6291464 | tf_op jit(solution)/shard_map/ppermute | solution.py:97
  755.3 31.0 %collective-permute-start.25 = (bf16[256,2048]{1,0:T(8,128)(2,1)}, bf16[256,2048]{1,0:T(8,128)(2,1)}, u32[]{:S(2)}, u32[]{:S(2)}) collective-permute-start(bf16[256,2048]{1,0:T(8,128)(2,1)} %pad_maximum_fusion.13), channel_id=1, source_target_pairs={{0,4},{4,0},{1,5},{5,1},{2,6},{6,2},{3,7},{7,3},{8,12},{12,8},{9,1... | collective-permute-start | bytes 3145736 | tf_op jit(solution)/shard_map/ppermute | solution.py:50
  784.9 65.7 %collective-permute-start.44 = (bf16[1024,2048]{1,0:T(8,128)(2,1)}, bf16[1024,2048]{1,0:T(8,128)(2,1)}, u32[]{:S(2)}, u32[]{:S(2)}) collective-permute-start(bf16[1024,2048]{1,0:T(8,128)(2,1)} %convolution_convert_fusion.1), channel_id=1, source_target_pairs={{0,1},{1,0},{2,3},{3,2},{4,5},{5,4},{6,7},{7,6},{8,9},{9,8},{10,11... | collective-permute-start | bytes 12582920 | tf_op jit(solution)/shard_map/ppermute | solution.py:54
  786.0 26.2 %collective-permute-start.27 = (bf16[256,2048]{1,0:T(8,128)(2,1)}, bf16[256,2048]{1,0:T(8,128)(2,1)S(1)}, u32[]{:S(2)}, u32[]{:S(2)}) collective-permute-start(bf16[256,2048]{1,0:T(8,128)(2,1)} %pad_maximum_fusion.14), channel_id=1, source_target_pairs={{0,2},{2,0},{1,3},{3,1},{4,6},{6,4},{5,7},{7,5},{8,10},{10,8},{9,1... | collective-permute-start | bytes 3145736 | tf_op jit(solution)/shard_map/ppermute | solution.py:46
  791.3 32.2 %collective-permute-start.26 = (bf16[128,2048]{1,0:T(8,128)(2,1)}, bf16[128,2048]{1,0:T(8,128)(2,1)}, u32[]{:S(2)}, u32[]{:S(2)}) collective-permute-start(bf16[128,2048]{1,0:T(8,128)(2,1)} %fusion.111), channel_id=1, source_target_pairs={{0,2},{2,0},{1,3},{3,1},{4,6},{6,4},{5,7},{7,5},{8,10},{10,8},{9,1... | collective-permute-start | bytes 1572872 | tf_op jit(solution)/shard_map/ppermute | solution.py:46
  798.1 64.4 %all-to-all-start.10 = ((bf16[4,128,1024]{2,1,0:T(8,128)(2,1)}), bf16[4,128,1024]{2,1,0:T(8,128)(2,1)}, u32[]{:S(2)}, u32[]{:S(2)}) async-start(bf16[4,128,1024]{2,1,0:T(8,128)(2,1)} %bitcast.262), calls=%async_computation.10 | async-start | bytes 2097152 | tf_op jit(solution)/shard_map/all_to_all | solution.py:141
  860.2 37.6 %collective-permute-start.45 = (bf16[256,2048]{1,0:T(8,128)(2,1)}, bf16[256,2048]{1,0:T(8,128)(2,1)}, u32[]{:S(2)}, u32[]{:S(2)}) collective-permute-start(bf16[256,2048]{1,0:T(8,128)(2,1)} %pad_maximum_fusion.21), channel_id=1, source_target_pairs={{0,4},{4,0},{1,5},{5,1},{2,6},{6,2},{3,7},{7,3},{8,12},{12,8},{9,1... | collective-permute-start | bytes 3145736 | tf_op jit(solution)/shard_map/ppermute | solution.py:50
  862.5 50.1 %all-to-all-start.9 = ((bf16[4,128,2048]{2,1,0:T(8,128)(2,1)}), bf16[4,128,2048]{2,1,0:T(8,128)(2,1)S(1)}, u32[]{:S(2)}, u32[]{:S(2)}) async-start(bf16[4,128,2048]{2,1,0:T(8,128)(2,1)} %bitcast.258), calls=%async_computation.9 | async-start | bytes 4194304 | tf_op jit(solution)/shard_map/all_to_all | solution.py:141
  870.9 35.7 %collective-permute-start.53 = (bf16[512,256]{1,0:T(8,128)(2,1)S(1)}, bf16[512,256]{1,0:T(8,128)(2,1)S(1)}, u32[]{:S(2)}, u32[]{:S(2)}) collective-permute-start(bf16[512,256]{1,0:T(8,128)(2,1)S(1)} %fusion.88), channel_id=1, source_target_pairs={{0,8},{8,16},{16,24},{24,0},{1,9},{9,17},{17,25},{25,1},{2,10},{10... | collective-permute-start | bytes 786440 | tf_op jit(solution)/shard_map/ppermute | solution.py:97
  879.5 36.5 %collective-permute-start.50 = (bf16[512,768]{1,0:T(8,128)(2,1)}, bf16[512,768]{1,0:T(8,128)(2,1)}, u32[]{:S(2)}, u32[]{:S(2)}) collective-permute-start(bf16[512,768]{1,0:T(8,128)(2,1)} %add_convert_fusion.13), channel_id=1, source_target_pairs={{0,8},{8,16},{16,24},{24,0},{1,9},{9,17},{17,25},{25,1},{2,10},{10... | collective-permute-start | bytes 2359304 | tf_op jit(solution)/shard_map/ppermute | solution.py:97
  880.7 41.7 %collective-permute-start.47 = (bf16[256,2048]{1,0:T(8,128)(2,1)}, bf16[256,2048]{1,0:T(8,128)(2,1)}, u32[]{:S(2)}, u32[]{:S(2)}) collective-permute-start(bf16[256,2048]{1,0:T(8,128)(2,1)} %pad_maximum_fusion.22), channel_id=1, source_target_pairs={{0,2},{2,0},{1,3},{3,1},{4,6},{6,4},{5,7},{7,5},{8,10},{10,8},{9,1... | collective-permute-start | bytes 3145736 | tf_op jit(solution)/shard_map/ppermute | solution.py:46
  902.6 31.9 %collective-permute-start.46 = (bf16[128,2048]{1,0:T(8,128)(2,1)}, bf16[128,2048]{1,0:T(8,128)(2,1)}, u32[]{:S(2)}, u32[]{:S(2)}) collective-permute-start(bf16[128,2048]{1,0:T(8,128)(2,1)} %fusion.103), channel_id=1, source_target_pairs={{0,2},{2,0},{1,3},{3,1},{4,6},{6,4},{5,7},{7,5},{8,10},{10,8},{9,1... | collective-permute-start | bytes 1572872 | tf_op jit(solution)/shard_map/ppermute | solution.py:46
  909.7 27.4 %collective-permute-start.54 = (bf16[512,256]{1,0:T(8,128)(2,1)}, bf16[512,256]{1,0:T(8,128)(2,1)S(1)}, u32[]{:S(2)}, u32[]{:S(2)}) collective-permute-start(bf16[512,256]{1,0:T(8,128)(2,1)} %fusion.91), channel_id=1, source_target_pairs={{0,8},{8,16},{16,24},{24,0},{1,9},{9,17},{17,25},{25,1},{2,10},{10... | collective-permute-start | bytes 786440 | tf_op jit(solution)/shard_map/ppermute | solution.py:97
  912.6 48.5 %all-to-all-start.4 = ((bf16[32,8,2048]{2,1,0:T(8,128)(2,1)}), bf16[32,8,2048]{2,1,0:T(8,128)(2,1)}, u32[]{:S(2)}, u32[]{:S(2)}) async-start(bf16[32,8,2048]{2,1,0:T(8,128)(2,1)} %fusion.17), calls=%async_computation.4 | async-start | bytes 2097152 | tf_op jit(solution)/shard_map/all_to_all | solution.py:282
  920.8 33.5 %collective-permute-start.51 = (bf16[512,768]{1,0:T(8,128)(2,1)S(1)}, bf16[512,768]{1,0:T(8,128)(2,1)S(1)}, u32[]{:S(2)}, u32[]{:S(2)}) collective-permute-start(bf16[512,768]{1,0:T(8,128)(2,1)S(1)} %add_convert_fusion.12), channel_id=1, source_target_pairs={{0,8},{8,16},{16,24},{24,0},{1,9},{9,17},{17,25},{25,1},{2,10},{10... | collective-permute-start | bytes 2359304 | tf_op jit(solution)/shard_map/ppermute | solution.py:97
  983.9 33.4 %all-to-all-start.6 = ((bf16[32,8,2048]{2,1,0:T(8,128)(2,1)}), bf16[32,8,2048]{2,1,0:T(8,128)(2,1)}, u32[]{:S(2)}, u32[]{:S(2)}) async-start(bf16[32,8,2048]{2,1,0:T(8,128)(2,1)} %fusion.19), calls=%async_computation.6 | async-start | bytes 2097152 | tf_op jit(solution)/shard_map/all_to_all | solution.py:282
  (98 other events, 2107.5 us)

commit v2 on v1

--- a/solution.py
+++ b/solution.py
@@ -1,3 +1,4 @@
+import functools
 import math
 
 import jax
@@ -14,7 +15,8 @@
 NEG_LARGE = -1e30
 F32 = jnp.float32
 BF16 = jnp.bfloat16
-FLIP = ((0, 1), (1, 0))
+MESH = pl.DeviceIdType.MESH
+IDS = ("gather_one", "gather_up", "gather_two", "gather_middle", "product_out", "product_down", "product_forward", "product_qkv")
 
 
 def project(left, right):
@@ -42,88 +44,269 @@
     return (gradient - mean_grad - normed * mean_both) * scale
 
 
-def to_x(values):
-    return lax.ppermute(values, "x", FLIP)
-
-
-def to_y(values):
-    return lax.ppermute(values, "y", FLIP)
-
-
-def to_core(values):
-    return lax.ppermute(values, "c", FLIP)
-
-
-def plane_gather(rows):
-    half = rows.shape[0] // 2
-    first, second = rows[:half], rows[half:]
-    first_x = to_x(first)
-    second_y = to_y(second)
-    first_far = to_y(jnp.concatenate([first, first_x]))
-    second_far = to_x(jnp.concatenate([second, second_y]))
-    mine = jnp.concatenate(
-        [
-            first,
-            second,
-            first_x,
-            second_far[:half],
-            first_far[:half],
-            second_y,
-            first_far[half:],
-            second_far[half:],
-        ]
-    )
-    return jnp.concatenate([mine, to_core(mine)])
-
-
-def plane_scatter(far, near):
-    block = near.shape[0] // 4
+def flip(axis):
+    return {axis: 1 - lax.axis_index(axis)}
+
+
+def greet(axes, ring):
+    barrier = pltpu.get_barrier_semaphore()
+    for axis in axes:
+        pl.semaphore_signal(barrier, inc=1, device_id=flip(axis), device_id_type=MESH)
+    count = len(axes)
+    if ring:
+        total = lax.axis_size("z")
+        behind = lax.rem(lax.axis_index("z") + total - 1, total)
+        pl.semaphore_signal(barrier, inc=1, device_id={"z": behind}, device_id_type=MESH)
+        count += 1
+    pl.semaphore_wait(barrier, count)
+
+
+def ring_copy(source, target, send, recv):
+    total = lax.axis_size("z")
+    ahead = lax.rem(lax.axis_index("z") + 1, total)
+    return pltpu.make_async_remote_copy(
+        src_ref=source,
+        dst_ref=target,
+        send_sem=send,
+        recv_sem=recv,
+        device_id={"z": ahead},
+        device_id_type=MESH,
+    )
+
+
+def gather_kernel(ring, *refs):
+    if ring:
+        own, passing, out, passed, send, recv, local = refs
+    else:
+        own, out, send, recv, local = refs
+    rows = own.shape[0]
+    half = rows // 2
+
+    def part(block, side):
+        return out.at[pl.ds(block * rows + side * half, half)]
+
+    def push(axis, source, target, slot):
+        copy = pltpu.make_async_remote_copy(
+            src_ref=source,
+            dst_ref=target,
+            send_sem=send.at[slot],
+            recv_sem=recv.at[slot],
+            device_id=flip(axis),
+            device_id_type=MESH,
+        )
+        copy.start()
+        return copy
+
+    keep = pltpu.make_async_copy(own, out.at[pl.ds(0, rows)], local)
+    keep.start()
+    greet(("x", "y", "c"), ring)
+    first, second = own.at[pl.ds(0, half)], own.at[pl.ds(half, half)]
+    x_first = push("x", first, part(1, 0), 0)
+    y_second = push("y", second, part(2, 1), 1)
+    x_second = push("x", second, part(1, 1), 2)
+    y_first = push("y", first, part(2, 0), 3)
+    if ring:
+        around = ring_copy(passing, passed, send.at[13], recv.at[13])
+        around.start()
+    across = [push("c", own, out.at[pl.ds(4 * rows, rows)], 4)]
+    x_first.wait_recv()
+    far_first = push("y", part(1, 0), part(3, 0), 5)
+    across.append(push("c", part(1, 0), part(5, 0), 6))
+    y_second.wait_recv()
+    far_second = push("x", part(2, 1), part(3, 1), 7)
+    across.append(push("c", part(2, 1), part(6, 1), 8))
+    x_second.wait_recv()
+    across.append(push("c", part(1, 1), part(5, 1), 9))
+    y_first.wait_recv()
+    across.append(push("c", part(2, 0), part(6, 0), 10))
+    far_first.wait_recv()
+    across.append(push("c", part(3, 0), part(7, 0), 11))
+    far_second.wait_recv()
+    across.append(push("c", part(3, 1), part(7, 1), 12))
+    for copy in across:
+        copy.wait_recv()
+    for copy in across + [x_first, y_second, x_second, y_first, far_first, far_second]:
+        copy.wait_send()
+    keep.wait()
+    if ring:
+        around.wait()
+
+
+def plane_gather(rows, name, passing=None):
+    ring = passing is not None
+    shapes = [jax.ShapeDtypeStruct((8 * rows.shape[0], rows.shape[1]), rows.dtype)]
+    operands = [rows]
+    if ring:
+        shapes.append(jax.ShapeDtypeStruct(passing.shape, passing.dtype))
+        operands.append(passing)
+    got = pl.pallas_call(
+        functools.partial(gather_kernel, ring),
+        in_specs=[pl.BlockSpec(memory_space=pl.ANY)] * len(operands),
+        out_specs=[pl.BlockSpec(memory_space=pl.ANY)] * len(shapes),
+        out_shape=shapes,
+        scratch_shapes=[
+            pltpu.SemaphoreType.DMA((14,)),
+            pltpu.SemaphoreType.DMA((14,)),
+            pltpu.SemaphoreType.DMA(()),
+        ],
+        compiler_params=pltpu.CompilerParams(
+            collective_id=IDS.index(name), has_side_effects=True
+        ),
+        cost_estimate=pl.CostEstimate(flops=0, bytes_accessed=120 << 20, transcendentals=0),
+        name=name,
+    )(*operands)
+    return tuple(got) if ring else got[0]
+
+
+def scatter_kernel(ring, *refs):
+    if ring:
+        rows_ref, weight_ref, passing, out_ref, passed = refs[:5]
+    else:
+        rows_ref, weight_ref, out_ref = refs[:3]
+    left, weight, away, got, near, by_y, by_x, end_y, end_x, send, recv, local = refs[-12:]
+    block, width = out_ref.shape
     half = block // 2
-    got = to_core(far.astype(BF16))
-    paired = (near + got.astype(F32)).astype(BF16).reshape(4, 2, half, -1)
-    by_y = to_y(jnp.concatenate([paired[2, 0], paired[3, 0]])).astype(F32)
-    by_x = to_x(jnp.concatenate([paired[1, 1], paired[3, 1]])).astype(F32)
-    own_first = paired[0, 0].astype(F32) + by_y[:half]
-    own_second = paired[0, 1].astype(F32) + by_x[:half]
-    x_first = (paired[1, 0].astype(F32) + by_y[half:]).astype(BF16)
-    y_second = (paired[2, 1].astype(F32) + by_x[half:]).astype(BF16)
-    return jnp.concatenate(
-        [own_first + to_x(x_first).astype(F32), own_second + to_y(y_second).astype(F32)]
-    )
-
-
-def ring_next(values):
-    total = lax.axis_size("z")
-    return lax.ppermute(values, "z", [(i, (i + 1) % total) for i in range(total)])
+    tile = 512
+
+    def push(axis, source, target, slot):
+        copy = pltpu.make_async_remote_copy(
+            src_ref=source,
+            dst_ref=target,
+            send_sem=send.at[slot],
+            recv_sem=recv.at[slot],
+            device_id=flip(axis),
+            device_id_type=MESH,
+        )
+        copy.start()
+        return copy
+
+    fetch_weight = pltpu.make_async_copy(weight_ref, weight, local.at[8])
+    fetch_weight.start()
+    order = (7, 6, 3, 5, 2, 4, 1, 0)
+    fetches = {}
+    for index in order:
+        at = pl.ds(index * block, block)
+        fetches[index] = pltpu.make_async_copy(rows_ref.at[at], left.at[at], local.at[index])
+        fetches[index].start()
+    greet(("x", "y", "c"), ring)
+    if ring:
+        around = ring_copy(passing, passed, send.at[10], recv.at[10])
+        around.start()
+    fetch_weight.wait()
+
+    def multiply(index, store):
+        fetches[index].wait()
+        here = left[pl.ds(index * block, block), :]
+
+        @pl.loop(0, width // tile)
+        def _(step):
+            at = pl.ds(pl.multiple_of(step * tile, tile), tile)
+            store(at, project_t(here, weight[at, :]))
+
+    crossing = {}
+    sent = []
+
+    def compute_far(index):
+        def store(at, value):
+            away[index, :, at] = value.astype(BF16)
+
+        multiply(4 + index, store)
+        crossing[index] = push("c", away.at[index], got.at[index], index)
+
+    def compute_near(index):
+        crossing[index].wait_recv()
+
+        def store(at, value):
+            near[index, :, at] = (value + got[index, :, at].astype(F32)).astype(BF16)
+
+        multiply(index, store)
+
+    lower, upper = pl.ds(0, half), pl.ds(half, half)
+    compute_far(3)
+    compute_far(2)
+    compute_near(3)
+    y_far = push("y", near.at[3, lower], by_y.at[1], 4)
+    x_far = push("x", near.at[3, upper], by_x.at[1], 5)
+    compute_far(1)
+    compute_near(2)
+    y_near = push("y", near.at[2, lower], by_y.at[0], 6)
+    compute_far(0)
+    compute_near(1)
+    x_near = push("x", near.at[1, upper], by_x.at[0], 7)
+    compute_near(0)
+    y_far.wait_recv()
+    near[1, lower, :] = (near[1, lower, :].astype(F32) + by_y[1].astype(F32)).astype(BF16)
+    x_last = push("x", near.at[1, lower], end_x, 8)
+    x_far.wait_recv()
+    near[2, upper, :] = (near[2, upper, :].astype(F32) + by_x[1].astype(F32)).astype(BF16)
+    y_last = push("y", near.at[2, upper], end_y, 9)
+    y_near.wait_recv()
+    out_ref[lower, :] = near[0, lower, :].astype(F32) + by_y[0].astype(F32)
+    x_near.wait_recv()
+    out_ref[upper, :] = near[0, upper, :].astype(F32) + by_x[0].astype(F32)
+    x_last.wait_recv()
+    out_ref[lower, :] += end_x[...].astype(F32)
+    y_last.wait_recv()
+    out_ref[upper, :] += end_y[...].astype(F32)
+    for copy in (crossing[0], crossing[1], crossing[2], crossing[3]):
+        copy.wait_send()
+    for copy in (y_far, x_far, y_near, x_near, x_last, y_last):
+        copy.wait_send()
+    if ring:
+        around.wait()
+
+
+def plane_product(rows, weight, name, passing=None):
+    ring = passing is not None
+    total, inner = rows.shape
+    width = weight.shape[0]
+    block = total // 8
+    half = block // 2
+    shapes = [jax.ShapeDtypeStruct((block, width), F32)]
+    operands = [rows, weight]
+    specs = [pl.BlockSpec(memory_space=pl.ANY)] * 2
+    out_specs = [pl.BlockSpec(memory_space=pltpu.VMEM)]
+    if ring:
+        shapes.append(jax.ShapeDtypeStruct(passing.shape, passing.dtype))
+        operands.append(passing)
+        specs.append(pl.BlockSpec(memory_space=pl.ANY))
+        out_specs.append(pl.BlockSpec(memory_space=pl.ANY))
+    got = pl.pallas_call(
+        functools.partial(scatter_kernel, ring),
+        in_specs=specs,
+        out_specs=out_specs,
+        out_shape=shapes,
+        scratch_shapes=[
+            pltpu.VMEM((total, inner), BF16),
+            pltpu.VMEM((width, inner), BF16),
+            pltpu.VMEM((4, block, width), BF16),
+            pltpu.VMEM((4, block, width), BF16),
+            pltpu.VMEM((4, block, width), BF16),
+            pltpu.VMEM((2, half, width), BF16),
+            pltpu.VMEM((2, half, width), BF16),
+            pltpu.VMEM((half, width), BF16),
+            pltpu.VMEM((half, width), BF16),
+            pltpu.SemaphoreType.DMA((11,)),
+            pltpu.SemaphoreType.DMA((11,)),
+            pltpu.SemaphoreType.DMA((9,)),
+        ],
+        compiler_params=pltpu.CompilerParams(
+            collective_id=IDS.index(name), has_side_effects=True, vmem_limit_bytes=48 << 20
+        ),
+        cost_estimate=pl.CostEstimate(
+            flops=2 * total * inner * width, bytes_accessed=120 << 20, transcendentals=0
+        ),
+        name=name,
+    )(*operands)
+    return tuple(got) if ring else got[0]
 
 
 def ring_gather(block):
-    total = lax.axis_size("z")
-    place = lax.axis_index("z")
-    rows = block.shape[0]
-    whole = jnp.zeros((total * rows, block.shape[1]), block.dtype)
-    current = block
-    whole = lax.dynamic_update_slice(whole, current, (place * rows, 0))
-    for step in range(1, total):
-        current = ring_next(current)
-        owner = lax.rem(place - step + total, total)
-        whole = lax.dynamic_update_slice(whole, current, (owner * rows, 0))
-    return whole, current
-
-
-def ring_outer(left, right):
-    total = lax.axis_size("z")
-    place = lax.axis_index("z")
-    columns = left.shape[1] // total
-    running = None
-    for step in range(total):
-        owner = lax.rem(place + 2 * total - 1 - step, total)
-        piece = lax.dynamic_slice(left, (0, owner * columns), (left.shape[0], columns))
-        term = outer_sum(piece, right)
-        if running is not None:
-            term = term + ring_next(running).astype(F32)
-        running = term.astype(BF16)
-    return running
+    return lax.all_gather(block, "z", axis=0, tiled=True)
+
+
+def ring_sum(values):
+    return lax.psum_scatter(values.astype(BF16), "z", scatter_dimension=0, tiled=True)
 
 
 def to_plane(values):
@@ -322,9 +505,9 @@
     )
     forward_block = to_plane(jnp.concatenate([spread(w_gate), spread(w_up)], axis=2))
     down_block = to_plane(spread(w_down.T))
-    attention_w, attention_last = ring_gather(attention_block)
-    forward_w, forward_last = ring_gather(after(forward_block, attention_last))
-    down_w, _ = ring_gather(after(down_block, forward_last))
+    attention_w = ring_gather(attention_block)
+    forward_w = ring_gather(after(forward_block, attention_block))
+    down_w = ring_gather(after(down_block, forward_block))
     head_width = attention_w.shape[1] // 4
     hidden_width = down_w.shape[1]
     qkv_w = attention_w[:, : 3 * head_width]
@@ -341,44 +524,34 @@
     sin_rows = jnp.concatenate([-sin_half, sin_half], axis=1)
 
     normed_one, scale_one = norm_parts(arrived)
-    seen_one = plane_gather(normed_one.astype(BF16))
-    total_rows = seen_one.shape[0]
-    middle_row = total_rows // 2
+    seen_one = plane_gather(normed_one.astype(BF16), "gather_one")
+    grad_two_all = plane_gather(after(upstream_low, seen_one), "gather_up")
     qkv_lin = project(seen_one, qkv_w)
     qkv_low, attended = attend(qkv_lin, cos_rows, sin_rows, places, tok_rows)
-    middle = arrived + plane_scatter(
-        project_t(attended[middle_row:], out_w), project_t(attended[:middle_row], out_w)
-    )
+    middle = arrived + plane_product(attended, out_w, "product_out")
     normed_two, scale_two = norm_parts(middle)
-    seen_two = plane_gather(normed_two.astype(BF16))
-    grad_two_all = plane_gather(upstream_low)
+    seen_two = plane_gather(normed_two.astype(BF16), "gather_two")
 
     gate_lin = project(seen_two, forward_w[:, :hidden_width])
     up_lin = project(seen_two, forward_w[:, hidden_width:])
     sigmoid = jax.nn.sigmoid(gate_lin)
     hidden = (gate_lin * sigmoid * up_lin).astype(BF16)
-    summed_down = from_plane(ring_outer(grad_two_all, hidden))
-    output = middle + plane_scatter(
-        project_t(hidden[middle_row:], down_w), project_t(hidden[:middle_row], down_w)
-    )
+    summed_down = from_plane(ring_sum(outer_sum(grad_two_all, hidden)))
     grad_hidden = project(grad_two_all, down_w)
     grad_gate = grad_hidden * up_lin * (sigmoid * (1.0 + gate_lin * (1.0 - sigmoid)))
     grad_up = grad_hidden * (gate_lin * sigmoid)
     grad_both = jnp.concatenate([grad_gate.astype(BF16), grad_up.astype(BF16)], axis=1)
-    grad_normed_two = plane_scatter(
-        project_t(grad_both[middle_row:], forward_w), project_t(grad_both[:middle_row], forward_w)
-    )
-    summed_forward = from_plane(ring_outer(seen_two, grad_both))
+    summed_forward = from_plane(ring_sum(outer_sum(seen_two, grad_both)))
+    grad_normed_two = plane_product(grad_both, forward_w, "product_forward")
     grad_middle = upstream + norm_back(normed_two, scale_two, grad_normed_two)
-    grad_one_all = plane_gather(grad_middle.astype(BF16))
+    grad_one_all = plane_gather(grad_middle.astype(BF16), "gather_middle")
     grad_attended = project(grad_one_all, out_w).astype(BF16)
     grad_qkv = attend_back(qkv_low, grad_attended, cos_rows, sin_rows, places, tok_rows)
-    grad_normed_one = plane_scatter(
-        project_t(grad_qkv[middle_row:], qkv_w), project_t(grad_qkv[:middle_row], qkv_w)
-    )
+    summed_qkv = from_plane(ring_sum(outer_sum(seen_one, grad_qkv)))
+    summed_out = from_plane(ring_sum(outer_sum(grad_one_all, attended)))
+    grad_normed_one = plane_product(grad_qkv, qkv_w, "product_qkv")
     grad_inputs = grad_middle + norm_back(normed_one, scale_one, grad_normed_one)
-    summed_out = from_plane(ring_outer(grad_one_all, attended))
-    summed_qkv = from_plane(ring_outer(seen_one, grad_qkv))
+    output = middle + plane_product(after(hidden, grad_normed_one), down_w, "product_down")
 
     def give_back(rows):
         packed = outer_sum(recv_pick, rows.astype(BF16)).astype(BF16)

time: 1030 us -> 924 us (0.90)
  Pallas kernels: 24.4 us -> 380 us
  waiting for transfers between devices: 468 us -> 167 us
  blocking collectives: 16.4 us -> 132 us
  matrix products: 238 us -> 145 us
  starting transfers between devices: 104 us -> 19 us
  local copies, waits for them, and re-layouts: 107 us -> 25.1 us
  other arithmetic: 59.8 us -> 31.3 us
  between operations: 2.42 us -> 15.3 us
    ppermute x61 -> x0, waiting for transfers between devices: 403 us -> none  [the longest x21 236 us: ring_next(): lax.ppermute(values, 'z', [(i, (i + 1) % total) for i in range(total)])]
    pallas_call x0 -> x8, Pallas kernels: none -> 355 us  [the longest x4 191 us: plane_product(): pl.pallas_call(functools.partial(scatter_kernel, ring), in_specs=specs, o...]
    all_to_all x0 -> x6, blocking collectives: none -> 123 us  [the longest x2 47.2 us: to_plane(): lax.all_to_all(pieces, ('y', 'x'), split_axis=0, concat_axis=0, tiled=True)]
    reduce_scatter x0 -> x4, waiting for transfers between devices: none -> 92 us  [ring_sum(): lax.psum_scatter(values.astype(BF16), 'z', scatter_dimension=0, tiled=True)]
    dot_general x8 -> x0, matrix products: 66.1 us -> none  [project_t(): lax.dot_general(left, right, (((1,), (1,)), ((), ())), preferred_element_...]
    ppermute x61 -> x0, starting transfers between devices: 52.1 us -> none  [the longest x16 23.6 us: to_x(): return lax.ppermute(values, 'x', FLIP)]
    unnamed x194 -> x54, local copies, waits for them, and re-layouts: 53.5 us -> 5.74 us
    dot_general x20 -> x8, matrix products: 98.4 us -> 63.5 us  [outer_sum(): lax.dot_general(left, right, (((0,), (0,)), ((), ())), preferred_element_...]
  transfers between devices with their start and end apart: 72 -> 12, of which waited for: 36 -> 5; matrix products, arithmetic and copies ran while one was open for 31% -> 14% of each run, Pallas kernels for 2% -> 32%
where the time goes in v2:
time: 924 us; the launch traced here: 915 us
  Pallas kernels  380 us (41%)
  waiting for transfers between devices  167 us (18%)
  matrix products  145 us (16%)
  blocking collectives  132 us (14%)
  other arithmetic  31.3 us (3%)
  local copies, waits for them, and re-layouts  25.1 us (3%)
  starting transfers between devices  19 us (2%)
  between operations  15.3 us (2%)
    pallas_call x4, Pallas kernels, plane_product(): pl.pallas_call(functools.partial(scatter_kernel, ring), in_specs=specs, o...  191 us
    pallas_call x4, Pallas kernels, plane_gather(): pl.pallas_call(functools.partial(gather_kernel, ring), in_specs=[pl.Block...  165 us
    reduce_scatter x4, waiting for transfers between devices, ring_sum(): lax.psum_scatter(values.astype(BF16), 'z', scatter_dimension=0, tiled=True)  92 us
    dot_general x9, matrix products, project(): return jnp.dot(left, right, preferred_element_type=F32)  81.5 us
    dot_general x8, matrix products, outer_sum(): lax.dot_general(left, right, (((0,), (0,)), ((), ())), preferred_element_...  63.5 us
    all_to_all x2, blocking collectives, to_plane(): lax.all_to_all(pieces, ('y', 'x'), split_axis=0, concat_axis=0, tiled=True)  47.2 us
    all_to_all x3, blocking collectives, from_plane(): lax.all_to_all(block, ('y', 'x'), split_axis=0, concat_axis=0, tiled=True)  39.8 us
    all_to_all x1, blocking collectives, exchange(): return lax.all_to_all(rows, EVERY, split_axis=0, concat_axis=0, tiled=True)  36.2 us
  transfers between devices with their start and end apart: 12, of which 5 were waited for; matrix products, arithmetic and copies ran while one was open for 14% of the time, Pallas kernels for 32%

profile of v2, /device:TPU:0, one launch (start us, length us, event | category | flops | bytes accessed | tf_op | source)
XLA Modules:
  0.0 914.8 jit_solution(11146489310923889992)
XLA Ops:
  11.0 19.2 %all_to_all.111 = bf16[4,128,1024]{2,1,0:T(8,128)(2,1)} all-to-all(bf16[4,128,1024]{2,1,0:T(8,128)(2,1)S(1)} %pad_maximum_fusion.2), channel_id=1, replica_groups=mesh['z'=4,'y'=2,'x'=2,'c'=2] {'y','x'}, dimensions={0} | all-to-all | bytes 2097152 | tf_op jit(solution)/shard_map/all_to_all | solution.py:314
  33.3 4.4 all-to-all-start.4
  40.0 10.1 %all-to-all-done.4 = bf16[4,128,1024]{2,1,0:T(8,128)(2,1)} async-done(((bf16[4,128,1024]{2,1,0:T(8,128)(2,1)}), bf16[4,128,1024]{2,1,0:T(8,128)(2,1)}, u32[]{:S(2)}, u32[]{:S(2)}) %all-to-all-start.4) | async-done | bytes 1048608 | tf_op jit(solution)/shard_map/all_to_all | solution.py:314
  50.1 28.0 %all_to_all.112 = bf16[4,128,2048]{2,1,0:T(8,128)(2,1)} all-to-all(bf16[4,128,2048]{2,1,0:T(8,128)(2,1)S(1)} %pad_maximum_fusion.1), channel_id=1, replica_groups=mesh['z'=4,'y'=2,'x'=2,'c'=2] {'y','x'}, dimensions={0} | all-to-all | bytes 4194304 | tf_op jit(solution)/shard_map/all_to_all | solution.py:314
  80.7 4.4 all-to-all-start
  85.2 8.8 all-gather.1
  96.0 3.7 fusion.22
  99.8 33.2 %all-to-all-done = bf16[32,8,2048]{2,1,0:T(8,128)(2,1)} async-done(((bf16[32,8,2048]{2,1,0:T(8,128)(2,1)}), bf16[32,8,2048]{2,1,0:T(8,128)(2,1)}, u32[]{:S(2)}, u32[]{:S(2)}) %all-to-all-start) | async-done | bytes 1048608 | tf_op jit(solution)/shard_map/all_to_all | solution.py:465
  133.0 3.4 all-to-all-start.3
  136.6 1.9 reshape.179.place_ref
  138.5 1.9 pad_maximum_fusion.3
  140.5 1.9 fusion.40
  145.0 45.6 %gather_one.1 = bf16[2048,2048]{1,0:T(8,128)(2,1)} custom-call(bf16[256,2048]{1,0:T(8,128)(2,1)} %fusion.9.refs_0_), custom_call_target="tpu_custom_call" | custom-call | bytes 125829120 | tf_op jit(solution)/shard_map/gather_one/pallas_call | solution.py:142
  190.7 2.7 convolution_convert_fusion.5.refs_0_
  193.4 39.9 %gather_up.1 = bf16[2048,2048]{1,0:T(8,128)(2,1)} custom-call(bf16[256,2048]{1,0:T(8,128)(2,1)} %convolution_convert_fusion.5.refs_0_), custom_call_target="tpu_custom_call" | custom-call | bytes 125829120 | tf_op jit(solution)/shard_map/gather_up/pallas_call | solution.py:142
  234.7 12.2 %fusion.33.lin_ref = f32[2048,768]{1,0:T(8,128)} fusion(bf16[2048,2048]{1,0:T(8,128)(2,1)} %gather_one.1, bf16[2048,1024]{1,0:T(8,128)(2,1)} %all-gather.6.cloned.1.call-done), kind=kOutput, calls=%fused_computation.109 | convolution fusion | flops 6442450944 | bytes 17825792 | tf_op jit(solution)/shard_map/dot_general | solution.py:23
  246.9 11.5 %attend.1 = (bf16[2048,768]{1,0:T(8,128)(2,1)}, bf16[2048,256]{1,0:T(8,128)(2,1)}) custom-call(f32[2048,768]{1,0:T(8,128)} %fusion.33.lin_ref, f32[2048,128]{1,0:T(8,128)} %get-tuple-element.46.cos_ref, f32[2048,128]{1,0:T(8,128)} %get-tuple-element.47.sin_ref, s32[2048,1]{1,0:T(8,128)} %reshape.179.place_ref), custom_call_target="tpu_custom_call" | custom-call | flops 536870912 | bytes 12582912 | tf_op jit(solution)/shard_map/attend/pallas_call | solution.py:396
  259.6 43.3 %product_out.1 = f32[256,2048]{1,0:T(8,128)S(1)} custom-call(bf16[2048,256]{1,0:T(8,128)(2,1)S(1)} %copy-done.3, bf16[2048,256]{1,0:T(8,128)(2,1)S(1)} %slice.37.refs_1_), custom_call_target="tpu_custom_call" | custom-call | flops 2147483648 | bytes 125829120 | tf_op jit(solution)/shard_map/product_out/pallas_call | solution.py:274
  304.8 39.4 %gather_two.1 = bf16[2048,2048]{1,0:T(8,128)(2,1)} custom-call(bf16[256,2048]{1,0:T(8,128)(2,1)} %fusion.10.refs_0_), custom_call_target="tpu_custom_call" | custom-call | bytes 125829120 | tf_op jit(solution)/shard_map/gather_two/pallas_call | solution.py:142
  344.2 14.5 %fusion.41 = f32[2048,1024]{1,0:T(8,128)} fusion(bf16[2048,2048]{1,0:T(8,128)(2,1)} %gather_up.1, bf16[2048,1024]{1,0:T(8,128)(2,1)} %all-gather.10.cloned.1.call-done.refs_1_), kind=kOutput, calls=%fused_computation.117 | convolution fusion | flops 8589934592 | bytes 20971520 | tf_op jit(solution)/shard_map/dot_general | solution.py:23
  358.7 22.0 %all-gather.8.cloned.1.call-done.refs_1_ = bf16[2048,2048]{1,0:T(8,128)(2,1)} async-done(((bf16[512,2048]{1,0:T(8,128)(2,1)}), bf16[2048,2048]{1,0:T(8,128)(2,1)}) %all-gather.8.cloned.1.call-update) | async-done | bytes 8388624 | tf_op jit(solution)/shard_map/all_gather | solution.py:305
  380.7 14.8 %fusion.1 = f32[2048,1024]{1,0:T(8,128)} fusion(bf16[2048,2048]{1,0:T(8,128)(2,1)} %gather_two.1, bf16[2048,2048]{1,0:T(8,128)(2,1)} %all-gather.8.cloned.1.call-done.refs_1_), kind=kOutput, calls=%fused_computation.7 | convolution fusion | flops 8589934592 | bytes 20971520 | tf_op jit(solution)/shard_map/dot_general | solution.py:23
  395.4 23.4 %multiply_convert_fusion.1 = (bf16[2048,1024]{1,0:T(8,128)(2,1)}, bf16[2048,1024]{1,0:T(8,128)(2,1)}, bf16[2048,1024]{1,0:T(8,128)(2,1)}) fusion(f32[2048,1024]{1,0:T(8,128)} %fusion.41, f32[2048,1024]{1,0:T(8,128)} %fusion.1, bf16[2048,2048]{1,0:T(8,128)(2,1)} %gather_two.1, bf16[2048,2048]{1,0:T(8,128)(2,1)} %all-gather.8.cloned.1.call-done.refs_1_), kind=kOutput, calls=%fused_computation.2 | convolution fusion | flops 8621391872 | bytes 41943040 | tf_op jit(solution)/shard_map/dot_general | solution.py:23
  418.8 8.2 pad_maximum_fusion.refs_0_
  427.0 50.0 %product_forward.1 = f32[256,2048]{1,0:T(8,128)S(1)} custom-call(bf16[2048,2048]{1,0:T(8,128)(2,1)} %pad_maximum_fusion.refs_0_, bf16[2048,2048]{1,0:T(8,128)(2,1)} %all-gather.8.cloned.1.call-done.refs_1_), custom_call_target="tpu_custom_call" | custom-call | flops 17179869184 | bytes 125829120 | tf_op jit(solution)/shard_map/product_forward/pallas_call | solution.py:274
  478.2 2.6 fusion.37
  480.8 39.8 %gather_middle.1 = bf16[2048,2048]{1,0:T(8,128)(2,1)} custom-call(bf16[256,2048]{1,0:T(8,128)(2,1)} %get-tuple-element.25.refs_0_), custom_call_target="tpu_custom_call" | custom-call | bytes 125829120 | tf_op jit(solution)/shard_map/gather_middle/pallas_call | solution.py:142
  520.6 6.9 convolution_convert_fusion.8
  527.6 7.1 convolution_convert_fusion.9.grad_ref
  534.7 13.0 %attend_back.1.refs_0_ = bf16[2048,768]{1,0:T(8,128)(2,1)} custom-call(bf16[2048,768]{1,0:T(8,128)(2,1)} %get-tuple-element.17.low_ref, bf16[2048,256]{1,0:T(8,128)(2,1)} %convolution_convert_fusion.9.grad_ref, f32[2048,128]{1,0:T(8,128)} %get-tuple-element.46.cos_ref, f32[2048,128]{1,0:T(8,128)} %get-tuple-element.47.sin_ref, s32[2048,1]{1,0:T(8,128)} %reshape.179.place_ref), custom_call_target="tpu_custom_call" | custom-call | flops 1342177280 | bytes 9437184 | tf_op jit(solution)/shard_map/attend_back/pallas_call | solution.py:421
  547.7 11.4 %convolution_convert_fusion.2 = bf16[2048,768]{1,0:T(8,128)(2,1)} fusion(bf16[2048,2048]{1,0:T(8,128)(2,1)} %gather_one.1, bf16[2048,768]{1,0:T(8,128)(2,1)} %attend_back.1.refs_0_), kind=kOutput, calls=%fused_computation.12 | convolution fusion | flops 6444023808 | bytes 14680064 | tf_op jit(solution)/shard_map/dot_general | solution.py:31
  559.2 14.6 %convolution_convert_fusion.1 = bf16[2048,1024]{1,0:T(8,128)(2,1)} fusion(bf16[2048,2048]{1,0:T(8,128)(2,1)} %gather_up.1, bf16[2048,1024]{1,0:T(8,128)(2,1)} %get-tuple-element.20.refs_0_), kind=kOutput, calls=%fused_computation.11 | convolution fusion | flops 8592031744 | bytes 16777216 | tf_op jit(solution)/shard_map/dot_general | solution.py:31
  573.8 24.0 %convolution_convert_fusion = bf16[2048,2048]{1,0:T(8,128)(2,1)} fusion(bf16[2048,2048]{1,0:T(8,128)(2,1)} %gather_two.1, bf16[2048,1024]{1,0:T(8,128)(2,1)} %get-tuple-element.32, bf16[2048,1024]{1,0:T(8,128)(2,1)} %get-tuple-element.31), kind=kOutput, calls=%fused_computation.6 | convolution fusion | flops 17200840704 | bytes 25165824 | tf_op jit(solution)/shard_map/dot_general | solution.py:31
  597.9 3.9 slice.36.refs_1_
  601.9 44.5 %product_qkv.1 = f32[256,2048]{1,0:T(8,128)S(1)} custom-call(bf16[2048,768]{1,0:T(8,128)(2,1)S(1)} %copy-done.2, bf16[2048,768]{1,0:T(8,128)(2,1)} %slice.36.refs_1_), custom_call_target="tpu_custom_call" | custom-call | flops 6442450944 | bytes 125829120 | tf_op jit(solution)/shard_map/product_qkv/pallas_call | solution.py:274
  647.9 1.9 fusion.8
  649.8 2.9 all-to-all-start.6
  652.8 52.9 %product_down.1 = f32[256,2048]{1,0:T(8,128)S(1)} custom-call(bf16[2048,1024]{1,0:T(8,128)(2,1)} %get-tuple-element.20.refs_0_, bf16[2048,1024]{1,0:T(8,128)(2,1)} %all-gather.10.cloned.1.call-done.refs_1_), custom_call_target="tpu_custom_call" | custom-call | flops 8589934592 | bytes 125829120 | tf_op jit(solution)/shard_map/product_down/pallas_call | solution.py:274
  707.3 36.2 %all_to_all.113 = bf16[32,8,2048]{2,1,0:T(8,128)(2,1)} all-to-all(bf16[32,8,2048]{2,1,0:T(8,128)(2,1)} %fusion.7), channel_id=1, replica_groups=mesh['z'=4,'y'=2,'x'=2,'c'=2] {'z','y','x','c'}, dimensions={0} | all-to-all | bytes 2097152 | tf_op jit(solution)/shard_map/all_to_all | solution.py:465
  743.5 9.4 %all_to_all.114 = bf16[4,128,256]{2,1,0:T(8,128)(2,1)S(1)} all-to-all(bf16[4,128,256]{2,1,0:T(8,128)(2,1)} %bitcast.139), channel_id=1, replica_groups=mesh['z'=4,'y'=2,'x'=2,'c'=2] {'y','x'}, dimensions={0} | all-to-all | bytes 524288 | tf_op jit(solution)/shard_map/all_to_all | solution.py:324
  752.8 14.8 %all_to_all.115 = bf16[4,128,768]{2,1,0:T(8,128)(2,1)} all-to-all(bf16[4,128,768]{2,1,0:T(8,128)(2,1)} %bitcast.134), channel_id=1, replica_groups=mesh['z'=4,'y'=2,'x'=2,'c'=2] {'y','x'}, dimensions={0} | all-to-all | bytes 1572864 | tf_op jit(solution)/shard_map/all_to_all | solution.py:324
  767.6 15.7 %all_to_all.116 = bf16[4,128,1024]{2,1,0:T(8,128)(2,1)S(1)} all-to-all(bf16[4,128,1024]{2,1,0:T(8,128)(2,1)} %bitcast.129), channel_id=1, replica_groups=mesh['z'=4,'y'=2,'x'=2,'c'=2] {'y','x'}, dimensions={0} | all-to-all | bytes 2097152 | tf_op jit(solution)/shard_map/all_to_all | solution.py:324
  783.3 92.0 %reduce-scatter.9.cloned.1.call-done = bf16[512,2048]{1,0:T(8,128)(2,1)} async-done(((bf16[2048,2048]{1,0:T(8,128)(2,1)}), bf16[512,2048]{1,0:T(8,128)(2,1)}) %reduce-scatter.9.cloned.1.call-update) | async-done | bytes 2097168 | tf_op jit(solution)/shard_map/reduce_scatter | solution.py:309
  875.3 3.6 all-to-all-start.9
  878.9 3.1 fusion.11
  884.6 2.0 copy.137
  892.1 2.9 copy.140
  894.9 9.1 all-to-all-done.9
  (136 shorter events, 36.9 us)
Async XLA Ops:
  7.2 72.0 %copy-start = (bf16[256,2048]{1,0:T(8,128)(2,1)S(1)}, bf16[256,2048]{1,0:T(8,128)(2,1)}, u32[]{:S(2)}) copy-start(bf16[256,2048]{1,0:T(8,128)(2,1)} %param.12) | copy-start | bytes 3145732
  7.2 3.4 copy-start.14
  7.2 226.2 %all-gather.6.cloned.1.call-start = ((), (), s32[]{:S(2)}) async-start(), calls=%async_computation.15 | async-start | bytes 5242880 | tf_op jit(solution)/shard_map/all_gather | solution.py:305
  33.3 4.4 copy-start.11
  33.3 16.8 %all-to-all-start.4 = ((bf16[4,128,1024]{2,1,0:T(8,128)(2,1)}), bf16[4,128,1024]{2,1,0:T(8,128)(2,1)}, u32[]{:S(2)}, u32[]{:S(2)}) async-start(bf16[4,128,1024]{2,1,0:T(8,128)(2,1)} %bitcast.18), calls=%async_computation.4 | async-start | bytes 2097152 | tf_op jit(solution)/shard_map/all_to_all | solution.py:314
  37.6 306.6 %all-gather.10.cloned.1.call-start = ((), (), s32[]{:S(2)}) async-start(), calls=%async_computation.17 | async-start | bytes 5242880 | tf_op jit(solution)/shard_map/all_gather | solution.py:305
  37.7 1.8 copy-start.12
  40.0 38.9 %copy-start.23 = (s32[256]{0:T(256)S(1)}, s32[256]{0:T(256)}, u32[]{:S(2)}) copy-start(s32[256]{0:T(256)} %param.15) | copy-start | bytes 3076
  78.1 7.0 copy-start.25
  78.2 16.3 %copy-start.13 = (bf16[256,2048]{1,0:T(8,128)(2,1)S(1)}, bf16[256,2048]{1,0:T(8,128)(2,1)}, u32[]{:S(2)}) copy-start(bf16[256,2048]{1,0:T(8,128)(2,1)} %param.13) | copy-start | bytes 3145732
  78.2 302.5 %all-gather.8.cloned.1.call-start = ((), (), s32[]{:S(2)}) async-start(), calls=%async_computation.16 | async-start | bytes 10485760 | tf_op jit(solution)/shard_map/all_gather | solution.py:305
  79.2 16.9 %copy-start.17 = (s32[256]{0:T(256)}, s32[256]{0:T(256)S(1)}, u32[]{:S(2)}) copy-start(s32[256]{0:T(256)S(1)} %multiply_add_fusion.3) | copy-start | bytes 3076
  79.2 16.8 %copy-start.24 = (s32[256]{0:T(256)S(1)}, s32[256]{0:T(256)}, u32[]{:S(2)}) copy-start(s32[256]{0:T(256)} %param.16) | copy-start | bytes 3076
  80.7 52.3 %all-to-all-start = ((bf16[32,8,2048]{2,1,0:T(8,128)(2,1)}), bf16[32,8,2048]{2,1,0:T(8,128)(2,1)}, u32[]{:S(2)}, u32[]{:S(2)}) async-start(bf16[32,8,2048]{2,1,0:T(8,128)(2,1)} %fusion.5), calls=%async_computation | async-start | bytes 2097152 | tf_op jit(solution)/shard_map/all_to_all | solution.py:465
  133.0 57.7 %all-to-all-start.3 = ((bf16[32,8,2048]{2,1,0:T(8,128)(2,1)}), bf16[32,8,2048]{2,1,0:T(8,128)(2,1)}, u32[]{:S(2)}, u32[]{:S(2)}) async-start(bf16[32,8,2048]{2,1,0:T(8,128)(2,1)} %fusion.6), calls=%async_computation.3 | async-start | bytes 2097152 | tf_op jit(solution)/shard_map/all_to_all | solution.py:465
  136.4 607.1 %reduce-scatter.7.cloned.1.call-start = ((), (), s32[]{:S(2)}) async-start(), calls=%async_computation.19 | async-start | bytes 1310720 | tf_op jit(solution)/shard_map/reduce_scatter | solution.py:309
  138.5 52.1 %copy-start.19 = (s32[256]{0:T(256)}, s32[256]{0:T(256)S(1)}, u32[]{:S(2)}) copy-start(s32[256]{0:T(256)S(1)} %multiply_add_fusion.2) | copy-start | bytes 3076
  142.4 1.3 copy-start.4
  142.4 48.2 %copy-start.15 = (f32[256]{0:T(256)}, f32[256]{0:T(256)S(1)}, u32[]{:S(2)}) copy-start(f32[256]{0:T(256)S(1)} %broadcast_multiply_fusion.5) | copy-start | bytes 3076
  143.7 46.9 %copy-start.21 = (f32[256]{0:T(256)}, f32[256]{0:T(256)S(1)}, u32[]{:S(2)}) copy-start(f32[256]{0:T(256)S(1)} %add_rsqrt_fusion.1) | copy-start | bytes 3076
  258.3 1.2 copy-start.3
  259.6 43.3 %copy-start.5 = (f32[256,2048]{1,0:T(8,128)S(1)}, f32[256,2048]{1,0:T(8,128)}, u32[]{:S(2)}) copy-start(f32[256,2048]{1,0:T(8,128)} %copy-done.4) | copy-start | bytes 6291460
  477.0 1.2 copy-start.7
  527.5 225.3 %reduce-scatter.5.cloned.1.call-start = ((), (), s32[]{:S(2)}) async-start(), calls=%async_computation.18 | async-start | bytes 3932160 | tf_op jit(solution)/shard_map/reduce_scatter | solution.py:309
  559.1 208.5 %reduce-scatter.11.cloned.1.call-start = ((), (), s32[]{:S(2)}) async-start(), calls=%async_computation.21 | async-start | bytes 5242880 | tf_op jit(solution)/shard_map/reduce_scatter | solution.py:309
  573.8 301.5 %reduce-scatter.9.cloned.1.call-start = ((), (), s32[]{:S(2)}) async-start(), calls=%async_computation.20 | async-start | bytes 10485760 | tf_op jit(solution)/shard_map/reduce_scatter | solution.py:309
  597.9 3.9 copy-start.2
  601.8 44.5 %copy-start.6 = (f32[256,2048]{1,0:T(8,128)S(1)}, f32[256,2048]{1,0:T(8,128)}, u32[]{:S(2)}) copy-start(f32[256,2048]{1,0:T(8,128)} %copy-done.4) | copy-start | bytes 6291460
  601.8 44.5 %copy-start.16 = (f32[256]{0:T(256)S(1)}, f32[256]{0:T(256)}, u32[]{:S(2)}) copy-start(f32[256]{0:T(256)} %copy-done.15) | copy-start | bytes 3076
  601.8 44.5 %copy-start.22 = (f32[256]{0:T(256)S(1)}, f32[256]{0:T(256)}, u32[]{:S(2)}) copy-start(f32[256]{0:T(256)} %copy-done.21) | copy-start | bytes 3076
  646.3 1.6 copy-start.8
  646.4 1.6 copy-start.20
  649.8 57.4 %all-to-all-start.6 = ((bf16[32,8,2048]{2,1,0:T(8,128)(2,1)}), bf16[32,8,2048]{2,1,0:T(8,128)(2,1)S(1)}, u32[]{:S(2)}, u32[]{:S(2)}) async-start(bf16[32,8,2048]{2,1,0:T(8,128)(2,1)} %fusion.8), calls=%async_computation.6 | async-start | bytes 2097152 | tf_op jit(solution)/shard_map/all_to_all | solution.py:465
  707.3 60.3 %copy-start.9 = (bf16[32,8,2048]{2,1,0:T(8,128)(2,1)}, bf16[32,8,2048]{2,1,0:T(8,128)(2,1)S(1)}, u32[]{:S(2)}) copy-start(bf16[32,8,2048]{2,1,0:T(8,128)(2,1)S(1)} %all-to-all-done.6) | copy-start | bytes 3145732
  767.6 111.3 %copy-start.18 = (s32[256]{0:T(256)S(1)}, s32[256]{0:T(256)}, u32[]{:S(2)}) copy-start(s32[256]{0:T(256)} %copy-done.17) | copy-start | bytes 3076
  875.3 28.8 %all-to-all-start.9 = ((bf16[4,128,2048]{2,1,0:T(8,128)(2,1)}), bf16[4,128,2048]{2,1,0:T(8,128)(2,1)S(1)}, u32[]{:S(2)}, u32[]{:S(2)}) async-start(bf16[4,128,2048]{2,1,0:T(8,128)(2,1)} %bitcast.123), calls=%async_computation.12 | async-start | bytes 4194304 | tf_op jit(solution)/shard_map/all_to_all | solution.py:324
  878.9 3.1 copy-start.10
  904.5 2.9 copy-start.1
Sparse Core Ops, SparseCore 0:
  30.4 102.6 all-gather.5
  134.6 95.7 all-gather.9
  232.0 148.6 all-gather.7
  527.6 23.7 reduce-scatter.6
  559.3 56.6 reduce-scatter.4
  618.2 93.6 reduce-scatter.10
  714.3 160.9 reduce-scatter.8

commit v3 on v1

v3 whole, which is shorter than its diff:
```python
import functools
import math

import jax
import jax.numpy as jnp
from jax import lax
from jax.experimental import pallas as pl
from jax.experimental.pallas import tpu as pltpu
from jax.sharding import Mesh
from jax.sharding import PartitionSpec as P

HEAD_DIM = 128
SEGS = 4
EPSILON = 1e-05
NEG_LARGE = -1e30
F32 = jnp.float32
BF16 = jnp.bfloat16
MESH = pl.DeviceIdType.MESH
IDS = (
    "dispatch",
    "gather_one",
    "gather_two",
    "gather_middle",
    "product_out",
    "product_forward",
    "product_qkv",
    "product_down",
    "gather_up",
    "attend",
    "attend_back",
)


def project(left, right):
    return jnp.dot(left, right, preferred_element_type=F32)


def project_t(left, right):
    return lax.dot_general(left, right, (((1,), (1,)), ((), ())), preferred_element_type=F32)


def outer_sum(left, right):
    return lax.dot_general(left, right, (((0,), (0,)), ((), ())), preferred_element_type=F32)


def norm_parts(values):
    center = values - jnp.mean(values, axis=-1, keepdims=True)
    spread = jnp.mean(center * center, axis=-1, keepdims=True)
    scale = lax.rsqrt(spread + EPSILON)
    return center * scale, scale


def norm_back(normed, scale, gradient):
    mean_grad = jnp.mean(gradient, axis=-1, keepdims=True)
    mean_both = jnp.mean(gradient * normed, axis=-1, keepdims=True)
    return (gradient - mean_grad - normed * mean_both) * scale


def flip(*axes):
    return {axis: 1 - lax.axis_index(axis) for axis in axes}


def owner_at(step):
    total = lax.axis_size("z")
    return lax.rem(lax.axis_index("z") + total - step, total)


def greet(peers, ring):
    barrier = pltpu.get_barrier_semaphore()
    for axes in peers:
        pl.semaphore_signal(barrier, inc=1, device_id=flip(*axes), device_id_type=MESH)
    count = len(peers)
    if ring:
        pl.semaphore_signal(barrier, inc=1, device_id={"z": owner_at(1)}, device_id_type=MESH)
        count += 1
    pl.semaphore_wait(barrier, count)


def push(axes, source, target, send, recv):
    copy = pltpu.make_async_remote_copy(
        src_ref=source,
        dst_ref=target,
        send_sem=send,
        recv_sem=recv,
        device_id=flip(*axes),
        device_id_type=MESH,
    )
    copy.start()
    return copy


class Ride:
    def __init__(self, gathers=(), sums=()):
        self.gathers, self.sums = tuple(gathers), tuple(sums)
        self.operands, self.shapes, self.scratch = [], [], []
        self.aliases = {}
        self.steps = 0
        for whole, first, count in self.gathers:
            self.aliases[len(self.operands)] = len(self.shapes)
            self.operands.append(whole)
            self.shapes.append(jax.ShapeDtypeStruct(whole.shape, whole.dtype))
            self.steps += count
        for running, adds in self.sums:
            self.operands += [running, *adds]
            self.shapes.append(jax.ShapeDtypeStruct(running.shape, running.dtype))
            self.steps += 1 + len(adds)
            for _ in adds:
                self.scratch += [
                    pltpu.VMEM(running.shape, running.dtype),
                    pltpu.VMEM(running.shape, running.dtype),
                    pltpu.SemaphoreType.DMA(()),
                ]
        if self.steps:
            self.scratch += [
                pltpu.SemaphoreType.DMA((self.steps,)),
                pltpu.SemaphoreType.DMA((self.steps,)),
            ]

    def board(self, inputs, outputs, scratch):
        inputs, outputs, scratch = list(inputs), list(outputs), list(scratch)
        self.loads, self.copies, self.prepares, self.begun = [], [], [], 0
        if not self.steps:
            return
        send, recv = scratch[-2], scratch[-1]
        ahead = {"z": owner_at(lax.axis_size("z") - 1)}

        def plan(source, target, prepare=None):
            slot = len(self.copies)
            self.copies.append(
                pltpu.make_async_remote_copy(
                    src_ref=source,
                    dst_ref=target,
                    send_sem=send.at[slot],
                    recv_sem=recv.at[slot],
                    device_id=ahead,
                    device_id_type=MESH,
                )
            )
            self.prepares.append(prepare)

        def adding(load, landed, own):
            def prepare():
                load.wait()
                height = 64

                @pl.loop(0, own.shape[0] // height)
                def _(index):
                    at = pl.ds(pl.multiple_of(index * height, height), height)
                    own[at, :] = (own[at, :].astype(F32) + landed[at, :].astype(F32)).astype(BF16)

            return prepare

        for _, first, count in self.gathers:
            inputs.pop(0)
            whole = outputs.pop(0)
            rows = whole.shape[0] // lax.axis_size("z")
            for step in range(first, first + count):
                at = pl.ds(pl.multiple_of(owner_at(step) * rows, rows), rows)
                plan(whole.at[at], whole.at[at])
        for _, adds in self.sums:
            running = inputs.pop(0)
            final = outputs.pop(0)
            held = []
            for _ in adds:
                landed, own, loaded = scratch[:3]
                scratch = scratch[3:]
                load = pltpu.make_async_copy(inputs.pop(0), own, loaded)
                held.append((load, landed, own))
                self.loads.append(load)
            targets = [landed for _, landed, _ in held] + [final]
            plan(running, targets[0])
            for (load, landed, own), target in zip(held, targets[1:]):
                plan(own, target, adding(load, landed, own))

    def start(self, number):
        if self.prepares[number]:
            self.prepares[number]()
        self.copies[number].start()
        self.begun = number + 1

    def begin(self):
        for load in self.loads:
            load.start()
        if self.copies:
            self.start(0)

    def advance(self):
        if 0 < self.begun < len(self.copies):
            self.copies[self.begun - 1].wait_recv()
            self.start(self.begun)

    def finish(self):
        while self.begun < len(self.copies):
            self.advance()
        if self.copies:
            self.copies[-1].wait_recv()
        for copy in self.copies:
            copy.wait_send()


def block_at(core, y, x):
    def moved(axis, offset):
        here = lax.axis_index(axis)
        return 1 - here if offset else here

    return (moved("y", y) * 2 + moved("x", x)) * 2 + moved("c", core)


def communicate(body, operands, specs, shapes, out_specs, scratch, name, ride, flops=0):
    ride = ride or Ride()
    count_in, count_out, count_scratch = len(operands), len(shapes), len(scratch)
    all_in = count_in + len(ride.operands)
    all_out = count_out + len(ride.shapes)

    def kernel(*refs):
        inputs, outputs, held = refs[:all_in], refs[all_in : all_in + all_out], refs[all_in + all_out :]
        ride.board(inputs[count_in:], outputs[count_out:], held[count_scratch:])
        body(inputs[:count_in], outputs[:count_out], held[:count_scratch], ride)

    anywhere = pl.BlockSpec(memory_space=pl.ANY)
    got = pl.pallas_call(
        kernel,
        in_specs=list(specs) + [anywhere] * len(ride.operands),
        out_specs=list(out_specs) + [anywhere] * len(ride.shapes),
        out_shape=list(shapes) + ride.shapes,
        scratch_shapes=list(scratch) + ride.scratch,
        input_output_aliases={count_in + k: count_out + v for k, v in ride.aliases.items()},
        compiler_params=pltpu.CompilerParams(
            collective_id=IDS.index(name), has_side_effects=True, vmem_limit_bytes=50 << 20
        ),
        cost_estimate=pl.CostEstimate(
            flops=flops, bytes_accessed=120 << 20, transcendentals=0
        ),
        name=name,
    )(*operands, *ride.operands)
    return list(got)


class OwnRide(Ride):
    def __init__(self, count):
        super().__init__()
        self.steps = count

    def take(self, whole, semaphores):
        self.gathers = ((None, 0, self.steps),)
        super().board([None], [whole], semaphores)


def dispatch_kernel(count, narrow, steps, *refs):
    inputs, refs = refs[:count], refs[count:]
    places, packed, refs = refs[0], refs[1], refs[2:]
    wholes, refs = refs[: count - narrow + 1], refs[count - narrow + 1 :]
    all_places, landed, send, recv, local, rows_send, rows_recv = refs[:7]
    ride = OwnRide(steps)
    ride.take(wholes[0], refs[7:])
    me_y, me_x = lax.axis_index("y"), lax.axis_index("x")
    me_z, me_c = lax.axis_index("z"), lax.axis_index("c")
    rank = me_y * 2 + me_x
    rows = inputs[0].shape[0]
    at = pl.ds(pl.multiple_of(me_z * (4 * rows) + rank * rows, rows), rows)
    peers = ((("x",), me_y * 2 + 1 - me_x), (("y",), (1 - me_y) * 2 + me_x))
    peers += ((("y", "x"), (1 - me_y) * 2 + 1 - me_x),)

    def piece(index, owner):
        width = inputs[index].shape[1] // 4
        return inputs[index].at[:, pl.ds(pl.multiple_of(owner * width, width), width)]

    def target(index):
        width = inputs[index].shape[1] // 4
        if index < narrow:
            return wholes[0].at[at, pl.ds(index * width, width)]
        return wholes[index - narrow + 1].at[at]

    devices = packed.shape[0]
    me = (me_z * 4 + rank) * 2 + me_c
    keeps = [
        pltpu.make_async_copy(piece(index, rank), target(index), local.at[index])
        for index in range(count)
    ]
    keeps.append(pltpu.make_async_copy(places, all_places.at[rank], local.at[count]))
    keeps.append(pltpu.make_async_copy(packed.at[me], landed.at[me], local.at[count + 1]))
    for keep in keeps:
        keep.start()

    def device(shift):
        other = lax.rem(me + shift, devices)
        chip = other // 2
        return {"z": chip // 4, "y": lax.rem(chip // 2, 2), "x": lax.rem(chip, 2), "c": lax.rem(other, 2)}

    barrier = pltpu.get_barrier_semaphore()

    @pl.loop(1, devices)
    def _(shift):
        pl.semaphore_signal(barrier, inc=1, device_id=device(shift), device_id_type=MESH)

    pl.semaphore_wait(barrier, devices - 1)
    copies = {}

    def share(index, source_of, goal):
        for number, (axes, owner) in enumerate(peers):
            slot = 3 * index + number
            copies[index, number] = push(axes, source_of(owner), goal, send.at[slot], recv.at[slot])

    def arrive(index):
        keeps[index].wait()
        for number in range(3):
            copies[index, number].wait_recv()

    for index in range(narrow):
        share(index, functools.partial(piece, index), target(index))
    share(count, lambda owner: places, all_places.at[rank])

    @pl.loop(1, devices)
    def _(shift):
        other = lax.rem(me + shift, devices)
        pltpu.make_async_remote_copy(
            src_ref=packed.at[other],
            dst_ref=landed.at[me],
            send_sem=rows_send,
            recv_sem=rows_recv,
            device_id=device(shift),
            device_id_type=MESH,
        ).start()

    for index in range(narrow):
        arrive(index)
    ride.begin()
    for index in range(narrow, count):
        share(index, functools.partial(piece, index), target(index))
    most = pl.ds(0, devices - 1)
    pltpu.make_async_copy(packed.at[most], landed.at[most], rows_recv).wait()
    ride.advance()
    for index in range(narrow, count + 1):
        arrive(index)
    keeps[count + 1].wait()
    ride.finish()
    for copy in copies.values():
        copy.wait_send()
    pltpu.make_async_copy(packed.at[most], packed.at[most], rows_send).wait()


def dispatch(weights, narrow, places, packed, steps, name):
    rows = weights[0].shape[0]
    total = lax.axis_size("z")
    anywhere = pl.BlockSpec(memory_space=pl.ANY)
    count = len(weights)
    widths = [sum(weight.shape[1] // 4 for weight in weights[:narrow])]
    widths += [weight.shape[1] // 4 for weight in weights[narrow:]]
    shapes = [jax.ShapeDtypeStruct((total * 4 * rows, width), BF16) for width in widths]
    shapes.append(jax.ShapeDtypeStruct((4, *places.shape), places.dtype))
    shapes.append(jax.ShapeDtypeStruct(packed.shape, packed.dtype))
    return pl.pallas_call(
        functools.partial(dispatch_kernel, count, narrow, steps),
        in_specs=[anywhere] * (count + 2),
        out_specs=[anywhere] * len(shapes),
        out_shape=shapes,
        scratch_shapes=[
            pltpu.SemaphoreType.DMA((3 * count + 3,)),
            pltpu.SemaphoreType.DMA((3 * count + 3,)),
            pltpu.SemaphoreType.DMA((count + 2,)),
            pltpu.SemaphoreType.DMA(()),
            pltpu.SemaphoreType.DMA(()),
            pltpu.SemaphoreType.DMA((steps,)),
            pltpu.SemaphoreType.DMA((steps,)),
        ],
        compiler_params=pltpu.CompilerParams(
            collective_id=IDS.index(name), has_side_effects=True
        ),
        cost_estimate=pl.CostEstimate(flops=0, bytes_accessed=120 << 20, transcendentals=0),
        name=name,
    )(*weights, places, packed)


def gather_body(inputs, outputs, scratch, ride):
    (own,), (out,), (send, recv, local) = inputs, outputs, scratch
    rows = own.shape[0]
    half = rows // 2

    def part(core, y, x, side):
        start = block_at(core, y, x) * rows + side * half
        return out.at[pl.ds(pl.multiple_of(start, half), half)]

    def over(axis, source, target, slot):
        return push((axis,), source, target, send.at[slot], recv.at[slot])

    def across(y, x, side, slot):
        here = part(0, y, x, side)
        return over("c", here, here, slot)

    whole = out.at[pl.ds(pl.multiple_of(block_at(0, 0, 0) * rows, rows), rows)]
    keep = pltpu.make_async_copy(own, whole, local)
    keep.start()
    greet((("x",), ("y",), ("c",)), ride.steps > 0)
    first, second = own.at[pl.ds(0, half)], own.at[pl.ds(half, half)]
    x_first = over("x", first, part(0, 0, 0, 0), 0)
    y_second = over("y", second, part(0, 0, 0, 1), 1)
    x_second = over("x", second, part(0, 0, 0, 1), 2)
    y_first = over("y", first, part(0, 0, 0, 0), 3)
    ride.begin()
    crossed = [over("c", own, whole, 4)]
    x_first.wait_recv()
    far_first = over("y", part(0, 0, 1, 0), part(0, 0, 1, 0), 5)
    crossed.append(across(0, 1, 0, 6))
    y_second.wait_recv()
    far_second = over("x", part(0, 1, 0, 1), part(0, 1, 0, 1), 7)
    crossed.append(across(1, 0, 1, 8))
    x_second.wait_recv()
    crossed.append(across(0, 1, 1, 9))
    y_first.wait_recv()
    crossed.append(across(1, 0, 0, 10))
    ride.advance()
    far_first.wait_recv()
    crossed.append(across(1, 1, 0, 11))
    far_second.wait_recv()
    crossed.append(across(1, 1, 1, 12))
    for copy in crossed:
        copy.wait_recv()
    ride.finish()
    for copy in crossed + [x_first, y_second, x_second, y_first, far_first, far_second]:
        copy.wait_send()
    keep.wait()


def plane_gather(rows, name, ride=None):
    got = communicate(
        gather_body,
        [rows],
        [pl.BlockSpec(memory_space=pl.ANY)],
        [jax.ShapeDtypeStruct((8 * rows.shape[0], rows.shape[1]), rows.dtype)],
        [pl.BlockSpec(memory_space=pl.ANY)],
        [
            pltpu.SemaphoreType.DMA((13,)),
            pltpu.SemaphoreType.DMA((13,)),
            pltpu.SemaphoreType.DMA(()),
        ],
        name,
        ride,
    )
    return got[0], got[1:]


def product_body(starts, inputs, outputs, scratch, ride):
    (out_ref,) = outputs
    left, weight, away, got, near, by_y, by_x, end_y, end_x, send, recv, local = scratch
    block, width = out_ref.shape
    half = block // 2
    tile = 512
    pairs = [(inputs[2 * i], inputs[2 * i + 1], start) for i, start in enumerate(starts)]

    def over(axis, source, target, slot):
        return push((axis,), source, target, send.at[slot], recv.at[slot])

    waits = {"weight": []}
    column = 0
    for index, (rows_ref, weight_ref, start) in enumerate(pairs):
        inner = rows_ref.shape[1]
        copy = pltpu.make_async_copy(
            weight_ref.at[:, pl.ds(start, inner)],
            weight.at[:, pl.ds(column, inner)],
            local.at[index, 8],
        )
        copy.start()
        waits["weight"].append(copy)
        column += inner
    order = ((1, 1, 1), (1, 1, 0), (0, 1, 1), (1, 0, 1), (0, 1, 0), (1, 0, 0), (0, 0, 1), (0, 0, 0))
    for slot, key in enumerate(order):
        start = pl.multiple_of(block_at(*key) * block, block)
        waits[key] = []
        column = 0
        for index, (rows_ref, _, _) in enumerate(pairs):
            inner = rows_ref.shape[1]
            copy = pltpu.make_async_copy(
                rows_ref.at[pl.ds(start, block)],
                left.at[slot, :, pl.ds(column, inner)],
                local.at[index, slot],
            )
            copy.start()
            waits[key].append(copy)
            column += inner
    greet((("x",), ("y",), ("c",)), ride.steps > 0)
    ride.begin()
    for copy in waits["weight"]:
        copy.wait()

    def multiply(key, store):
        for copy in waits[key]:
            copy.wait()
        here = left[order.index(key)]

        @pl.loop(0, width // tile)
        def _(step):
            at = pl.ds(pl.multiple_of(step * tile, tile), tile)
            store(at, project_t(here, weight[at, :]))

    crossing = {}

    def compute_far(y, x):
        index = 2 * y + x

        def store(at, value):
            away[index, :, at] = value.astype(BF16)

        multiply((1, y, x), store)
        crossing[index] = over("c", away.at[index], got.at[index], index)

    def compute_near(y, x):
        index = 2 * y + x
        crossing[index].wait_recv()

        def store(at, value):
            near[index, :, at] = (value + got[index, :, at].astype(F32)).astype(BF16)

        multiply((0, y, x), store)

    lower, upper = pl.ds(0, half), pl.ds(half, half)
    compute_far(1, 1)
    compute_far(1, 0)
    compute_near(1, 1)
    y_far = over("y", near.at[3, lower], by_y.at[1], 4)
    x_far = over("x", near.at[3, upper], by_x.at[1], 5)
    compute_far(0, 1)
    compute_near(1, 0)
    y_near = over("y", near.at[2, lower], by_y.at[0], 6)
    compute_far(0, 0)
    compute_near(0, 1)
    x_near = over("x", near.at[1, upper], by_x.at[0], 7)
    compute_near(0, 0)
    y_far.wait_recv()
    near[1, lower, :] = (near[1, lower, :].astype(F32) + by_y[1].astype(F32)).astype(BF16)
    x_last = over("x", near.at[1, lower], end_x, 8)
    x_far.wait_recv()
    near[2, upper, :] = (near[2, upper, :].astype(F32) + by_x[1].astype(F32)).astype(BF16)
    y_last = over("y", near.at[2, upper], end_y, 9)
    ride.advance()
    y_near.wait_recv()
    out_ref[lower, :] = near[0, lower, :].astype(F32) + by_y[0].astype(F32)
    x_near.wait_recv()
    out_ref[upper, :] = near[0, upper, :].astype(F32) + by_x[0].astype(F32)
    x_last.wait_recv()
    out_ref[lower, :] += end_x[...].astype(F32)
    y_last.wait_recv()
    out_ref[upper, :] += end_y[...].astype(F32)
    ride.finish()
    for copy in list(crossing.values()) + [y_far, x_far, y_near, x_near, x_last, y_last]:
        copy.wait_send()


def plane_product(pairs, name, ride=None):
    total = pairs[0][0].shape[0]
    inner = sum(rows.shape[1] for rows, _, _ in pairs)
    width = pairs[0][1].shape[0]
    block = total // 8
    half = block // 2
    operands = []
    for rows, weight, _ in pairs:
        operands += [rows, weight]
    got = communicate(
        functools.partial(product_body, [start for _, _, start in pairs]),
        operands,
        [pl.BlockSpec(memory_space=pl.ANY)] * len(operands),
        [jax.ShapeDtypeStruct((block, width), F32)],
        [pl.BlockSpec(memory_space=pltpu.VMEM)],
        [
            pltpu.VMEM((8, block, inner), BF16),
            pltpu.VMEM((width, inner), BF16),
            pltpu.VMEM((4, block, width), BF16),
            pltpu.VMEM((4, block, width), BF16),
            pltpu.VMEM((4, block, width), BF16),
            pltpu.VMEM((2, half, width), BF16),
            pltpu.VMEM((2, half, width), BF16),
            pltpu.VMEM((half, width), BF16),
            pltpu.VMEM((half, width), BF16),
            pltpu.SemaphoreType.DMA((10,)),
            pltpu.SemaphoreType.DMA((10,)),
            pltpu.SemaphoreType.DMA((len(pairs), 9)),
        ],
        name,
        ride,
        flops=2 * total * inner * width,
    )
    return got[0], got[1:]


def ring_next(values):
    total = lax.axis_size("z")
    return lax.ppermute(values, "z", [(i, (i + 1) % total) for i in range(total)])


def ring_rows(whole, owner):
    rows = whole.shape[0] // lax.axis_size("z")
    return lax.dynamic_slice(whole, (owner * rows, 0), (rows, whole.shape[1]))


class Gathered:
    def __init__(self, whole, step=0):
        self.whole, self.step = whole, step

    def ride(self, count):
        count = min(count, lax.axis_size("z") - 1 - self.step)
        item = (self.whole, self.step, count)
        self.step += count
        return item

    def land(self, whole):
        self.whole = whole

    def walk(self, count):
        total = lax.axis_size("z")
        rows = self.whole.shape[0] // total
        last = min(self.step + count, total - 1)
        current = ring_rows(self.whole, owner_at(self.step)) if self.step < last else None
        while self.step < last:
            self.step += 1
            current = ring_next(current)
            self.whole = lax.dynamic_update_slice(self.whole, current, (owner_at(self.step) * rows, 0))

    def finish(self):
        self.walk(lax.axis_size("z"))
        return self.whole


class Summed:
    def __init__(self, whole):
        self.whole, self.step = whole, 0
        self.running = ring_rows(whole, owner_at(1))

    def block(self, step):
        return ring_rows(self.whole, owner_at((step + 1) % lax.axis_size("z")))

    def ride(self, count):
        count = min(count, lax.axis_size("z") - 1 - self.step)
        adds = tuple(self.block(self.step + 1 + k) for k in range(count - 1))
        self.step += count
        return (self.running, adds)

    def land(self, received):
        self.running = (received.astype(F32) + self.block(self.step).astype(F32)).astype(BF16)

    def walk(self, count):
        for _ in range(min(count, lax.axis_size("z") - 1 - self.step)):
            self.step += 1
            self.land(ring_next(self.running))

    def finish(self):
        self.walk(lax.axis_size("z"))
        return self.running


def from_plane(block):
    rows = block.shape[0] // 4
    me_y, me_x = lax.axis_index("y"), lax.axis_index("x")

    def piece(y, x):
        return lax.dynamic_slice(block, ((y * 2 + x) * rows, 0), (rows, block.shape[1]))

    own = piece(me_y, me_x)
    by_x = lax.ppermute(piece(me_y, 1 - me_x), "x", ((0, 1), (1, 0)))
    by_y = lax.ppermute(piece(1 - me_y, me_x), "y", ((0, 1), (1, 0)))
    far = lax.ppermute(piece(1 - me_y, 1 - me_x), ("y", "x"), ((0, 3), (1, 2), (2, 1), (3, 0)))

    def chosen(y, x):
        same_y, same_x = me_y == y, me_x == x
        return jnp.where(
            same_y, jnp.where(same_x, own, by_x), jnp.where(same_x, by_y, far)
        )

    return [chosen(y, x) for y in range(2) for x in range(2)]


def side_by_side(pieces, start=0, stop=None):
    return jnp.concatenate([piece[:, start:stop].astype(F32) for piece in pieces], axis=1)


def turn(values, cos_rows, sin_rows):
    return values * cos_rows + pltpu.roll(values, HEAD_DIM // 2, 1) * sin_rows


def visible_of(places):
    size = places.shape[0]
    row = lax.broadcasted_iota(jnp.int32, (size, size), 0)
    column = lax.broadcasted_iota(jnp.int32, (size, size), 1)
    return (column <= row) & (row - column <= places)


def soft_of(queries, keys, visible):
    scores = project_t(queries, keys) * (1.0 / math.sqrt(HEAD_DIM))
    scores = jnp.where(visible, scores, NEG_LARGE)
    weights = jnp.exp(scores - jnp.max(scores, axis=1, keepdims=True))
    return weights / jnp.sum(weights, axis=1, keepdims=True)


def attend_body(inputs, outputs):
    seen_ref, weight_ref, cos_ref, sin_ref, place_ref = inputs
    low_ref, out_ref = outputs
    width = out_ref.shape[1]
    cos_rows, sin_rows = cos_ref[...], sin_ref[...]
    visible = visible_of(place_ref[...])
    lin = project(seen_ref[...], weight_ref[...])
    for start in range(0, width, HEAD_DIM):
        here = slice(start, start + HEAD_DIM)
        key_at = slice(width + start, width + start + HEAD_DIM)
        value_at = slice(2 * width + start, 2 * width + start + HEAD_DIM)
        queries = turn(lin[:, here], cos_rows, sin_rows).astype(BF16)
        keys = turn(lin[:, key_at], cos_rows, sin_rows).astype(BF16)
        values = lin[:, value_at].astype(BF16)
        low_ref[:, here] = queries
        low_ref[:, key_at] = keys
        low_ref[:, value_at] = values
        soft = soft_of(queries, keys, visible).astype(BF16)
        out_ref[:, here] = project(soft, values).astype(BF16)


def attend_back_body(inputs, outputs):
    low_ref, seen_ref, weight_ref, cos_ref, sin_ref, place_ref = inputs
    (out_ref,) = outputs
    width = weight_ref.shape[1]
    cos_rows, sin_rows = cos_ref[...], -sin_ref[...]
    visible = visible_of(place_ref[...])
    scale = 1.0 / math.sqrt(HEAD_DIM)
    grad_all = project(seen_ref[...], weight_ref[...]).astype(BF16)
    for start in range(0, width, HEAD_DIM):
        here = slice(start, start + HEAD_DIM)
        key_at = slice(width + start, width + start + HEAD_DIM)
        value_at = slice(2 * width + start, 2 * width + start + HEAD_DIM)
        queries, keys, values = low_ref[:, here], low_ref[:, key_at], low_ref[:, value_at]
        grad = grad_all[:, here]
        soft = soft_of(queries, keys, visible)
        grad_soft = project_t(grad, values)
        inner = jnp.sum(soft * grad_soft, axis=1, keepdims=True)
        grad_scores = (soft * (grad_soft - inner)).astype(BF16)
        grad_query = project(grad_scores, keys) * scale
        grad_key = outer_sum(grad_scores, queries) * scale
        out_ref[:, here] = turn(grad_query, cos_rows, sin_rows).astype(BF16)
        out_ref[:, key_at] = turn(grad_key, cos_rows, sin_rows).astype(BF16)
        out_ref[:, value_at] = outer_sum(soft.astype(BF16), grad).astype(BF16)


def plane_peers():
    me_y, me_x = lax.axis_index("y"), lax.axis_index("x")
    return (
        (("x",), me_y * 2 + 1 - me_x),
        (("y",), (1 - me_y) * 2 + me_x),
        (("y", "x"), (1 - me_y) * 2 + 1 - me_x),
    )


def collect_copies(blocks, outs, send, recv, local):
    rank = lax.axis_index("y") * 2 + lax.axis_index("x")
    keeps, copies = [], []
    for index, (block, out) in enumerate(zip(blocks, outs)):
        rows = block.shape[0] // 4

        def piece(owner, block=block, rows=rows):
            return block.at[pl.ds(pl.multiple_of(owner * rows, rows), rows)]

        keeps.append(pltpu.make_async_copy(piece(rank), out.at[rank], local.at[index]))
        for number, (axes, owner) in enumerate(plane_peers()):
            copies.append(
                pltpu.make_async_remote_copy(
                    src_ref=piece(owner),
                    dst_ref=out.at[rank],
                    send_sem=send.at[3 * index + number],
                    recv_sem=recv.at[3 * index + number],
                    device_id=flip(*axes),
                    device_id_type=MESH,
                )
            )
    return keeps, copies


def collected_shape(block):
    return jax.ShapeDtypeStruct((4, block.shape[0] // 4, block.shape[1]), block.dtype)


def by_blocks(body, operands, specs, shapes, out_specs, blocks, name, ride, flops, collect=()):
    extra = len(collect)
    operands, shapes = list(operands) + list(collect), list(shapes)
    shapes += [collected_shape(block) for block in collect]
    anywhere = pl.BlockSpec(memory_space=pl.ANY)
    specs, out_specs = list(specs) + [anywhere] * extra, list(out_specs) + [anywhere] * extra
    scratch = []
    if extra:
        scratch = [
            pltpu.SemaphoreType.DMA((3 * extra,)),
            pltpu.SemaphoreType.DMA((3 * extra,)),
            pltpu.SemaphoreType.DMA((extra,)),
        ]
    count_in, count_out = len(operands), len(shapes)
    all_in = count_in + len(ride.operands)
    all_out = count_out + len(ride.shapes)

    def kernel(*refs):
        inputs, outputs, held = refs[:all_in], refs[all_in : all_in + all_out], refs[all_in + all_out :]
        step = pl.program_id(0)
        ride.board(inputs[count_in:], outputs[count_out:], held[len(scratch) :])
        keeps, copies = [], []
        if extra:
            keeps, copies = collect_copies(
                inputs[count_in - extra : count_in], outputs[count_out - extra : count_out], *held[:3]
            )
        if ride.copies or extra:

            @pl.when(step == 0)
            def _():
                greet([axes for axes, _ in plane_peers()] if extra else (), bool(ride.copies))
                ride.begin()
                for copy in keeps + copies:
                    copy.start()

        body(inputs[: count_in - extra], outputs[: count_out - extra])
        if ride.copies or extra:

            @pl.when(step == blocks - 1)
            def _():
                for copy in keeps:
                    copy.wait()
                for copy in copies:
                    copy.wait()
                ride.finish()

    params = {"collective_id": IDS.index(name), "has_side_effects": True} if ride.steps or extra else {}
    got = pl.pallas_call(
        kernel,
        grid=(blocks,),
        in_specs=list(specs) + [anywhere] * len(ride.operands),
        out_specs=list(out_specs) + [anywhere] * len(ride.shapes),
        out_shape=list(shapes) + ride.shapes,
        scratch_shapes=scratch + ride.scratch,
        input_output_aliases={count_in + k: count_out + v for k, v in ride.aliases.items()},
        compiler_params=pltpu.CompilerParams(vmem_limit_bytes=40 << 20, **params),
        cost_estimate=pl.CostEstimate(flops=flops, bytes_accessed=40 << 20, transcendentals=0),
        name=name,
    )(*operands, *ride.operands)
    return list(got)


def row_spec(rows, columns):
    return pl.BlockSpec((rows, columns), lambda i: (i, 0))


def attend(seen, weight, cos_rows, sin_rows, places, block, ride):
    rows, depth = seen.shape
    width = weight.shape[1] // 4
    got = by_blocks(
        attend_body,
        [seen, weight, cos_rows, sin_rows, places],
        [
            row_spec(block, depth),
            pl.BlockSpec((depth, 3 * width), lambda i: (0, 0)),
            row_spec(block, HEAD_DIM),
            row_spec(block, HEAD_DIM),
            row_spec(block, 1),
        ],
        [
            jax.ShapeDtypeStruct((rows, 3 * width), BF16),
            jax.ShapeDtypeStruct((rows, width), BF16),
        ],
        [row_spec(block, 3 * width), row_spec(block, width)],
        rows // block,
        "attend",
        ride,
        4 * rows * block * width + 6 * rows * depth * width,
    )
    return got[:2], got[2:]


def attend_back(low, seen, weight, cos_rows, sin_rows, places, block, ride, collect):
    rows, depth = seen.shape
    width = weight.shape[1] // 4
    got = by_blocks(
        attend_back_body,
        [low, seen, weight, cos_rows, sin_rows, places],
        [
            row_spec(block, 3 * width),
            row_spec(block, depth),
            pl.BlockSpec((depth, width), lambda i: (0, 3)),
            row_spec(block, HEAD_DIM),
            row_spec(block, HEAD_DIM),
            row_spec(block, 1),
        ],
        [jax.ShapeDtypeStruct((rows, 3 * width), BF16)],
        [row_spec(block, 3 * width)],
        rows // block,
        "attend_back",
        ride,
        10 * rows * block * width + 2 * rows * depth * width,
        collect,
    )
    last = 1 + len(collect)
    return got[:last], got[last:]


def plane_places(segments):
    groups, size = segments.shape
    numbers = jnp.arange(SEGS, dtype=jnp.int32)
    starts = jnp.sum((segments[:, :, None] < numbers).astype(jnp.int32), axis=1)
    onehot = segments[:, :, None] == numbers
    offset = jnp.sum(jnp.where(onehot, starts[:, None, :], 0), axis=2)
    places = jnp.arange(size, dtype=jnp.int32)[None, :] - offset
    return places.reshape(-1, 1)


def after(values, *gates):
    return lax.optimization_barrier((values,) + gates)[0]


EVERY = ("z", "y", "x", "c")


def exchange(rows):
    return lax.all_to_all(rows, EVERY, split_axis=0, concat_axis=0, tiled=True)


def on_device(
    tokens_in,
    cotangent,
    segment_ids,
    destination,
    source,
    w_query,
    w_key,
    w_value,
    w_out,
    w_gate,
    w_up,
    w_down,
):
    tok_rows = tokens_in.shape[0]
    devices = lax.axis_size(EVERY)
    per_peer = tok_rows // devices
    row_index = jnp.arange(tok_rows, dtype=jnp.int32)
    peer_to = destination // tok_rows
    ahead_rows = (peer_to[None, :] == peer_to[:, None]) & (
        destination[None, :] < destination[:, None]
    )
    send_slot = peer_to * per_peer + jnp.sum(ahead_rows.astype(jnp.int32), axis=1)
    peer_from = source // tok_rows
    before = (peer_from[None, :] == peer_from[:, None]) & (row_index[None, :] < row_index[:, None])
    recv_slot = peer_from * per_peer + jnp.sum(before.astype(jnp.int32), axis=1)
    send_pick = (send_slot[:, None] == row_index[None, :]).astype(BF16)
    recv_pick = (recv_slot[:, None] == row_index[None, :]).astype(BF16)

    packed = outer_sum(send_pick, tokens_in).astype(BF16)
    weights = [w_query, w_key, w_value, w_out.T, w_gate, w_up, w_down.T]
    attention_whole, gate_whole, up_whole, down_whole, segments, landed = dispatch(
        [weight.astype(BF16) for weight in weights],
        4,
        segment_ids.reshape(-1, 128),
        packed.reshape(devices, per_peer, -1),
        1,
        "dispatch",
    )
    arrived = project(recv_pick, landed.reshape(tok_rows, -1))
    attention_w, gate_w = Gathered(attention_whole, 1), Gathered(gate_whole)
    up_w, down_w = Gathered(up_whole), Gathered(down_whole)
    head_width = w_query.shape[1] // 4
    places = plane_places(segments.reshape(4, -1))
    half_dim = HEAD_DIM // 2
    frequency = jnp.exp(
        -jnp.arange(half_dim, dtype=F32) * (2.0 * math.log(10000.0) / HEAD_DIM)
    )
    angles = places.astype(F32) * frequency[None, :]
    cos_half, sin_half = jnp.cos(angles), jnp.sin(angles)
    cos_rows = jnp.concatenate([cos_half, cos_half], axis=1)
    sin_rows = jnp.concatenate([-sin_half, sin_half], axis=1)

    normed_one, scale_one = norm_parts(arrived)
    def give_back(rows):
        packed = outer_sum(recv_pick, rows.astype(BF16)).astype(BF16)
        return project(send_pick, exchange(packed))

    def riding(call, gathers=(), sums=()):
        ride = Ride(
            [weight.ride(count) for weight, count in gathers],
            [gradient.ride(count) for gradient, count in sums],
        )
        result, landed = call(ride)
        for (item, _), value in zip(tuple(gathers) + tuple(sums), landed):
            item.land(value)
        return result

    seen_one = riding(
        lambda ride: plane_gather(normed_one.astype(BF16), "gather_one", ride),
        [(attention_w, 2)],
    )
    attention = attention_w.finish()
    upstream_low = project(
        recv_pick,
        exchange(outer_sum(send_pick, after(cotangent, seen_one)).astype(BF16)),
    ).astype(BF16)
    upstream = upstream_low.astype(F32)
    qkv_low, attended = riding(
        lambda ride: attend(seen_one, attention, cos_rows, sin_rows, places, tok_rows, ride),
        [(gate_w, 1)],
    )
    middle = arrived + riding(
        lambda ride: plane_product([(attended, attention, 3 * head_width)], "product_out", ride),
        [(gate_w, 2)],
    )
    normed_two, scale_two = norm_parts(middle)
    seen_two = riding(
        lambda ride: plane_gather(normed_two.astype(BF16), "gather_two", ride), [(up_w, 2)]
    )
    grad_two_all = riding(
        lambda ride: plane_gather(after(upstream_low, seen_two), "gather_up", ride),
        [(up_w, 1), (down_w, 1)],
    )
    gate_whole, up_whole = gate_w.finish(), up_w.finish()
    down_w.walk(1)
    gate_lin = project(after(seen_two, grad_two_all), gate_whole)
    up_lin = project(seen_two, up_whole)
    sigmoid = jax.nn.sigmoid(gate_lin)
    hidden = (gate_lin * sigmoid * up_lin).astype(BF16)
    weight_down = outer_sum(after(grad_two_all, down_w.whole, hidden), hidden).astype(BF16)
    down_whole = down_w.finish()
    weight_down = after(weight_down, down_whole)
    summed_down = Summed(weight_down)
    grad_hidden = project(after(grad_two_all, weight_down), down_whole)
    summed_down.walk(2)
    grad_gate = (grad_hidden * up_lin * (sigmoid * (1.0 + gate_lin * (1.0 - sigmoid)))).astype(BF16)
    grad_up = (grad_hidden * (gate_lin * sigmoid)).astype(BF16)
    weight_gate = outer_sum(seen_two, grad_gate).astype(BF16)
    summed_gate = Summed(weight_gate)
    summed_up = Summed(outer_sum(seen_two, grad_up).astype(BF16))
    grad_normed_two = riding(
        lambda ride: plane_product(
            [(after(grad_gate, weight_gate), gate_whole, 0), (grad_up, up_whole, 0)],
            "product_forward",
            ride,
        ),
        (),
        [(summed_down, 1), (summed_gate, 1)],
    )
    output = middle + riding(
        lambda ride: plane_product(
            [(after(hidden, grad_normed_two), down_whole, 0)], "product_down", ride
        ),
        (),
        [(summed_gate, 2)],
    )
    layer_out = give_back(output)
    grad_middle = upstream + norm_back(normed_two, scale_two, grad_normed_two)
    grad_one_all = riding(
        lambda ride: plane_gather(
            after(grad_middle.astype(BF16), output), "gather_middle", ride
        ),
        (),
        [(summed_up, 2)],
    )
    grad_qkv, own_down, own_gate = riding(
        lambda ride: attend_back(
            qkv_low,
            grad_one_all,
            attention,
            cos_rows,
            sin_rows,
            places,
            tok_rows,
            ride,
            (summed_down.finish(), summed_gate.finish()),
        ),
        (),
        [(summed_up, 1)],
    )
    own_up = from_plane(summed_up.finish())
    summed_attention = Summed(
        jnp.concatenate(
            [
                outer_sum(seen_one, grad_qkv).astype(BF16),
                outer_sum(grad_one_all, attended).astype(BF16),
            ],
            axis=1,
        )
    )
    grad_normed_one = riding(
        lambda ride: plane_product(
            [
                (
                    after(grad_qkv, summed_attention.whole, layer_out, *own_up),
                    attention,
                    0,
                )
            ], "product_qkv", ride
        ),
        (),
        [(summed_attention, 2)],
    )
    grad_inputs = grad_middle + norm_back(normed_one, scale_one, grad_normed_one)
    own_attention = from_plane(summed_attention.finish())

    return (
        layer_out,
        give_back(grad_inputs),
        side_by_side(own_attention, 0, head_width),
        side_by_side(own_attention, head_width, 2 * head_width),
        side_by_side(own_attention, 2 * head_width, 3 * head_width),
        side_by_side(own_attention, 3 * head_width).T,
        side_by_side(own_gate),
        side_by_side(own_up),
        side_by_side(own_down).T,
    )


def solution(mesh):
    groups, cores = mesh.shape["dp"], mesh.shape["tensor"]
    whole = Mesh(mesh.devices.reshape(groups // 4, 2, 2, cores), EVERY)
    rows = P(EVERY, None)
    tall = P(("z", "y", "x"), "c")
    wide = P("c", ("z", "y", "x"))
    in_specs = (
        rows,
        rows,
        P(("z", "y", "x")),
        P(EVERY),
        P(EVERY),
        tall,
        tall,
        tall,
        wide,
        tall,
        tall,
        wide,
    )
    out_specs = (rows, rows, tall, tall, tall, wide, tall, tall, wide)
    return jax.shard_map(
        on_device, mesh=whole, in_specs=in_specs, out_specs=out_specs, check_vma=False
    )
```

time: 1030 us -> 822 us (0.80)
  Pallas kernels: 24.4 us -> 539 us
  waiting for transfers between devices: 468 us -> 56.9 us
  matrix products: 238 us -> 117 us
  local copies, waits for them, and re-layouts: 107 us -> 25.1 us
  starting transfers between devices: 104 us -> 25.5 us
  blocking collectives: 16.4 us -> 0 us
  other arithmetic: 59.8 us -> 47.9 us
    pallas_call x2 -> x11, Pallas kernels: 24.4 us -> 539 us  [the longest x8 412 us: communicate(): pl.pallas_call(kernel, in_specs=list(specs) + [anywhere] * len(ride.opera...]
    ppermute x21 -> x5, waiting for transfers between devices: 236 us -> 33.8 us  [ring_next(): lax.ppermute(values, 'z', [(i, (i + 1) % total) for i in range(total)])]
    ppermute x40 -> x6, waiting for transfers between devices: 167 us -> 13 us  [the longest x2 8.12 us: from_plane(): lax.ppermute(piece(1 - me_y, 1 - me_x), ('y', 'x'), ((0, 3), (1, 2), (2,...]
    dot_general x8 -> x0, matrix products: 66.1 us -> none  [project_t(): lax.dot_general(left, right, (((1,), (1,)), ((), ())), preferred_element_...]
    all_to_all x4 -> x3, waiting for transfers between devices: 54.9 us -> 10 us  [exchange(): return lax.all_to_all(rows, EVERY, split_axis=0, concat_axis=0, tiled=True)]
    dot_general x20 -> x9, matrix products: 98.4 us -> 58.7 us  [outer_sum(): lax.dot_general(left, right, (((0,), (0,)), ((), ())), preferred_element_...]
    unnamed x194 -> x110, local copies, waits for them, and re-layouts: 53.5 us -> 19.7 us
    ppermute x40 -> x6, starting transfers between devices: 39.8 us -> 7.26 us  [the longest x2 4.6 us: from_plane(): lax.ppermute(piece(1 - me_y, 1 - me_x), ('y', 'x'), ((0, 3), (1, 2), (2,...]
  transfers between devices with their start and end apart: 72 -> 14, of which waited for: 36 -> 6; matrix products, arithmetic and copies ran while one was open for 31% -> 16% of each run, Pallas kernels for 2% -> 17%
where the time goes in v3:
time: 822 us; the launch traced here: 813 us
  Pallas kernels  539 us (66%)
  matrix products  117 us (14%)
  waiting for transfers between devices  56.9 us (7%)
  other arithmetic  47.9 us (6%)
  starting transfers between devices  25.5 us (3%)
  local copies, waits for them, and re-layouts  25.1 us (3%)
    pallas_call x8, Pallas kernels, communicate(): pl.pallas_call(kernel, in_specs=list(specs) + [anywhere] * len(ride.opera...  412 us
    pallas_call x1, Pallas kernels, dispatch(): pl.pallas_call(functools.partial(dispatch_kernel, count, narrow, steps),...  67.2 us
    pallas_call x2, Pallas kernels, by_blocks(): pl.pallas_call(kernel, grid=(blocks,), in_specs=list(specs) + [anywhere]...  59.5 us
    dot_general x9, matrix products, outer_sum(): lax.dot_general(left, right, (((0,), (0,)), ((), ())), preferred_element_...  58.7 us
    dot_general x7, matrix products, project(): return jnp.dot(left, right, preferred_element_type=F32)  58.2 us
    ppermute x5, waiting for transfers between devices, ring_next(): lax.ppermute(values, 'z', [(i, (i + 1) % total) for i in range(total)])  33.8 us
    unnamed x110, local copies, waits for them, and re-layouts  19.7 us
  transfers between devices with their start and end apart: 14, of which 6 were waited for; matrix products, arithmetic and copies ran while one was open for 16% of the time, Pallas kernels for 17%

profile of v3, /device:TPU:0, one launch (start us, length us, event | category | flops | bytes accessed | tf_op | source)
XLA Modules:
  0.0 813.4 jit_solution(4465712272932777844)
XLA Ops:
  2.5 2.6 copy.44
  12.9 67.2 %dispatch.1 = (bf16[2048,1024]{1,0:T(8,128)(2,1)}, bf16[2048,1024]{1,0:T(8,128)(2,1)}, bf16[2048,1024]{1,0:T(8,128)(2,1)}, bf16[2048,1024]{1,0:T(8,128)(2,1)}, s...) custom-call(bf16[128,1024]{1,0:T(8,128)(2,1)} %convert_element_type.239.refs_0_, ...), custom_call_target="tpu_custom_call" | custom-call | bytes 125829120 | tf_op jit(solution)/shard_map/dispatch/pallas_call | solution.py:352
  80.1 1.8 fusion.42
  83.2 51.5 %gather_one.1 = (bf16[2048,2048]{1,0:T(8,128)(2,1)}, bf16[2048,1024]{1,0:T(8,128)(2,1)}) custom-call(bf16[256,2048]{1,0:T(8,128)(2,1)S(1)} %fusion.5.refs_0_, bf16[2048,1024]{1,0:T(8,128)(2,1)} %get-tuple-element.51.refs_1_), custom_call_target="tpu_custom_call", output_to_operand_aliasing={{1}: (1, {})} | custom-call | bytes 125829120 | tf_op jit(solution)/shard_map/gather_one/pallas_call | solution.py:221
  136.3 3.4 all-to-all-start
  140.0 5.4 fusion.23
  147.7 2.6 copy-done.4
  150.2 33.4 %attend.1 = (bf16[2048,768]{1,0:T(8,128)(2,1)S(1)}, bf16[2048,256]{1,0:T(8,128)(2,1)S(1)}, bf16[2048,1024]{1,0:T(8,128)(2,1)S(1)}) custom-call(bf16[2048,2048]{1,0:T(8,128)(2,1)} %get-tuple-element.52.refs_0_, bf16[2048,1024]{1,0:T(8,128)(2,1)} %get-tuple-element.53.refs_1_.refs_2_, ...), custom_call_target="tpu_custom_call", output_to_operand_aliasing={{2}: (5, {})} | custom-call | flops 6979321856 | bytes 41943040 | tf_op jit(solution)/shard_map/attend/pallas_call | solution.py:822
  183.6 2.0 copy-done.5
  187.3 56.0 %product_out.1 = (f32[256,2048]{1,0:T(8,128)S(1)}, bf16[2048,1024]{1,0:T(8,128)(2,1)}) custom-call(bf16[2048,256]{1,0:T(8,128)(2,1)S(1)} %get-tuple-element.56.refs_0_, bf16[2048,1024]{1,0:T(8,128)(2,1)} %get-tuple-element.53.refs_1_.refs_2_, bf16[2048,1024]{1,0:T(8,128)(2,1)} %copy-done.5), custom_call_target="tpu_custom_call", output_to_operand_aliasing={{1}: (2, {})} | custom-call | flops 2147483648 | bytes 125829120 | tf_op jit(solution)/shard_map/product_out/pallas_call | solution.py:221
  244.9 48.7 %gather_two.1 = (bf16[2048,2048]{1,0:T(8,128)(2,1)}, bf16[2048,1024]{1,0:T(8,128)(2,1)}) custom-call(bf16[256,2048]{1,0:T(8,128)(2,1)S(1)} %fusion.6.refs_0_, bf16[2048,1024]{1,0:T(8,128)(2,1)} %get-tuple-element.59.refs_1_), custom_call_target="tpu_custom_call", output_to_operand_aliasing={{1}: (1, {})} | custom-call | bytes 125829120 | tf_op jit(solution)/shard_map/gather_two/pallas_call | solution.py:221
  295.4 48.5 %gather_up.1 = (bf16[2048,2048]{1,0:T(8,128)(2,1)}, bf16[2048,1024]{1,0:T(8,128)(2,1)}, bf16[2048,1024]{1,0:T(8,128)(2,1)}) custom-call(bf16[256,2048]{1,0:T(8,128)(2,1)S(1)} %convolution_convert_fusion.6.refs_0_, bf16[2048,1024]{1,0:T(8,128)(2,1)} %get-tuple-element.63.refs_1_, ...), custom_call_target="tpu_custom_call", output_to_operand_aliasing={{1}: (1, {}), {2}: (2, {})} | custom-call | bytes 125829120 | tf_op jit(solution)/shard_map/gather_up/pallas_call | solution.py:221
  345.2 1.8 collective-permute-start
  347.0 13.3 %fusion.43 = f32[2048,1024]{1,0:T(8,128)} fusion(bf16[2048,2048]{1,0:T(8,128)(2,1)} %get-tuple-element.66, bf16[2048,1024]{1,0:T(8,128)(2,1)S(1)} %copy-done.6), kind=kOutput, calls=%fused_computation.166 | convolution fusion | flops 8589934592 | bytes 20971520 | tf_op jit(solution)/shard_map/dot_general | solution.py:35
  360.3 15.1 %multiply_convert_fusion.2 = (bf16[2048,1024]{1,0:T(8,128)(2,1)S(1)}, f32[2048,1024]{1,0:T(8,128)}) fusion(f32[2048,1024]{1,0:T(8,128)} %fusion.43, bf16[2048,2048]{1,0:T(8,128)(2,1)} %get-tuple-element.66, bf16[2048,1024]{1,0:T(8,128)(2,1)S(1)} %copy-done.19), kind=kOutput, calls=%fused_computation.7 | convolution fusion | flops 8602517504 | bytes 33554432 | tf_op jit(solution)/shard_map/dot_general | solution.py:35
  377.4 11.5 %convolution_convert_fusion.2 = bf16[2048,1024]{1,0:T(8,128)(2,1)S(1)} fusion(bf16[2048,2048]{1,0:T(8,128)(2,1)} %get-tuple-element.72, bf16[2048,1024]{1,0:T(8,128)(2,1)S(1)} %get-tuple-element.75.refs_0_), kind=kOutput, calls=%fused_computation.16 | convolution fusion | flops 8592031744 | bytes 16777216 | tf_op jit(solution)/shard_map/dot_general | solution.py:43
  388.9 10.1 %collective-permute-done.1 = bf16[512,1024]{1,0:T(8,128)(2,1)S(1)} collective-permute-done((bf16[512,1024]{1,0:T(8,128)(2,1)S(1)}, bf16[512,1024]{1,0:T(8,128)(2,1)S(1)}, u32[]{:S(2)}, u32[]{:S(2)}) %collective-permute-start.1) | collective-permute-done | bytes 1048608 | tf_op jit(solution)/shard_map/ppermute | solution.py:586
  399.7 21.5 %multiply_convert_fusion = (bf16[2048,1024]{1,0:T(8,128)(2,1)}, bf16[2048,1024]{1,0:T(8,128)(2,1)}) fusion(f32[2048,1024]{1,0:T(8,128)} %fusion.43, f32[2048,1024]{1,0:T(8,128)} %get-tuple-element.180, bf16[2048,2048]{1,0:T(8,128)(2,1)} %get-tuple-element.72, bf16[2048,1024]{1,0:T(8,128)(2,1)S(1)} %constant_dynamic-update-slice_fusion.refs_1_), kind=kOutput, calls=%fused_computation.5 | convolution fusion | flops 8617197568 | bytes 37748736 | tf_op jit(solution)/shard_map/dot_general | solution.py:35
  421.2 12.8 %convolution_convert_fusion = bf16[2048,1024]{1,0:T(8,128)(2,1)S(1)} fusion(bf16[2048,2048]{1,0:T(8,128)(2,1)} %get-tuple-element.66, bf16[2048,1024]{1,0:T(8,128)(2,1)} %get-tuple-element.126.refs_2_), kind=kOutput, calls=%fused_computation.14 | convolution fusion | flops 8592031744 | bytes 16777216 | tf_op jit(solution)/shard_map/dot_general | solution.py:43
  434.0 2.4 add_convert_fusion.9
  436.5 1.7 collective-permute-start.3
  438.2 11.5 %convolution_convert_fusion.1 = bf16[2048,1024]{1,0:T(8,128)(2,1)S(1)} fusion(bf16[2048,2048]{1,0:T(8,128)(2,1)} %get-tuple-element.66, bf16[2048,1024]{1,0:T(8,128)(2,1)S(1)} %copy-done.50), kind=kOutput, calls=%fused_computation.15 | convolution fusion | flops 8592031744 | bytes 16777216 | tf_op jit(solution)/shard_map/dot_general | solution.py:43
  453.2 5.9 collective-permute-done.3
  459.5 53.8 %product_forward.1 = (f32[256,2048]{1,0:T(8,128)}, bf16[512,1024]{1,0:T(8,128)(2,1)S(1)}, bf16[512,1024]{1,0:T(8,128)(2,1)S(1)}) custom-call(bf16[2048,1024]{1,0:T(8,128)(2,1)} %get-tuple-element.73.refs_0_, bf16[2048,1024]{1,0:T(8,128)(2,1)} %get-tuple-element.67.refs_1_, bf16[2048,1024]{1,0:T(8,128)(2,1)} %get-tuple-element.126.refs_2_, ...), custom_call_target="tpu_custom_call" | custom-call | flops 17179869184 | bytes 125829120 | tf_op jit(solution)/shard_map/product_forward/pallas_call | solution.py:221
  513.3 2.1 fusion.35
  517.0 51.6 %product_down.1 = (f32[256,2048]{1,0:T(8,128)}, bf16[512,1024]{1,0:T(8,128)(2,1)S(1)}) custom-call(bf16[2048,1024]{1,0:T(8,128)(2,1)} %copy-done.49, bf16[2048,1024]{1,0:T(8,128)(2,1)} %copy-done.21, bf16[512,1024]{1,0:T(8,128)(2,1)S(1)} %add_convert_fusion.7.refs_2_, bf16[512,1024]{1,0:T(8,128)(2,1)S(1)} %get-tuple-element.132.refs_3_), custom_call_target="tpu_custom_call" | custom-call | flops 8589934592 | bytes 125829120 | tf_op jit(solution)/shard_map/product_down/pallas_call | solution.py:221
  568.7 2.0 add.173
  572.3 2.2 fusion.36
  574.5 51.9 %gather_middle.1 = (bf16[2048,2048]{1,0:T(8,128)(2,1)}, bf16[512,1024]{1,0:T(8,128)(2,1)S(1)}) custom-call(bf16[256,2048]{1,0:T(8,128)(2,1)S(1)} %get-tuple-element.79.refs_0_, bf16[512,1024]{1,0:T(8,128)(2,1)S(1)} %get-tuple-element.131.refs_1_, bf16[512,1024]{1,0:T(8,128)(2,1)} %get-tuple-element.130.refs_2_), custom_call_target="tpu_custom_call" | custom-call | bytes 125829120 | tf_op jit(solution)/shard_map/gather_middle/pallas_call | solution.py:221
  629.7 1.7 add_convert_fusion.6.refs_6_
  631.4 26.1 %attend_back.1 = (bf16[2048,768]{1,0:T(8,128)(2,1)S(1)}, bf16[4,128,1024]{2,1,0:T(8,128)(2,1)S(1)}, bf16[4,128,1024]{2,1,0:T(8,128)(2,1)S(1)}, bf16[512,1024]{1,0:T(8,128)(2,1)S(1)}) custom-call(bf16[2048,768]{1,0:T(8,128)(2,1)} %copy-done.9, bf16[2048,2048]{1,0:T(8,128)(2,1)} %get-tuple-element.80.refs_1_, ...), custom_call_target="tpu_custom_call" | custom-call | flops 3489660928 | bytes 41943040 | tf_op jit(solution)/shard_map/attend_back/pallas_call | solution.py:822
  657.7 2.4 add_convert_fusion.3
  664.8 10.4 %convolution_convert_fusion.3 = bf16[2048,768]{1,0:T(8,128)(2,1)} fusion(bf16[2048,2048]{1,0:T(8,128)(2,1)} %get-tuple-element.52.refs_0_, bf16[2048,768]{1,0:T(8,128)(2,1)S(1)} %get-tuple-element.86.refs_0_), kind=kOutput, calls=%fused_computation.17 | convolution fusion | flops 6444023808 | bytes 14680064 | tf_op jit(solution)/shard_map/dot_general | solution.py:43
  675.2 3.6 all-to-all-start.1
  680.5 5.9 convolution_convert_fusion.9
  687.9 2.9 copy.51
  692.5 2.6 broadcast_select_fusion.2
  695.0 10.0 %all-to-all-done.1 = bf16[32,8,2048]{2,1,0:T(8,128)(2,1)} async-done(((bf16[32,8,2048]{2,1,0:T(8,128)(2,1)}), bf16[32,8,2048]{2,1,0:T(8,128)(2,1)}, u32[]{:S(2)}, u32[]{:S(2)}) %all-to-all-start.1) | async-done | bytes 1048608 | tf_op jit(solution)/shard_map/all_to_all | solution.py:911
  705.0 3.0 fusion.13
  708.1 50.4 %product_qkv.1 = (f32[256,2048]{1,0:T(8,128)}, bf16[512,1024]{1,0:T(8,128)(2,1)S(1)}) custom-call(bf16[2048,768]{1,0:T(8,128)(2,1)} %copy-done.12, bf16[2048,1024]{1,0:T(8,128)(2,1)} %get-tuple-element.53.refs_1_.refs_2_, bf16[512,1024]{1,0:T(8,128)(2,1)S(1)} %get-tuple-element.129.refs_2_, bf16[512,1024]{1,0:T(8,128)(2,1)S(1)} %get-tuple-element.128.refs_3_), custom_call_target="tpu_custom_call" | custom-call | flops 6442450944 | bytes 125829120 | tf_op jit(solution)/shard_map/product_qkv/pallas_call | solution.py:221
  762.3 2.0 fusion.4
  764.3 4.8 all-to-all-start.2
  769.2 17.8 %collective-permute-done.7 = bf16[512,1024]{1,0:T(8,128)(2,1)} collective-permute-done((bf16[512,1024]{1,0:T(8,128)(2,1)S(1)}, bf16[512,1024]{1,0:T(8,128)(2,1)}, u32[]{:S(2)}, u32[]{:S(2)}) %collective-permute-start.7) | collective-permute-done | bytes 1048608 | tf_op jit(solution)/shard_map/ppermute | solution.py:586
  787.0 1.7 add_convert_fusion
  788.8 3.1 collective-permute-start.10
  794.1 8.1 collective-permute-done.10
  802.3 4.9 collective-permute-done.8
  811.2 1.8 fusion.11
  (185 shorter events, 53.9 us)
Async XLA Ops:
  0.6 10.8 %copy-start = (bf16[256,2048]{1,0:T(8,128)(2,1)S(1)}, bf16[256,2048]{1,0:T(8,128)(2,1)}, u32[]{:S(2)}) copy-start(bf16[256,2048]{1,0:T(8,128)(2,1)} %param.12) | copy-start | bytes 3145732
  0.7 4.4 copy-start.30
  2.5 132.2 %copy-start.42 = (s32[256]{0:T(256)}, s32[256]{0:T(256)S(1)}, u32[]{:S(2)}) copy-start(s32[256]{0:T(256)S(1)} %multiply_add_fusion.2) | copy-start | bytes 3076
  7.0 2.7 copy-start.38
  7.0 3.4 copy-start.39
  11.4 282.2 %copy-start.44 = (s32[256]{0:T(256)}, s32[256]{0:T(256)S(1)}, u32[]{:S(2)}) copy-start(s32[256]{0:T(256)S(1)} %multiply_add_fusion.1) | copy-start | bytes 3076
  82.3 52.4 %copy-start.46 = (f32[256]{0:T(256)}, f32[256]{0:T(256)S(1)}, u32[]{:S(2)}) copy-start(f32[256]{0:T(256)S(1)} %add_rsqrt_fusion.1) | copy-start | bytes 3076
  83.2 51.5 %copy-start.32 = (bf16[256,2048]{1,0:T(8,128)(2,1)S(1)}, bf16[256,2048]{1,0:T(8,128)(2,1)}, u32[]{:S(2)}) copy-start(bf16[256,2048]{1,0:T(8,128)(2,1)} %param.13) | copy-start | bytes 3145732
  134.7 4.9 copy-start.48
  136.3 157.4 %all-to-all-start = ((bf16[32,8,2048]{2,1,0:T(8,128)(2,1)}), bf16[32,8,2048]{2,1,0:T(8,128)(2,1)}, u32[]{:S(2)}, u32[]{:S(2)}) async-start(bf16[32,8,2048]{2,1,0:T(8,128)(2,1)} %fusion.2), calls=%async_computation | async-start | bytes 2097152 | tf_op jit(solution)/shard_map/all_to_all | solution.py:911
  147.6 36.0 %copy-start.7 = (f32[2048,128]{1,0:T(8,128)}, f32[2048,128]{1,0:T(8,128)S(1)}, u32[]{:S(2)}) copy-start(f32[2048,128]{1,0:T(8,128)S(1)} %pad_maximum_fusion.2.refs_3_.refs_4_) | copy-start | bytes 3145732
  147.7 2.6 copy-start.4
  187.3 56.0 %copy-start.14 = (f32[256,2048]{1,0:T(8,128)S(1)}, f32[256,2048]{1,0:T(8,128)}, u32[]{:S(2)}) copy-start(f32[256,2048]{1,0:T(8,128)} %copy-done.13) | copy-start | bytes 6291460
  295.3 48.6 %copy-start.2 = (bf16[256,2048]{1,0:T(8,128)(2,1)}, bf16[256,2048]{1,0:T(8,128)(2,1)S(1)}, u32[]{:S(2)}) copy-start(bf16[256,2048]{1,0:T(8,128)(2,1)S(1)} %convolution_convert_fusion.6.refs_0_) | copy-start | bytes 3145732
  295.4 51.7 %copy-start.6 = (bf16[2048,1024]{1,0:T(8,128)(2,1)S(1)}, bf16[2048,1024]{1,0:T(8,128)(2,1)}, u32[]{:S(2)}) copy-start(bf16[2048,1024]{1,0:T(8,128)(2,1)} %get-tuple-element.67.refs_1_) | copy-start | bytes 12582916
  345.2 30.2 %collective-permute-start = (bf16[512,1024]{1,0:T(8,128)(2,1)S(1)}, bf16[512,1024]{1,0:T(8,128)(2,1)S(1)}, u32[]{:S(2)}, u32[]{:S(2)}) collective-permute-start(bf16[512,1024]{1,0:T(8,128)(2,1)S(1)} %constant_dynamic-slice_fusion.12), channel_id=1, source_target_pairs={{0,8},{8,16},{16,24},{24,0},{1,9},{9,17},{17,25},{25,1},{2,10},{10... | collective-permute-start | bytes 3145736 | tf_op jit(solution)/shard_map/ppermute | solution.py:586
  347.0 13.3 %copy-start.19 = (bf16[2048,1024]{1,0:T(8,128)(2,1)S(1)}, bf16[2048,1024]{1,0:T(8,128)(2,1)}, u32[]{:S(2)}) copy-start(bf16[2048,1024]{1,0:T(8,128)(2,1)} %get-tuple-element.68.refs_3_) | copy-start | bytes 12582916
  360.3 15.1 %copy-start.20 = (bf16[2048,1024]{1,0:T(8,128)(2,1)S(1)}, bf16[2048,1024]{1,0:T(8,128)(2,1)}, u32[]{:S(2)}) copy-start(bf16[2048,1024]{1,0:T(8,128)(2,1)} %get-tuple-element.69) | copy-start | bytes 12582916
  375.6 23.4 %collective-permute-start.1 = (bf16[512,1024]{1,0:T(8,128)(2,1)S(1)}, bf16[512,1024]{1,0:T(8,128)(2,1)S(1)}, u32[]{:S(2)}, u32[]{:S(2)}) collective-permute-start(bf16[512,1024]{1,0:T(8,128)(2,1)S(1)} %constant_dynamic-slice_fusion.11), channel_id=1, source_target_pairs={{0,8},{8,16},{16,24},{24,0},{1,9},{9,17},{17,25},{25,1},{2,10},{10... | collective-permute-start | bytes 3145736 | tf_op jit(solution)/shard_map/ppermute | solution.py:586
  388.9 10.3 %copy-start.26 = (bf16[2048,1024]{1,0:T(8,128)(2,1)}, bf16[2048,1024]{1,0:T(8,128)(2,1)S(1)}, u32[]{:S(2)}) copy-start(bf16[2048,1024]{1,0:T(8,128)(2,1)S(1)} %convolution_convert_fusion.2) | copy-start | bytes 12582916
  399.1 22.1 %copy-start.21 = (bf16[2048,1024]{1,0:T(8,128)(2,1)}, bf16[2048,1024]{1,0:T(8,128)(2,1)S(1)}, u32[]{:S(2)}) copy-start(bf16[2048,1024]{1,0:T(8,128)(2,1)S(1)} %constant_dynamic-update-slice_fusion.refs_1_) | copy-start | bytes 12582916
  399.2 34.8 %collective-permute-start.2 = (bf16[512,1024]{1,0:T(8,128)(2,1)S(1)}, bf16[512,1024]{1,0:T(8,128)(2,1)}, u32[]{:S(2)}, u32[]{:S(2)}) collective-permute-start(bf16[512,1024]{1,0:T(8,128)(2,1)S(1)} %constant_dynamic-slice_fusion.10), channel_id=1, source_target_pairs={{0,8},{8,16},{16,24},{24,0},{1,9},{9,17},{17,25},{25,1},{2,10},{10... | collective-permute-start | bytes 3145736 | tf_op jit(solution)/shard_map/ppermute | solution.py:586
  421.2 12.9 %copy-start.27 = (bf16[2048,1024]{1,0:T(8,128)(2,1)S(1)}, bf16[2048,1024]{1,0:T(8,128)(2,1)}, u32[]{:S(2)}) copy-start(bf16[2048,1024]{1,0:T(8,128)(2,1)} %copy-done.26) | copy-start | bytes 12582916
  421.2 17.0 %copy-start.50 = (bf16[2048,1024]{1,0:T(8,128)(2,1)S(1)}, bf16[2048,1024]{1,0:T(8,128)(2,1)}, u32[]{:S(2)}) copy-start(bf16[2048,1024]{1,0:T(8,128)(2,1)} %get-tuple-element.73.refs_0_) | copy-start | bytes 12582916
  434.0 17.1 %copy-start.25 = (bf16[2048,1024]{1,0:T(8,128)(2,1)}, bf16[2048,1024]{1,0:T(8,128)(2,1)S(1)}, u32[]{:S(2)}) copy-start(bf16[2048,1024]{1,0:T(8,128)(2,1)S(1)} %convolution_convert_fusion) | copy-start | bytes 12582916
  436.5 22.6 %collective-permute-start.3 = (bf16[512,1024]{1,0:T(8,128)(2,1)S(1)}, bf16[512,1024]{1,0:T(8,128)(2,1)S(1)}, u32[]{:S(2)}, u32[]{:S(2)}) collective-permute-start(bf16[512,1024]{1,0:T(8,128)(2,1)S(1)} %add_convert_fusion.9), channel_id=1, source_target_pairs={{0,8},{8,16},{16,24},{24,0},{1,9},{9,17},{17,25},{25,1},{2,10},{10... | collective-permute-start | bytes 3145736 | tf_op jit(solution)/shard_map/ppermute | solution.py:586
  449.7 2.3 copy-start.28
  459.5 53.8 %copy-start.17 = (f32[256,2048]{1,0:T(8,128)S(1)}, f32[256,2048]{1,0:T(8,128)}, u32[]{:S(2)}) copy-start(f32[256,2048]{1,0:T(8,128)} %copy-done.16) | copy-start | bytes 6291460
  568.7 3.6 copy-start.24
  657.6 2.5 copy-start.10
  657.6 7.2 copy-start.12
  661.3 31.1 %collective-permute-start.4 = (bf16[128,1024]{1,0:T(8,128)(2,1)}, bf16[128,1024]{1,0:T(8,128)(2,1)}, u32[]{:S(2)}, u32[]{:S(2)}) collective-permute-start(bf16[128,1024]{1,0:T(8,128)(2,1)} %get-tuple-element.153), channel_id=1, source_target_pairs={{0,2},{2,0},{1,3},{3,1},{4,6},{6,4},{5,7},{7,5},{8,10},{10,8},{9,1... | collective-permute-start | bytes 786440 | tf_op jit(solution)/shard_map/ppermute | solution.py:657
  661.9 30.5 %collective-permute-start.5 = (bf16[128,1024]{1,0:T(8,128)(2,1)}, bf16[128,1024]{1,0:T(8,128)(2,1)}, u32[]{:S(2)}, u32[]{:S(2)}) collective-permute-start(bf16[128,1024]{1,0:T(8,128)(2,1)} %get-tuple-element.155), channel_id=1, source_target_pairs={{0,4},{4,0},{1,5},{5,1},{2,6},{6,2},{3,7},{7,3},{8,12},{12,8},{9,1... | collective-permute-start | bytes 786440 | tf_op jit(solution)/shard_map/ppermute | solution.py:658
  663.3 29.1 %collective-permute-start.6 = (bf16[128,1024]{1,0:T(8,128)(2,1)S(1)}, bf16[128,1024]{1,0:T(8,128)(2,1)}, u32[]{:S(2)}, u32[]{:S(2)}) collective-permute-start(bf16[128,1024]{1,0:T(8,128)(2,1)S(1)} %get-tuple-element.154), channel_id=1, source_target_pairs={{0,6},{2,4},{4,2},{6,0},{1,7},{3,5},{5,3},{7,1},{8,14},{10,12},{12... | collective-permute-start | bytes 786440 | tf_op jit(solution)/shard_map/ppermute | solution.py:659
  675.2 29.8 %all-to-all-start.1 = ((bf16[32,8,2048]{2,1,0:T(8,128)(2,1)}), bf16[32,8,2048]{2,1,0:T(8,128)(2,1)}, u32[]{:S(2)}, u32[]{:S(2)}) async-start(bf16[32,8,2048]{2,1,0:T(8,128)(2,1)} %fusion.3), calls=%async_computation.1 | async-start | bytes 2097152 | tf_op jit(solution)/shard_map/all_to_all | solution.py:911
  692.4 12.6 %copy-start.43 = (s32[256]{0:T(256)S(1)}, s32[256]{0:T(256)}, u32[]{:S(2)}) copy-start(s32[256]{0:T(256)} %copy-done.42) | copy-start | bytes 3076
  708.1 50.4 %copy-start.18 = (bf16[2048,768]{1,0:T(8,128)(2,1)S(1)}, bf16[2048,768]{1,0:T(8,128)(2,1)}, u32[]{:S(2)}) copy-start(bf16[2048,768]{1,0:T(8,128)(2,1)} %convolution_convert_fusion.3) | copy-start | bytes 9437188
  758.5 2.2 copy-start.22
  758.5 2.2 copy-start.41
  758.9 28.1 %collective-permute-start.7 = (bf16[512,1024]{1,0:T(8,128)(2,1)S(1)}, bf16[512,1024]{1,0:T(8,128)(2,1)}, u32[]{:S(2)}, u32[]{:S(2)}) collective-permute-start(bf16[512,1024]{1,0:T(8,128)(2,1)S(1)} %add_convert_fusion.1), channel_id=1, source_target_pairs={{0,8},{8,16},{16,24},{24,0},{1,9},{9,17},{17,25},{25,1},{2,10},{10... | collective-permute-start | bytes 3145736 | tf_op jit(solution)/shard_map/ppermute | solution.py:586
  764.3 46.9 %all-to-all-start.2 = ((bf16[32,8,2048]{2,1,0:T(8,128)(2,1)}), bf16[32,8,2048]{2,1,0:T(8,128)(2,1)S(1)}, u32[]{:S(2)}, u32[]{:S(2)}) async-start(bf16[32,8,2048]{2,1,0:T(8,128)(2,1)} %fusion.4), calls=%async_computation.2 | async-start | bytes 2097152 | tf_op jit(solution)/shard_map/all_to_all | solution.py:911
  769.1 23.5 %copy-start.33 = (bf16[128,1024]{1,0:T(8,128)(2,1)S(1)}, bf16[128,1024]{1,0:T(8,128)(2,1)}, u32[]{:S(2)}) copy-start(bf16[128,1024]{1,0:T(8,128)(2,1)} %get-tuple-element.139) | copy-start | bytes 786436
  769.2 23.5 %copy-start.34 = (bf16[128,1024]{1,0:T(8,128)(2,1)S(1)}, bf16[128,1024]{1,0:T(8,128)(2,1)}, u32[]{:S(2)}) copy-start(bf16[128,1024]{1,0:T(8,128)(2,1)} %get-tuple-element.140) | copy-start | bytes 786436
  769.2 23.4 %copy-start.35 = (bf16[128,1024]{1,0:T(8,128)(2,1)S(1)}, bf16[128,1024]{1,0:T(8,128)(2,1)}, u32[]{:S(2)}) copy-start(bf16[128,1024]{1,0:T(8,128)(2,1)} %get-tuple-element.141) | copy-start | bytes 786436
  788.8 13.4 %collective-permute-start.10 = (bf16[128,1024]{1,0:T(8,128)(2,1)S(1)}, bf16[128,1024]{1,0:T(8,128)(2,1)S(1)}, u32[]{:S(2)}, u32[]{:S(2)}) collective-permute-start(bf16[128,1024]{1,0:T(8,128)(2,1)S(1)} %get-tuple-element.151), channel_id=1, source_target_pairs={{0,6},{2,4},{4,2},{6,0},{1,7},{3,5},{5,3},{7,1},{8,14},{10,12},{12... | collective-permute-start | bytes 786440 | tf_op jit(solution)/shard_map/ppermute | solution.py:659
  792.0 15.2 %collective-permute-start.8 = (bf16[128,1024]{1,0:T(8,128)(2,1)S(1)}, bf16[128,1024]{1,0:T(8,128)(2,1)S(1)}, u32[]{:S(2)}, u32[]{:S(2)}) collective-permute-start(bf16[128,1024]{1,0:T(8,128)(2,1)S(1)} %get-tuple-element.150), channel_id=1, source_target_pairs={{0,2},{2,0},{1,3},{3,1},{4,6},{6,4},{5,7},{7,5},{8,10},{10,8},{9,1... | collective-permute-start | bytes 786440 | tf_op jit(solution)/shard_map/ppermute | solution.py:657
  792.4 14.7 %collective-permute-start.9 = (bf16[128,1024]{1,0:T(8,128)(2,1)S(1)}, bf16[128,1024]{1,0:T(8,128)(2,1)S(1)}, u32[]{:S(2)}, u32[]{:S(2)}) collective-permute-start(bf16[128,1024]{1,0:T(8,128)(2,1)S(1)} %get-tuple-element.152), channel_id=1, source_target_pairs={{0,4},{4,0},{1,5},{5,1},{2,6},{6,2},{3,7},{7,3},{8,12},{12,8},{9,1... | collective-permute-start | bytes 786440 | tf_op jit(solution)/shard_map/ppermute | solution.py:658
  809.5 3.5 copy-start.1
  (17 other events, 28.5 us)

commit v4 on v3

--- a/solution.py
+++ b/solution.py
@@ -13,6 +13,7 @@
 SEGS = 4
 EPSILON = 1e-05
 NEG_LARGE = -1e30
+VMEM_BYTES = 60 << 20
 F32 = jnp.float32
 BF16 = jnp.bfloat16
 MESH = pl.DeviceIdType.MESH
@@ -100,16 +101,16 @@
             self.operands.append(whole)
             self.shapes.append(jax.ShapeDtypeStruct(whole.shape, whole.dtype))
             self.steps += count
-        for running, adds in self.sums:
-            self.operands += [running, *adds]
-            self.shapes.append(jax.ShapeDtypeStruct(running.shape, running.dtype))
-            self.steps += 1 + len(adds)
-            for _ in adds:
-                self.scratch += [
-                    pltpu.VMEM(running.shape, running.dtype),
-                    pltpu.VMEM(running.shape, running.dtype),
-                    pltpu.SemaphoreType.DMA(()),
-                ]
+        for running, whole, first, count in self.sums:
+            self.operands += [whole] if running is None else [running, whole]
+            block = (whole.shape[0] // lax.axis_size("z"), whole.shape[1])
+            self.shapes.append(jax.ShapeDtypeStruct(block, whole.dtype))
+            self.steps += count
+            self.scratch += [
+                pltpu.VMEM((count, *block), whole.dtype),
+                pltpu.VMEM((count, *block), whole.dtype),
+                pltpu.SemaphoreType.DMA((count + 1,)),
+            ]
         if self.steps:
             self.scratch += [
                 pltpu.SemaphoreType.DMA((self.steps,)),
@@ -119,10 +120,16 @@
     def board(self, inputs, outputs, scratch):
         inputs, outputs, scratch = list(inputs), list(outputs), list(scratch)
         self.loads, self.copies, self.prepares, self.begun = [], [], [], 0
+        self.ends = []
         if not self.steps:
             return
+        total = lax.axis_size("z")
         send, recv = scratch[-2], scratch[-1]
-        ahead = {"z": owner_at(lax.axis_size("z") - 1)}
+        ahead = {"z": owner_at(total - 1)}
+
+        def rows_of(whole, step):
+            rows = whole.shape[0] // total
+            return whole.at[pl.ds(pl.multiple_of(owner_at(step % total) * rows, rows), rows)]
 
         def plan(source, target, prepare=None):
             slot = len(self.copies)
@@ -153,24 +160,24 @@
         for _, first, count in self.gathers:
             inputs.pop(0)
             whole = outputs.pop(0)
-            rows = whole.shape[0] // lax.axis_size("z")
             for step in range(first, first + count):
-                at = pl.ds(pl.multiple_of(owner_at(step) * rows, rows), rows)
-                plan(whole.at[at], whole.at[at])
-        for _, adds in self.sums:
-            running = inputs.pop(0)
-            final = outputs.pop(0)
-            held = []
-            for _ in adds:
-                landed, own, loaded = scratch[:3]
-                scratch = scratch[3:]
-                load = pltpu.make_async_copy(inputs.pop(0), own, loaded)
-                held.append((load, landed, own))
+                plan(rows_of(whole, step), rows_of(whole, step))
+        for running, _, first, count in self.sums:
+            source = None if running is None else inputs.pop(0)
+            whole, final = inputs.pop(0), outputs.pop(0)
+            landed, own, loaded = scratch[:3]
+            scratch = scratch[3:]
+            if source is None:
+                source = rows_of(whole, 1)
+            prepare = None
+            for k in range(count):
+                load = pltpu.make_async_copy(rows_of(whole, first + 2 + k), own.at[k], loaded.at[k])
                 self.loads.append(load)
-            targets = [landed for _, landed, _ in held] + [final]
-            plan(running, targets[0])
-            for (load, landed, own), target in zip(held, targets[1:]):
-                plan(own, target, adding(load, landed, own))
+                plan(source, landed.at[k], prepare)
+                prepare, source = adding(load, landed.at[k], own.at[k]), own.at[k]
+            last = len(self.copies) - 1
+            keep = pltpu.make_async_copy(own.at[count - 1], final, loaded.at[count])
+            self.ends.append((last, prepare, keep))
 
     def start(self, number):
         if self.prepares[number]:
@@ -194,8 +201,13 @@
             self.advance()
         if self.copies:
             self.copies[-1].wait_recv()
+        for _, prepare, keep in self.ends:
+            prepare()
+            keep.start()
         for copy in self.copies:
             copy.wait_send()
+        for _, _, keep in self.ends:
+            keep.wait()
 
 
 def block_at(core, y, x):
@@ -217,7 +229,7 @@
         ride.board(inputs[count_in:], outputs[count_out:], held[count_scratch:])
         body(inputs[:count_in], outputs[:count_out], held[:count_scratch], ride)
 
-    anywhere = pl.BlockSpec(memory_space=pl.ANY)
+    anywhere = pl.BlockSpec(memory_space=pltpu.HBM)
     got = pl.pallas_call(
         kernel,
         in_specs=list(specs) + [anywhere] * len(ride.operands),
@@ -226,7 +238,7 @@
         scratch_shapes=list(scratch) + ride.scratch,
         input_output_aliases={count_in + k: count_out + v for k, v in ride.aliases.items()},
         compiler_params=pltpu.CompilerParams(
-            collective_id=IDS.index(name), has_side_effects=True, vmem_limit_bytes=50 << 20
+            collective_id=IDS.index(name), has_side_effects=True, vmem_limit_bytes=VMEM_BYTES
         ),
         cost_estimate=pl.CostEstimate(
             flops=flops, bytes_accessed=120 << 20, transcendentals=0
@@ -342,7 +354,7 @@
 def dispatch(weights, narrow, places, packed, steps, name):
     rows = weights[0].shape[0]
     total = lax.axis_size("z")
-    anywhere = pl.BlockSpec(memory_space=pl.ANY)
+    anywhere = pl.BlockSpec(memory_space=pltpu.HBM)
     count = len(weights)
     widths = [sum(weight.shape[1] // 4 for weight in weights[:narrow])]
     widths += [weight.shape[1] // 4 for weight in weights[narrow:]]
@@ -364,15 +376,14 @@
             pltpu.SemaphoreType.DMA((steps,)),
         ],
         compiler_params=pltpu.CompilerParams(
-            collective_id=IDS.index(name), has_side_effects=True
+            collective_id=IDS.index(name), has_side_effects=True, vmem_limit_bytes=VMEM_BYTES
         ),
         cost_estimate=pl.CostEstimate(flops=0, bytes_accessed=120 << 20, transcendentals=0),
         name=name,
     )(*weights, places, packed)
 
 
-def gather_body(inputs, outputs, scratch, ride):
-    (own,), (out,), (send, recv, local) = inputs, outputs, scratch
+def gather_stages(own, out, send, recv, local, ride):
     rows = own.shape[0]
     half = rows // 2
 
@@ -398,36 +409,202 @@
     y_first = over("y", first, part(0, 0, 0, 0), 3)
     ride.begin()
     crossed = [over("c", own, whole, 4)]
+    yield
     x_first.wait_recv()
     far_first = over("y", part(0, 0, 1, 0), part(0, 0, 1, 0), 5)
     crossed.append(across(0, 1, 0, 6))
     y_second.wait_recv()
     far_second = over("x", part(0, 1, 0, 1), part(0, 1, 0, 1), 7)
     crossed.append(across(1, 0, 1, 8))
+    yield
     x_second.wait_recv()
     crossed.append(across(0, 1, 1, 9))
     y_first.wait_recv()
     crossed.append(across(1, 0, 0, 10))
     ride.advance()
+    yield
     far_first.wait_recv()
     crossed.append(across(1, 1, 0, 11))
     far_second.wait_recv()
     crossed.append(across(1, 1, 1, 12))
     for copy in crossed:
         copy.wait_recv()
+    keep.wait()
+    ride.advance()
+    yield
     ride.finish()
     for copy in crossed + [x_first, y_second, x_second, y_first, far_first, far_second]:
         copy.wait_send()
-    keep.wait()
+    yield
+
+
+def gather_body(inputs, outputs, scratch, ride):
+    for _ in gather_stages(inputs[0], outputs[0], *scratch, ride):
+        pass
+
+
+def outer_tiles(sources, targets, tiles, stage, loads, stores, between=lambda: None):
+    count = tiles[0].shape[0]
+    tile = tiles[0].shape[2]
+    total = sources[0][0].shape[1] // tile
+
+    def fetch(index, slot):
+        at = pl.ds(pl.multiple_of(index * tile, tile), tile)
+        return [
+            pltpu.make_async_copy(source.at[:, at], held.at[slot], loads.at[number, slot])
+            for number, ((source, _), held) in enumerate(zip(sources, tiles))
+        ]
+
+    def keep(index, slot):
+        at = pl.ds(pl.multiple_of(index * tile, tile), tile)
+        return [
+            pltpu.make_async_copy(
+                stage.at[slot, :, pl.ds(start, size)], target.at[at], stores.at[number, slot]
+            )
+            for number, (target, start, size) in enumerate(targets)
+        ]
+
+    for copy in fetch(0, 0):
+        copy.start()
+
+    def multiply(index):
+        slot = lax.rem(index, count)
+
+        @pl.when(index + 1 < total)
+        def _():
+            for copy in fetch(index + 1, lax.rem(index + 1, count)):
+                copy.start()
+
+        @pl.when(index >= count)
+        def _():
+            for copy in keep(index - count, slot):
+                copy.wait()
+
+        for copy in fetch(index, slot):
+            copy.wait()
+        for (_, parts), held in zip(sources, tiles):
+            left = held[slot]
+            for start, size, right in parts:
+                stage[slot, :, pl.ds(start, size)] = outer_sum(left, right()).astype(BF16)
+        for copy in keep(index, slot):
+            copy.start()
+
+    pl.loop(0, total // 2)(multiply)
+    between()
+    pl.loop(total // 2, total)(multiply)
+    for index in range(max(total - count, 0), total):
+        for copy in keep(index, index % count):
+            copy.wait()
+
+
+def outer_scratch(rows, sources, columns, targets, tile=256):
+    return [pltpu.VMEM((2, rows, tile), BF16)] * sources + [
+        pltpu.VMEM((2, tile, columns), BF16),
+        pltpu.SemaphoreType.DMA((sources, 2)),
+        pltpu.SemaphoreType.DMA((targets, 2)),
+    ]
+
+
+def gather_hidden_body(inputs, outputs, scratch, ride):
+    own, seen_ref, gate_ref, up_ref = inputs
+    out, hidden_ref, by_gate_ref, by_up_ref, weight_ref = outputs
+    seen, gate_w, up_w, hidden, by_gate, by_up, loads, stores, *outer = scratch[3:]
+    blocks, block = seen.shape[0], seen.shape[1]
+    width = gate_w.shape[1]
+    tile = 512
+    fetch = [
+        pltpu.make_async_copy(gate_ref, gate_w, loads.at[0]),
+        pltpu.make_async_copy(up_ref, up_w, loads.at[1]),
+    ]
+    for index in range(blocks):
+        at = pl.ds(index * block, block)
+        fetch.append(pltpu.make_async_copy(seen_ref.at[at], seen.at[index], loads.at[2 + index]))
+    for index in (0, 2, 1, *range(3, len(fetch))):
+        fetch[index].start()
+    stages = gather_stages(own, out, *scratch[:3], ride)
+    next(stages)
+    fetch[0].wait()
+    fetch[1].wait()
+    kept = []
+    for index in range(blocks):
+        fetch[2 + index].wait()
+
+        @pl.loop(0, width // tile)
+        def _(step):
+            at = pl.ds(pl.multiple_of(step * tile, tile), tile)
+            here = seen[index]
+            gate = project(here, gate_w[:, at])
+            up = project(here, up_w[:, at])
+            turned = 1.0 / (1.0 + jnp.exp(-gate))
+            silu = gate * turned
+            hidden[pl.ds(index * block, block), at] = (silu * up).astype(BF16)
+            by_up[pl.ds(index * block, block), at] = silu.astype(BF16)
+            by_gate[pl.ds(index * block, block), at] = (up * (turned * (1.0 + gate * (1.0 - turned)))).astype(BF16)
+
+        rows_at = pl.ds(index * block, block)
+        pairs = ((hidden, hidden_ref), (by_gate, by_gate_ref), (by_up, by_up_ref))
+        for number, (held, target) in enumerate(pairs):
+            copy = pltpu.make_async_copy(
+                held.at[rows_at], target.at[rows_at], stores.at[number, index]
+            )
+            copy.start()
+            kept.append(copy)
+        if index in (3, 6):
+            next(stages)
+    next(stages)
+    outer_tiles(
+        [(out, [(0, width, lambda: hidden[...])])],
+        [(weight_ref, 0, width)],
+        outer[:1],
+        *outer[1:],
+    )
+    next(stages)
+    for copy in kept:
+        copy.wait()
+
+
+def plane_gather_hidden(rows, seen, gate_w, up_w, name, ride=None):
+    total, depth = seen.shape
+    width = gate_w.shape[1]
+    block = rows.shape[0]
+    blocks = total // block
+    anywhere = pl.BlockSpec(memory_space=pltpu.HBM)
+    got = communicate(
+        gather_hidden_body,
+        [rows, seen, gate_w, up_w],
+        [anywhere] * 4,
+        [jax.ShapeDtypeStruct((8 * rows.shape[0], rows.shape[1]), rows.dtype)]
+        + [jax.ShapeDtypeStruct((total, width), BF16)] * 3
+        + [jax.ShapeDtypeStruct((rows.shape[1], width), BF16)],
+        [anywhere] * 5,
+        [
+            pltpu.SemaphoreType.DMA((13,)),
+            pltpu.SemaphoreType.DMA((13,)),
+            pltpu.SemaphoreType.DMA(()),
+            pltpu.VMEM((blocks, block, depth), BF16),
+            pltpu.VMEM((depth, width), BF16),
+            pltpu.VMEM((depth, width), BF16),
+            pltpu.VMEM((total, width), BF16),
+            pltpu.VMEM((total, width), BF16),
+            pltpu.VMEM((total, width), BF16),
+            pltpu.SemaphoreType.DMA((2 + blocks,)),
+            pltpu.SemaphoreType.DMA((3, blocks)),
+        ]
+        + outer_scratch(total, 1, width, 1),
+        name,
+        ride,
+        flops=6 * total * depth * width,
+    )
+    return got[:5], got[5:]
 
 
 def plane_gather(rows, name, ride=None):
     got = communicate(
         gather_body,
         [rows],
-        [pl.BlockSpec(memory_space=pl.ANY)],
+        [pl.BlockSpec(memory_space=pltpu.HBM)],
         [jax.ShapeDtypeStruct((8 * rows.shape[0], rows.shape[1]), rows.dtype)],
-        [pl.BlockSpec(memory_space=pl.ANY)],
+        [pl.BlockSpec(memory_space=pltpu.HBM)],
         [
             pltpu.SemaphoreType.DMA((13,)),
             pltpu.SemaphoreType.DMA((13,)),
@@ -439,12 +616,12 @@
     return got[0], got[1:]
 
 
-def product_body(starts, inputs, outputs, scratch, ride):
-    (out_ref,) = outputs
-    left, weight, away, got, near, by_y, by_x, end_y, end_x, send, recv, local = scratch
+def product_body(make, starts, inputs, outputs, scratch, ride):
+    out_ref = outputs[0]
+    left, weight, away, got, near, by_y, by_x, end_y, end_x, send, recv, local = scratch[:12]
     block, width = out_ref.shape
     half = block // 2
-    tile = 512
+    tile = 1024
     pairs = [(inputs[2 * i], inputs[2 * i + 1], start) for i, start in enumerate(starts)]
 
     def over(axis, source, target, slot):
@@ -453,7 +630,7 @@
     waits = {"weight": []}
     column = 0
     for index, (rows_ref, weight_ref, start) in enumerate(pairs):
-        inner = rows_ref.shape[1]
+        inner = weight_ref.shape[1] if make else rows_ref.shape[1]
         copy = pltpu.make_async_copy(
             weight_ref.at[:, pl.ds(start, inner)],
             weight.at[:, pl.ds(column, inner)],
@@ -463,33 +640,38 @@
         waits["weight"].append(copy)
         column += inner
     order = ((1, 1, 1), (1, 1, 0), (0, 1, 1), (1, 0, 1), (0, 1, 0), (1, 0, 0), (0, 0, 1), (0, 0, 0))
-    for slot, key in enumerate(order):
-        start = pl.multiple_of(block_at(*key) * block, block)
-        waits[key] = []
-        column = 0
-        for index, (rows_ref, _, _) in enumerate(pairs):
-            inner = rows_ref.shape[1]
-            copy = pltpu.make_async_copy(
-                rows_ref.at[pl.ds(start, block)],
-                left.at[slot, :, pl.ds(column, inner)],
-                local.at[index, slot],
-            )
-            copy.start()
-            waits[key].append(copy)
-            column += inner
+    places = [pl.ds(pl.multiple_of(block_at(*key) * block, block), block) for key in order]
+    if make:
+        fill, follow = make(inputs, outputs, scratch[12:], left, places)
+    else:
+        for slot, key in enumerate(order):
+            waits[key] = []
+            column = 0
+            for index, (rows_ref, _, _) in enumerate(pairs):
+                inner = rows_ref.shape[1]
+                copy = pltpu.make_async_copy(
+                    rows_ref.at[places[slot]],
+                    left.at[places[slot], pl.ds(column, inner)],
+                    local.at[index, slot],
+                )
+                copy.start()
+                waits[key].append(copy)
+                column += inner
     greet((("x",), ("y",), ("c",)), ride.steps > 0)
     ride.begin()
     for copy in waits["weight"]:
         copy.wait()
 
     def multiply(key, store):
-        for copy in waits[key]:
-            copy.wait()
-        here = left[order.index(key)]
-
-        @pl.loop(0, width // tile)
-        def _(step):
-            at = pl.ds(pl.multiple_of(step * tile, tile), tile)
+        slot = order.index(key)
+        if make:
+            fill(slot)
+        else:
+            for copy in waits[key]:
+                copy.wait()
+        here = left[places[slot], :]
+        for start in range(0, width, tile):
+            at = pl.ds(start, tile)
             store(at, project_t(here, weight[at, :]))
 
     crossing = {}
@@ -521,17 +703,22 @@
     compute_far(0, 1)
     compute_near(1, 0)
     y_near = over("y", near.at[2, lower], by_y.at[0], 6)
+    if make:
+        ride.advance()
     compute_far(0, 0)
     compute_near(0, 1)
     x_near = over("x", near.at[1, upper], by_x.at[0], 7)
-    compute_near(0, 0)
     y_far.wait_recv()
     near[1, lower, :] = (near[1, lower, :].astype(F32) + by_y[1].astype(F32)).astype(BF16)
     x_last = over("x", near.at[1, lower], end_x, 8)
     x_far.wait_recv()
     near[2, upper, :] = (near[2, upper, :].astype(F32) + by_x[1].astype(F32)).astype(BF16)
     y_last = over("y", near.at[2, upper], end_y, 9)
-    ride.advance()
+    if not make:
+        ride.advance()
+    compute_near(0, 0)
+    if make:
+        follow(ride.advance)
     y_near.wait_recv()
     out_ref[lower, :] = near[0, lower, :].astype(F32) + by_y[0].astype(F32)
     x_near.wait_recv()
@@ -545,35 +732,124 @@
         copy.wait_send()
 
 
+def product_scratch(total, inner, width, pairs):
+    block = total // 8
+    half = block // 2
+    return [
+        pltpu.VMEM((total, inner), BF16),
+        pltpu.VMEM((width, inner), BF16),
+        pltpu.VMEM((4, block, width), BF16),
+        pltpu.VMEM((4, block, width), BF16),
+        pltpu.VMEM((4, block, width), BF16),
+        pltpu.VMEM((2, half, width), BF16),
+        pltpu.VMEM((2, half, width), BF16),
+        pltpu.VMEM((half, width), BF16),
+        pltpu.VMEM((half, width), BF16),
+        pltpu.SemaphoreType.DMA((10,)),
+        pltpu.SemaphoreType.DMA((10,)),
+        pltpu.SemaphoreType.DMA((pairs, 9)),
+    ]
+
+
+def hidden_back(inputs, outputs, scratch, left, places):
+    by_gate_ref, gate_w, by_up_ref, up_w, grad_ref, down_ref, seen_ref = inputs
+    weight_gate, weight_up = outputs[1:]
+    down, rows, factors, down_load, row_loads, *outer = scratch
+    width = down.shape[1]
+    tile = 1024
+    fetch_down = pltpu.make_async_copy(down_ref, down, down_load)
+    fetch_down.start()
+
+    def fetch(slot):
+        at, held = places[slot], slot % 2
+        return [
+            pltpu.make_async_copy(grad_ref.at[at], rows.at[held], row_loads.at[0, held]),
+            pltpu.make_async_copy(by_gate_ref.at[at], factors.at[held, 0], row_loads.at[1, held]),
+            pltpu.make_async_copy(by_up_ref.at[at], factors.at[held, 1], row_loads.at[2, held]),
+        ]
+
+    for copy in fetch(0):
+        copy.start()
+
+    def fill(slot):
+        if slot == 0:
+            fetch_down.wait()
+        for copy in fetch(slot):
+            copy.wait()
+        if slot + 1 < len(places):
+            for copy in fetch(slot + 1):
+                copy.start()
+        held = slot % 2
+
+        for start in range(0, width, tile):
+            at, beside = pl.ds(start, tile), pl.ds(width + start, tile)
+            grad = project(rows[held], down[:, at])
+            left[places[slot], at] = (grad * factors[held, 0, :, at].astype(F32)).astype(BF16)
+            left[places[slot], beside] = (grad * factors[held, 1, :, at].astype(F32)).astype(BF16)
+
+    def follow(between):
+        outer_tiles(
+            [
+                (
+                    seen_ref,
+                    [
+                        (0, width, lambda: left[:, pl.ds(0, width)]),
+                        (width, width, lambda: left[:, pl.ds(width, width)]),
+                    ],
+                )
+            ],
+            [(weight_gate, 0, width), (weight_up, width, width)],
+            outer[:1],
+            *outer[1:],
+            between,
+        )
+
+    return fill, follow
+
+
+def plane_product_back(grads, down, by_gate, by_up, gate_w, up_w, seen, name, ride):
+    total, depth = grads.shape
+    width = gate_w.shape[1]
+    block = total // 8
+    operands = [by_gate, gate_w, by_up, up_w, grads, down, seen]
+    anywhere = pl.BlockSpec(memory_space=pltpu.HBM)
+    got = communicate(
+        functools.partial(product_body, hidden_back, [0, 0]),
+        operands,
+        [anywhere] * len(operands),
+        [jax.ShapeDtypeStruct((block, depth), F32)]
+        + [jax.ShapeDtypeStruct((depth, width), BF16)] * 2,
+        [pl.BlockSpec(memory_space=pltpu.VMEM), anywhere, anywhere],
+        product_scratch(total, 2 * width, depth, 2)
+        + [
+            pltpu.VMEM((depth, width), BF16),
+            pltpu.VMEM((2, block, depth), BF16),
+            pltpu.VMEM((2, 2, block, width), BF16),
+            pltpu.SemaphoreType.DMA(()),
+            pltpu.SemaphoreType.DMA((3, 2)),
+        ]
+        + outer_scratch(total, 1, 2 * width, 2),
+        name,
+        ride,
+        flops=10 * total * depth * width,
+    )
+    return got[:3], got[3:]
+
+
 def plane_product(pairs, name, ride=None):
     total = pairs[0][0].shape[0]
     inner = sum(rows.shape[1] for rows, _, _ in pairs)
     width = pairs[0][1].shape[0]
-    block = total // 8
-    half = block // 2
     operands = []
     for rows, weight, _ in pairs:
         operands += [rows, weight]
     got = communicate(
-        functools.partial(product_body, [start for _, _, start in pairs]),
+        functools.partial(product_body, None, [start for _, _, start in pairs]),
         operands,
-        [pl.BlockSpec(memory_space=pl.ANY)] * len(operands),
-        [jax.ShapeDtypeStruct((block, width), F32)],
+        [pl.BlockSpec(memory_space=pltpu.HBM)] * len(operands),
+        [jax.ShapeDtypeStruct((total // 8, width), F32)],
         [pl.BlockSpec(memory_space=pltpu.VMEM)],
-        [
-            pltpu.VMEM((8, block, inner), BF16),
-            pltpu.VMEM((width, inner), BF16),
-            pltpu.VMEM((4, block, width), BF16),
-            pltpu.VMEM((4, block, width), BF16),
-            pltpu.VMEM((4, block, width), BF16),
-            pltpu.VMEM((2, half, width), BF16),
-            pltpu.VMEM((2, half, width), BF16),
-            pltpu.VMEM((half, width), BF16),
-            pltpu.VMEM((half, width), BF16),
-            pltpu.SemaphoreType.DMA((10,)),
-            pltpu.SemaphoreType.DMA((10,)),
-            pltpu.SemaphoreType.DMA((len(pairs), 9)),
-        ],
+        product_scratch(total, inner, width, len(pairs)),
         name,
         ride,
         flops=2 * total * inner * width,
@@ -621,25 +897,24 @@
 
 class Summed:
     def __init__(self, whole):
-        self.whole, self.step = whole, 0
-        self.running = ring_rows(whole, owner_at(1))
-
-    def block(self, step):
-        return ring_rows(self.whole, owner_at((step + 1) % lax.axis_size("z")))
+        self.whole, self.step, self.running = whole, 0, None
 
     def ride(self, count):
         count = min(count, lax.axis_size("z") - 1 - self.step)
-        adds = tuple(self.block(self.step + 1 + k) for k in range(count - 1))
+        item = (self.running, self.whole, self.step, count)
         self.step += count
-        return (self.running, adds)
-
-    def land(self, received):
-        self.running = (received.astype(F32) + self.block(self.step).astype(F32)).astype(BF16)
+        return item
+
+    def land(self, running):
+        self.running = running
 
     def walk(self, count):
-        for _ in range(min(count, lax.axis_size("z") - 1 - self.step)):
+        total = lax.axis_size("z")
+        for _ in range(min(count, total - 1 - self.step)):
+            running = ring_rows(self.whole, owner_at(1)) if self.running is None else self.running
+            own = ring_rows(self.whole, owner_at((self.step + 2) % total))
+            self.running = (ring_next(running).astype(F32) + own.astype(F32)).astype(BF16)
             self.step += 1
-            self.land(ring_next(self.running))
 
     def finish(self):
         self.walk(lax.axis_size("z"))
@@ -710,9 +985,27 @@
         out_ref[:, here] = project(soft, values).astype(BF16)
 
 
-def attend_back_body(inputs, outputs):
+def attend_back_body(blocks, inputs, outputs, grads_held):
+    low_ref, seen_ref, weight_ref, cos_ref, sin_ref, place_ref = inputs[:6]
+    seen_tile, grad_tile, attended_ref = inputs[6:]
+    out_ref, outer_ref = outputs
+    step = pl.program_id(0)
+    block = out_ref.shape[0]
+
+    @pl.when(step < blocks)
+    def _():
+        attend_back_block(inputs[:6], out_ref)
+        grads_held[pl.ds(pl.multiple_of(step * block, block), block), :] = out_ref[...]
+
+    @pl.when(step >= blocks)
+    def _():
+        width = out_ref.shape[1]
+        outer_ref[:, :width] = outer_sum(seen_tile[...], grads_held[...]).astype(BF16)
+        outer_ref[:, width:] = outer_sum(grad_tile[...], attended_ref[...]).astype(BF16)
+
+
+def attend_back_block(inputs, out_ref):
     low_ref, seen_ref, weight_ref, cos_ref, sin_ref, place_ref = inputs
-    (out_ref,) = outputs
     width = weight_ref.shape[1]
     cos_rows, sin_rows = cos_ref[...], -sin_ref[...]
     visible = visible_of(place_ref[...])
@@ -772,15 +1065,17 @@
     return jax.ShapeDtypeStruct((4, block.shape[0] // 4, block.shape[1]), block.dtype)
 
 
-def by_blocks(body, operands, specs, shapes, out_specs, blocks, name, ride, flops, collect=()):
+def by_blocks(
+    body, operands, specs, shapes, out_specs, blocks, name, ride, flops, collect=(), own_scratch=(), advances=()
+):
     extra = len(collect)
     operands, shapes = list(operands) + list(collect), list(shapes)
     shapes += [collected_shape(block) for block in collect]
-    anywhere = pl.BlockSpec(memory_space=pl.ANY)
+    anywhere = pl.BlockSpec(memory_space=pltpu.HBM)
     specs, out_specs = list(specs) + [anywhere] * extra, list(out_specs) + [anywhere] * extra
-    scratch = []
+    scratch = list(own_scratch)
     if extra:
-        scratch = [
+        scratch += [
             pltpu.SemaphoreType.DMA((3 * extra,)),
             pltpu.SemaphoreType.DMA((3 * extra,)),
             pltpu.SemaphoreType.DMA((extra,)),
@@ -796,7 +1091,7 @@
         keeps, copies = [], []
         if extra:
             keeps, copies = collect_copies(
-                inputs[count_in - extra : count_in], outputs[count_out - extra : count_out], *held[:3]
+                inputs[count_in - extra : count_in], outputs[count_out - extra : count_out], *held[len(scratch) - 3 : len(scratch)]
             )
         if ride.copies or extra:
 
@@ -807,7 +1102,9 @@
                 for copy in keeps + copies:
                     copy.start()
 
-        body(inputs[: count_in - extra], outputs[: count_out - extra])
+        body(inputs[: count_in - extra], outputs[: count_out - extra], *held[: len(own_scratch)])
+        for number in advances:
+            pl.when(step == number)(ride.advance)
         if ride.copies or extra:
 
             @pl.when(step == blocks - 1)
@@ -827,7 +1124,7 @@
         out_shape=list(shapes) + ride.shapes,
         scratch_shapes=scratch + ride.scratch,
         input_output_aliases={count_in + k: count_out + v for k, v in ride.aliases.items()},
-        compiler_params=pltpu.CompilerParams(vmem_limit_bytes=40 << 20, **params),
+        compiler_params=pltpu.CompilerParams(vmem_limit_bytes=VMEM_BYTES, **params),
         cost_estimate=pl.CostEstimate(flops=flops, bytes_accessed=40 << 20, transcendentals=0),
         name=name,
     )(*operands, *ride.operands)
@@ -864,29 +1161,46 @@
     return got[:2], got[2:]
 
 
-def attend_back(low, seen, weight, cos_rows, sin_rows, places, block, ride, collect):
-    rows, depth = seen.shape
+def attend_back(low, grad_all, weight, cos_rows, sin_rows, places, seen, attended, block, ride, collect):
+    rows, depth = grad_all.shape
     width = weight.shape[1] // 4
+    blocks = rows // block
+    tile = 256
+
+    def early(columns):
+        return pl.BlockSpec((block, columns), lambda i: (jnp.minimum(i, blocks - 1), 0))
+
+    def late(i):
+        return jnp.maximum(i - blocks, 0)
+
     got = by_blocks(
-        attend_back_body,
-        [low, seen, weight, cos_rows, sin_rows, places],
+        functools.partial(attend_back_body, blocks),
+        [low, grad_all, weight, cos_rows, sin_rows, places, seen, grad_all, attended],
         [
-            row_spec(block, 3 * width),
-            row_spec(block, depth),
+            early(3 * width),
+            early(depth),
             pl.BlockSpec((depth, width), lambda i: (0, 3)),
-            row_spec(block, HEAD_DIM),
-            row_spec(block, HEAD_DIM),
-            row_spec(block, 1),
+            early(HEAD_DIM),
+            early(HEAD_DIM),
+            early(1),
+            pl.BlockSpec((rows, tile), lambda i: (0, late(i))),
+            pl.BlockSpec((rows, tile), lambda i: (0, late(i))),
+            pl.BlockSpec((rows, width), lambda i: (0, 0)),
         ],
-        [jax.ShapeDtypeStruct((rows, 3 * width), BF16)],
-        [row_spec(block, 3 * width)],
-        rows // block,
+        [
+            jax.ShapeDtypeStruct((rows, 3 * width), BF16),
+            jax.ShapeDtypeStruct((depth, 4 * width), BF16),
+        ],
+        [early(3 * width), pl.BlockSpec((tile, 4 * width), lambda i: (late(i), 0))],
+        blocks + depth // tile,
         "attend_back",
         ride,
-        10 * rows * block * width + 2 * rows * depth * width,
+        10 * rows * block * width + 10 * rows * depth * width,
         collect,
-    )
-    last = 1 + len(collect)
+        [pltpu.VMEM((rows, 3 * width), BF16)],
+        (blocks - 2, blocks + depth // tile - 3),
+    )
+    last = 2 + len(collect)
     return got[:last], got[last:]
 
 
@@ -947,11 +1261,11 @@
         4,
         segment_ids.reshape(-1, 128),
         packed.reshape(devices, per_peer, -1),
-        1,
+        2,
         "dispatch",
     )
     arrived = project(recv_pick, landed.reshape(tok_rows, -1))
-    attention_w, gate_w = Gathered(attention_whole, 1), Gathered(gate_whole)
+    attention_w, gate_w = Gathered(attention_whole, 2), Gathered(gate_whole)
     up_w, down_w = Gathered(up_whole), Gathered(down_whole)
     head_width = w_query.shape[1] // 4
     places = plane_places(segments.reshape(4, -1))
@@ -965,9 +1279,8 @@
     sin_rows = jnp.concatenate([-sin_half, sin_half], axis=1)
 
     normed_one, scale_one = norm_parts(arrived)
-    def give_back(rows):
-        packed = outer_sum(recv_pick, rows.astype(BF16)).astype(BF16)
-        return project(send_pick, exchange(packed))
+    def send_back(rows):
+        return exchange(outer_sum(recv_pick, rows.astype(BF16)).astype(BF16))
 
     def riding(call, gathers=(), sums=()):
         ride = Ride(
@@ -981,7 +1294,7 @@
 
     seen_one = riding(
         lambda ride: plane_gather(normed_one.astype(BF16), "gather_one", ride),
-        [(attention_w, 2)],
+        [(attention_w, 1), (gate_w, 1)],
     )
     attention = attention_w.finish()
     upstream_low = project(
@@ -995,42 +1308,37 @@
     )
     middle = arrived + riding(
         lambda ride: plane_product([(attended, attention, 3 * head_width)], "product_out", ride),
-        [(gate_w, 2)],
+        [(gate_w, 1), (up_w, 1)],
     )
     normed_two, scale_two = norm_parts(middle)
     seen_two = riding(
         lambda ride: plane_gather(normed_two.astype(BF16), "gather_two", ride), [(up_w, 2)]
     )
-    grad_two_all = riding(
-        lambda ride: plane_gather(after(upstream_low, seen_two), "gather_up", ride),
-        [(up_w, 1), (down_w, 1)],
-    )
     gate_whole, up_whole = gate_w.finish(), up_w.finish()
-    down_w.walk(1)
-    gate_lin = project(after(seen_two, grad_two_all), gate_whole)
-    up_lin = project(seen_two, up_whole)
-    sigmoid = jax.nn.sigmoid(gate_lin)
-    hidden = (gate_lin * sigmoid * up_lin).astype(BF16)
-    weight_down = outer_sum(after(grad_two_all, down_w.whole, hidden), hidden).astype(BF16)
+    grad_two_all, hidden, by_gate, by_up, weight_down = riding(
+        lambda ride: plane_gather_hidden(
+            upstream_low, seen_two, gate_whole, up_whole, "gather_up", ride
+        ),
+        [(down_w, 3)],
+    )
     down_whole = down_w.finish()
-    weight_down = after(weight_down, down_whole)
     summed_down = Summed(weight_down)
-    grad_hidden = project(after(grad_two_all, weight_down), down_whole)
-    summed_down.walk(2)
-    grad_gate = (grad_hidden * up_lin * (sigmoid * (1.0 + gate_lin * (1.0 - sigmoid)))).astype(BF16)
-    grad_up = (grad_hidden * (gate_lin * sigmoid)).astype(BF16)
-    weight_gate = outer_sum(seen_two, grad_gate).astype(BF16)
-    summed_gate = Summed(weight_gate)
-    summed_up = Summed(outer_sum(seen_two, grad_up).astype(BF16))
-    grad_normed_two = riding(
-        lambda ride: plane_product(
-            [(after(grad_gate, weight_gate), gate_whole, 0), (grad_up, up_whole, 0)],
+    grad_normed_two, weight_gate, weight_up = riding(
+        lambda ride: plane_product_back(
+            grad_two_all,
+            down_whole,
+            by_gate,
+            by_up,
+            gate_whole,
+            up_whole,
+            seen_two,
             "product_forward",
             ride,
         ),
         (),
-        [(summed_down, 1), (summed_gate, 1)],
-    )
+        [(summed_down, 3)],
+    )
+    summed_gate, summed_up = Summed(weight_gate), Summed(weight_up)
     output = middle + riding(
         lambda ride: plane_product(
             [(after(hidden, grad_normed_two), down_whole, 0)], "product_down", ride
@@ -1038,59 +1346,48 @@
         (),
         [(summed_gate, 2)],
     )
-    layer_out = give_back(output)
+    returned_out = send_back(output)
     grad_middle = upstream + norm_back(normed_two, scale_two, grad_normed_two)
     grad_one_all = riding(
         lambda ride: plane_gather(
             after(grad_middle.astype(BF16), output), "gather_middle", ride
         ),
         (),
-        [(summed_up, 2)],
-    )
-    grad_qkv, own_down, own_gate = riding(
+        [(summed_gate, 1)],
+    )
+    grad_qkv, weight_attention, own_down, own_gate = riding(
         lambda ride: attend_back(
-            qkv_low,
+            after(qkv_low, returned_out),
             grad_one_all,
             attention,
             cos_rows,
             sin_rows,
             places,
+            seen_one,
+            attended,
             tok_rows,
             ride,
             (summed_down.finish(), summed_gate.finish()),
         ),
         (),
-        [(summed_up, 1)],
-    )
-    own_up = from_plane(summed_up.finish())
-    summed_attention = Summed(
-        jnp.concatenate(
-            [
-                outer_sum(seen_one, grad_qkv).astype(BF16),
-                outer_sum(grad_one_all, attended).astype(BF16),
-            ],
-            axis=1,
-        )
-    )
+        [(summed_up, 3)],
+    )
+    summed_attention = Summed(weight_attention)
     grad_normed_one = riding(
-        lambda ride: plane_product(
-            [
-                (
-                    after(grad_qkv, summed_attention.whole, layer_out, *own_up),
-                    attention,
-                    0,
-                )
-            ], "product_qkv", ride
-        ),
+        lambda ride: plane_product([(grad_qkv, attention, 0)], "product_qkv", ride),
         (),
         [(summed_attention, 2)],
     )
     grad_inputs = grad_middle + norm_back(normed_one, scale_one, grad_normed_one)
-    own_attention = from_plane(summed_attention.finish())
+    own_up, last_attention = from_plane(summed_up.finish()), summed_attention.finish()
+    own_attention = from_plane(last_attention)
+    own_down, own_gate, own_up = [
+        after(own, last_attention) for own in (own_down, own_gate, jnp.stack(own_up))
+    ]
 
     return (
-        layer_out,
-        give_back(grad_inputs),
+        project(send_pick, after(returned_out, grad_normed_one)),
+        project(send_pick, send_back(grad_inputs)),
         side_by_side(own_attention, 0, head_width),
         side_by_side(own_attention, head_width, 2 * head_width),
         side_by_side(own_attention, 2 * head_width, 3 * head_width),

time: 822 us -> 772 us (0.939)
  Pallas kernels: 539 us -> 650 us
  matrix products: 117 us -> 15.9 us
  waiting for transfers between devices: 56.9 us -> 19.2 us
  local copies, waits for them, and re-layouts: 25.1 us -> 11.3 us
    pallas_call x2, Pallas kernels: 59.5 us -> 116 us  [by_blocks(): pl.pallas_call(kernel, grid=(blocks,), in_specs=list(specs) + [anywhere]...]
    dot_general x9 -> x4, matrix products: 58.7 us -> 6.6 us  [outer_sum(): lax.dot_general(left, right, (((0,), (0,)), ((), ())), preferred_element_...]
    dot_general x7 -> x4, matrix products: 58.2 us -> 9.3 us  [project(): return jnp.dot(left, right, preferred_element_type=F32)]
    pallas_call x8, Pallas kernels: 412 us -> 453 us  [communicate(): pl.pallas_call(kernel, in_specs=list(specs) + [anywhere] * len(ride.opera...]
    ppermute x5 -> x1, waiting for transfers between devices: 33.8 us -> 0.95 us  [ring_next(): lax.ppermute(values, 'z', [(i, (i + 1) % total) for i in range(total)])]
    ppermute x2, waiting for transfers between devices: 0.01 us -> 17.9 us  [from_plane(): by_y = lax.ppermute(piece(1 - me_y, me_x), 'y', ((0, 1), (1, 0)))]
    pallas_call x1, Pallas kernels: 67.2 us -> 80.5 us  [dispatch(): pl.pallas_call(functools.partial(dispatch_kernel, count, narrow, steps),...]
    convert_element_type x9 -> x1, other arithmetic: 13.9 us -> 1.94 us  [walk(): (ring_next(running).astype(F32) + own.astype(F32)).astype(BF16)]
  transfers between devices with their start and end apart: 14 -> 10, of which waited for: 6 -> 4; matrix products, arithmetic and copies ran while one was open for 16% -> 5% of each run, Pallas kernels for 17% -> 24%
where the time goes in v4:
time: 772 us; the launch traced here: 768 us
  Pallas kernels  650 us (84%)
  other arithmetic  46.6 us (6%)
  starting transfers between devices  23.5 us (3%)
  waiting for transfers between devices  19.2 us (2%)
  matrix products  15.9 us (2%)
  local copies, waits for them, and re-layouts  11.3 us (1%)
    pallas_call x8, Pallas kernels, communicate(): pl.pallas_call(kernel, in_specs=list(specs) + [anywhere] * len(ride.opera...  453 us
    pallas_call x2, Pallas kernels, by_blocks(): pl.pallas_call(kernel, grid=(blocks,), in_specs=list(specs) + [anywhere]...  116 us
    pallas_call x1, Pallas kernels, dispatch(): pl.pallas_call(functools.partial(dispatch_kernel, count, narrow, steps),...  80.5 us
    ppermute x2, waiting for transfers between devices, from_plane(): by_y = lax.ppermute(piece(1 - me_y, me_x), 'y', ((0, 1), (1, 0)))  17.9 us
  transfers between devices with their start and end apart: 10, of which 4 were waited for; matrix products, arithmetic and copies ran while one was open for 5% of the time, Pallas kernels for 24%

profile of v4, /device:TPU:0, one launch (start us, length us, event | category | flops | bytes accessed | tf_op | source)
XLA Modules:
  0.0 767.6 jit_solution(16234407318517238454)
XLA Ops:
  0.7 1.9 convert_element_type.155.refs_0_
  2.6 1.8 convert_element_type.156.refs_1_
  4.3 1.8 convert_element_type.157.refs_2_
  7.0 2.8 convert_element_type.160.refs_4_
  10.9 2.6 copy.39
  13.9 1.5 fusion.refs_8_
  15.5 80.5 %dispatch.1 = (bf16[2048,1024]{1,0:T(8,128)(2,1)}, bf16[2048,1024]{1,0:T(8,128)(2,1)}, bf16[2048,1024]{1,0:T(8,128)(2,1)}, bf16[2048,1024]{1,0:T(8,128)(2,1)}, s...) custom-call(bf16[128,1024]{1,0:T(8,128)(2,1)} %convert_element_type.155.refs_0_, ...), custom_call_target="tpu_custom_call" | custom-call | bytes 125829120 | tf_op jit(solution)/shard_map/dispatch/pallas_call | solution.py:364
  96.0 1.8 fusion.36
  99.5 49.3 %gather_one.1 = (bf16[2048,2048]{1,0:T(8,128)(2,1)}, bf16[2048,1024]{1,0:T(8,128)(2,1)}, bf16[2048,1024]{1,0:T(8,128)(2,1)}) custom-call(bf16[256,2048]{1,0:T(8,128)(2,1)} %fusion.4.refs_0_, bf16[2048,1024]{1,0:T(8,128)(2,1)} %get-tuple-element.56.refs_1_, bf16[2048,1024]{1,0:T(8,128)(2,1)} %get-tuple-element.57.refs_2_), custom_call_target="tpu_custom_call", output_to_operand_aliasing={{1}: (1, {}), {2}: (2, {})} | custom-call | bytes 125829120 | tf_op jit(solution)/shard_map/gather_one/pallas_call | solution.py:233
  148.8 1.5 fusion.1
  150.3 4.8 all-to-all-start
  155.4 5.4 fusion.16
  160.7 1.3 pad_maximum_fusion.refs_2_.refs_3_
  162.1 1.3 copy.47
  163.4 2.5 pad_maximum_fusion.1.refs_3_.refs_4_
  165.9 33.9 %attend.1 = (bf16[2048,768]{1,0:T(8,128)(2,1)}, bf16[2048,256]{1,0:T(8,128)(2,1)}, bf16[2048,1024]{1,0:T(8,128)(2,1)}) custom-call(bf16[2048,2048]{1,0:T(8,128)(2,1)} %get-tuple-element.58.refs_0_.refs_6_, bf16[2048,1024]{1,0:T(8,128)(2,1)} %get-tuple-element.59.refs_1_.refs_2_, ...), custom_call_target="tpu_custom_call", output_to_operand_aliasing={{2}: (5, {})} | custom-call | flops 6979321856 | bytes 41943040 | tf_op jit(solution)/shard_map/attend/pallas_call | solution.py:1119
  199.9 56.2 %product_out.1 = (f32[256,2048]{1,0:T(8,128)}, bf16[2048,1024]{1,0:T(8,128)(2,1)}, bf16[2048,1024]{1,0:T(8,128)(2,1)}) custom-call(bf16[2048,256]{1,0:T(8,128)(2,1)} %get-tuple-element.62.refs_0_.refs_8_, bf16[2048,1024]{1,0:T(8,128)(2,1)} %get-tuple-element.59.refs_1_.refs_2_, ...), custom_call_target="tpu_custom_call", output_to_operand_aliasing={{1}: (2, {}), {2}: (3, {})} | custom-call | flops 2147483648 | bytes 125829120 | tf_op jit(solution)/shard_map/product_out/pallas_call | solution.py:233
  256.1 1.9 fusion.31
  258.3 1.3 fusion.5.refs_0_
  259.7 48.8 %gather_two.1 = (bf16[2048,2048]{1,0:T(8,128)(2,1)}, bf16[2048,1024]{1,0:T(8,128)(2,1)}) custom-call(bf16[256,2048]{1,0:T(8,128)(2,1)} %fusion.5.refs_0_, bf16[2048,1024]{1,0:T(8,128)(2,1)} %get-tuple-element.67.refs_1_), custom_call_target="tpu_custom_call", output_to_operand_aliasing={{1}: (1, {})} | custom-call | bytes 125829120 | tf_op jit(solution)/shard_map/gather_two/pallas_call | solution.py:233
  308.5 2.7 convolution_convert_fusion.2.refs_0_
  311.2 73.8 %gather_up.1 = (bf16[2048,2048]{1,0:T(8,128)(2,1)}, bf16[2048,1024]{1,0:T(8,128)(2,1)}, bf16[2048,1024]{1,0:T(8,128)(2,1)}, bf16[2048,1024]{1,0:T(8,128)(2,1)}, ...) custom-call(bf16[256,2048]{1,0:T(8,128)(2,1)} %convolution_convert_fusion.2.refs_0_, ...), custom_call_target="tpu_custom_call", output_to_operand_aliasing={{5}: (4, {})} | custom-call | flops 25769803776 | bytes 125829120 | tf_op jit(solution)/shard_map/gather_up/pallas_call | solution.py:233
  385.0 73.3 %product_forward.1 = (f32[256,2048]{1,0:T(8,128)}, bf16[2048,1024]{1,0:T(8,128)(2,1)}, bf16[2048,1024]{1,0:T(8,128)(2,1)}, bf16[512,1024]{1,0:T(8,128)(2,1)}) custom-call(bf16[2048,1024]{1,0:T(8,128)(2,1)} %get-tuple-element.73.refs_0_, bf16[2048,1024]{1,0:T(8,128)(2,1)} %get-tuple-element.69.refs_2_.refs_1_, bf16[2048,1024]{1,0:T(8,128)(2,1)} %get-tuple-element.74.refs_2_, ...), custom_call_target="tpu_custom_call" | custom-call | flops 42949672960 | bytes 125829120 | tf_op jit(solution)/shard_map/product_forward/pallas_call | solution.py:233
  458.4 53.4 %product_down.1 = (f32[256,2048]{1,0:T(8,128)}, bf16[512,1024]{1,0:T(8,128)(2,1)}) custom-call(bf16[2048,1024]{1,0:T(8,128)(2,1)} %get-tuple-element.79.refs_0_, bf16[2048,1024]{1,0:T(8,128)(2,1)} %get-tuple-element.76.refs_5_.refs_1_, bf16[2048,1024]{1,0:T(8,128)(2,1)} %get-tuple-element.80.refs_2_), custom_call_target="tpu_custom_call" | custom-call | flops 8589934592 | bytes 125829120 | tf_op jit(solution)/shard_map/product_down/pallas_call | solution.py:233
  511.7 2.5 add.82
  514.2 1.6 fusion.2
  515.8 3.1 all-to-all-start.1
  518.9 2.8 fusion.29
  522.4 3.8 fusion.30
  526.1 46.7 %gather_middle.1 = (bf16[2048,2048]{1,0:T(8,128)(2,1)}, bf16[512,1024]{1,0:T(8,128)(2,1)}) custom-call(bf16[256,2048]{1,0:T(8,128)(2,1)} %get-tuple-element.84.refs_0_, bf16[512,1024]{1,0:T(8,128)(2,1)} %get-tuple-element.85.refs_1_, bf16[2048,1024]{1,0:T(8,128)(2,1)} %get-tuple-element.80.refs_2_), custom_call_target="tpu_custom_call" | custom-call | bytes 125829120 | tf_op jit(solution)/shard_map/gather_middle/pallas_call | solution.py:233
  572.9 82.3 %attend_back.1 = (bf16[2048,768]{1,0:T(8,128)(2,1)}, bf16[2048,1024]{1,0:T(8,128)(2,1)}, bf16[4,128,1024]{2,1,0:T(8,128)(2,1)}, bf16[4,128,1024]{2,1,0:T(8,128)(2,1)}, bf16[512,1024]{1,0:T(8,128)(2,1)}) custom-call(bf16[2048,768]{1,0:T(8,128)(2,1)} %get-tuple-element.83.refs_0_, bf16[2048,2048]{1,0:T(8,128)(2,1)} %get-tuple-element.86.refs_1_.refs_7_, ...), custom_call_target="tpu_custom_call" | custom-call | flops 12079595520 | bytes 41943040 | tf_op jit(solution)/shard_map/attend_back/pallas_call | solution.py:1119
  655.2 51.3 %product_qkv.1 = (f32[256,2048]{1,0:T(8,128)}, bf16[512,1024]{1,0:T(8,128)(2,1)}) custom-call(bf16[2048,768]{1,0:T(8,128)(2,1)} %get-tuple-element.90.refs_0_, bf16[2048,1024]{1,0:T(8,128)(2,1)} %get-tuple-element.59.refs_1_.refs_2_, bf16[2048,1024]{1,0:T(8,128)(2,1)} %get-tuple-element.91.refs_2_), custom_call_target="tpu_custom_call" | custom-call | flops 6442450944 | bytes 125829120 | tf_op jit(solution)/shard_map/product_qkv/pallas_call | solution.py:233
  706.6 2.2 fusion.28
  710.1 2.0 fusion.3
  712.0 6.5 all-to-all-start.2
  718.6 1.8 collective-permute-start.5
  720.4 1.5 collective-permute-start.6
  722.2 1.8 fusion.17
  724.0 11.9 %collective-permute-done.5 = bf16[128,1024]{1,0:T(8,128)(2,1)S(1)} collective-permute-done((bf16[128,1024]{1,0:T(8,128)(2,1)S(1)}, bf16[128,1024]{1,0:T(8,128)(2,1)S(1)}, u32[]{:S(2)}, u32[]{:S(2)}) %collective-permute-start.5) | collective-permute-done | bytes 262176 | tf_op jit(solution)/shard_map/ppermute | solution.py:933
  737.4 1.9 add_convert_fusion
  740.2 1.8 collective-permute-start.2
  742.0 2.0 collective-permute-start.3
  746.8 1.8 copy.43
  748.6 2.7 maximum_convert_fusion
  751.3 1.5 maximum_convert_fusion.1
  752.9 6.0 collective-permute-done.2
  759.2 1.4 broadcast_select_fusion.11
  764.3 3.0 fusion.6
  (93 shorter events, 16.0 us)
Async XLA Ops:
  0.6 13.3 %copy-start = (bf16[256,2048]{1,0:T(8,128)(2,1)S(1)}, bf16[256,2048]{1,0:T(8,128)(2,1)}, u32[]{:S(2)}) copy-start(bf16[256,2048]{1,0:T(8,128)(2,1)} %param.12) | copy-start | bytes 3145732
  0.7 5.5 copy-start.16
  7.0 2.8 copy-start.7
  10.9 2.6 copy-start.17
  10.9 2.6 copy-start.19
  99.4 49.3 %copy-start.10 = (bf16[256,2048]{1,0:T(8,128)(2,1)S(1)}, bf16[256,2048]{1,0:T(8,128)(2,1)}, u32[]{:S(2)}) copy-start(bf16[256,2048]{1,0:T(8,128)(2,1)} %param.13) | copy-start | bytes 3145732
  148.8 6.3 copy-start.18
  150.3 158.2 %all-to-all-start = ((bf16[32,8,2048]{2,1,0:T(8,128)(2,1)}), bf16[32,8,2048]{2,1,0:T(8,128)(2,1)}, u32[]{:S(2)}, u32[]{:S(2)}) async-start(bf16[32,8,2048]{2,1,0:T(8,128)(2,1)} %fusion.1), calls=%async_computation | async-start | bytes 2097152 | tf_op jit(solution)/shard_map/all_to_all | solution.py:1225
  257.9 1.7 copy-start.2
  515.8 57.1 %all-to-all-start.1 = ((bf16[32,8,2048]{2,1,0:T(8,128)(2,1)}), bf16[32,8,2048]{2,1,0:T(8,128)(2,1)S(1)}, u32[]{:S(2)}, u32[]{:S(2)}) async-start(bf16[32,8,2048]{2,1,0:T(8,128)(2,1)} %fusion.2), calls=%async_computation.1 | async-start | bytes 2097152 | tf_op jit(solution)/shard_map/all_to_all | solution.py:1225
  518.9 2.9 copy-start.3
  518.9 3.5 copy-start.5
  706.6 3.5 copy-start.4
  706.6 3.5 copy-start.6
  708.9 28.5 %collective-permute-start = (bf16[512,1024]{1,0:T(8,128)(2,1)}, bf16[512,1024]{1,0:T(8,128)(2,1)}, u32[]{:S(2)}, u32[]{:S(2)}) collective-permute-start(bf16[512,1024]{1,0:T(8,128)(2,1)} %get-tuple-element.94), channel_id=1, source_target_pairs={{0,8},{8,16},{16,24},{24,0},{1,9},{9,17},{17,25},{25,1},{2,10},{10... | collective-permute-start | bytes 3145736 | tf_op jit(solution)/shard_map/ppermute | solution.py:862
  712.0 6.5 copy-start.11
  712.0 52.3 %all-to-all-start.2 = ((bf16[32,8,2048]{2,1,0:T(8,128)(2,1)}), bf16[32,8,2048]{2,1,0:T(8,128)(2,1)}, u32[]{:S(2)}, u32[]{:S(2)}) async-start(bf16[32,8,2048]{2,1,0:T(8,128)(2,1)} %fusion.3), calls=%async_computation.2 | async-start | bytes 2097152 | tf_op jit(solution)/shard_map/all_to_all | solution.py:1225
  718.6 17.3 %collective-permute-start.5 = (bf16[128,1024]{1,0:T(8,128)(2,1)S(1)}, bf16[128,1024]{1,0:T(8,128)(2,1)S(1)}, u32[]{:S(2)}, u32[]{:S(2)}) collective-permute-start(bf16[128,1024]{1,0:T(8,128)(2,1)S(1)} %get-tuple-element.154), channel_id=1, source_target_pairs={{0,4},{4,0},{1,5},{5,1},{2,6},{6,2},{3,7},{7,3},{8,12},{12,8},{9,1... | collective-permute-start | bytes 786440 | tf_op jit(solution)/shard_map/ppermute | solution.py:933
  720.4 15.5 %collective-permute-start.6 = (bf16[128,1024]{1,0:T(8,128)(2,1)S(1)}, bf16[128,1024]{1,0:T(8,128)(2,1)S(1)}, u32[]{:S(2)}, u32[]{:S(2)}) collective-permute-start(bf16[128,1024]{1,0:T(8,128)(2,1)S(1)} %get-tuple-element.153), channel_id=1, source_target_pairs={{0,6},{2,4},{4,2},{6,0},{1,7},{3,5},{5,3},{7,1},{8,14},{10,12},{12... | collective-permute-start | bytes 786440 | tf_op jit(solution)/shard_map/ppermute | solution.py:934
  721.9 14.1 %collective-permute-start.4 = (bf16[128,1024]{1,0:T(8,128)(2,1)S(1)}, bf16[128,1024]{1,0:T(8,128)(2,1)S(1)}, u32[]{:S(2)}, u32[]{:S(2)}) collective-permute-start(bf16[128,1024]{1,0:T(8,128)(2,1)S(1)} %get-tuple-element.152), channel_id=1, source_target_pairs={{0,2},{2,0},{1,3},{3,1},{4,6},{6,4},{5,7},{7,5},{8,10},{10,8},{9,1... | collective-permute-start | bytes 786440 | tf_op jit(solution)/shard_map/ppermute | solution.py:932
  736.4 8.2 %copy-start.9 = (bf16[4,128,1024]{2,1,0:T(8,128)(2,1)S(1)}, bf16[4,128,1024]{2,1,0:T(8,128)(2,1)}, u32[]{:S(2)}) copy-start(bf16[4,128,1024]{2,1,0:T(8,128)(2,1)} %get-tuple-element.96) | copy-start | bytes 3145732
  740.2 18.6 %collective-permute-start.2 = (bf16[128,1024]{1,0:T(8,128)(2,1)}, bf16[128,1024]{1,0:T(8,128)(2,1)}, u32[]{:S(2)}, u32[]{:S(2)}) collective-permute-start(bf16[128,1024]{1,0:T(8,128)(2,1)} %get-tuple-element.161), channel_id=1, source_target_pairs={{0,4},{4,0},{1,5},{5,1},{2,6},{6,2},{3,7},{7,3},{8,12},{12,8},{9,1... | collective-permute-start | bytes 786440 | tf_op jit(solution)/shard_map/ppermute | solution.py:933
  742.0 16.8 %collective-permute-start.3 = (bf16[128,1024]{1,0:T(8,128)(2,1)}, bf16[128,1024]{1,0:T(8,128)(2,1)}, u32[]{:S(2)}, u32[]{:S(2)}) collective-permute-start(bf16[128,1024]{1,0:T(8,128)(2,1)} %get-tuple-element.160), channel_id=1, source_target_pairs={{0,6},{2,4},{4,2},{6,0},{1,7},{3,5},{5,3},{7,1},{8,14},{10,12},{12... | collective-permute-start | bytes 786440 | tf_op jit(solution)/shard_map/ppermute | solution.py:934
  744.0 15.2 %collective-permute-start.1 = (bf16[128,1024]{1,0:T(8,128)(2,1)}, bf16[128,1024]{1,0:T(8,128)(2,1)}, u32[]{:S(2)}, u32[]{:S(2)}) collective-permute-start(bf16[128,1024]{1,0:T(8,128)(2,1)} %get-tuple-element.159), channel_id=1, source_target_pairs={{0,2},{2,0},{1,3},{3,1},{4,6},{6,4},{5,7},{7,5},{8,10},{10,8},{9,1... | collective-permute-start | bytes 786440 | tf_op jit(solution)/shard_map/ppermute | solution.py:932
  744.6 1.9 copy-start.8
  748.6 2.7 copy-start.12
  748.6 2.7 copy-start.13
  748.6 2.7 copy-start.14
  748.6 2.7 copy-start.15
  762.6 4.7 copy-start.1

commit v5 on v4

--- a/solution.py
+++ b/solution.py
@@ -258,27 +258,50 @@
         super().board([None], [whole], semaphores)
 
 
-def dispatch_kernel(count, narrow, steps, *refs):
+def dispatch_kernel(turned, narrow, steps, *refs):
+    count = len(turned)
     inputs, refs = refs[:count], refs[count:]
     places, packed, refs = refs[0], refs[1], refs[2:]
     wholes, refs = refs[: count - narrow + 1], refs[count - narrow + 1 :]
-    all_places, landed, send, recv, local, rows_send, rows_recv = refs[:7]
+    all_places, landed, send, recv, local, rows_send, rows_recv, step_send, step_recv = refs[:9]
+    loaded, refs = refs[9], refs[10:]
+    wide, low = refs[:count], refs[count:]
     ride = OwnRide(steps)
-    ride.take(wholes[0], refs[7:])
+    ride.take(wholes[0], (step_send, step_recv))
+    loads = [
+        pltpu.make_async_copy(source, held, loaded.at[index])
+        for index, (source, held) in enumerate(zip(inputs, wide))
+    ]
+    for load in loads:
+        load.start()
     me_y, me_x = lax.axis_index("y"), lax.axis_index("x")
     me_z, me_c = lax.axis_index("z"), lax.axis_index("c")
     rank = me_y * 2 + me_x
-    rows = inputs[0].shape[0]
+    rows = low[0].shape[0]
     at = pl.ds(pl.multiple_of(me_z * (4 * rows) + rank * rows, rows), rows)
     peers = ((("x",), me_y * 2 + 1 - me_x), (("y",), (1 - me_y) * 2 + me_x))
     peers += ((("y", "x"), (1 - me_y) * 2 + 1 - me_x),)
 
     def piece(index, owner):
-        width = inputs[index].shape[1] // 4
-        return inputs[index].at[:, pl.ds(pl.multiple_of(owner * width, width), width)]
+        width = low[index].shape[1] // 4
+        return low[index].at[:, pl.ds(pl.multiple_of(owner * width, width), width)]
+
+    def fill(index):
+        loads[index].wait()
+        size = 512
+
+        @pl.loop(0, low[index].shape[1] // size)
+        def _(step):
+            here = pl.ds(pl.multiple_of(step * size, size), size)
+            if turned[index]:
+                low[index][:, here] = wide[index][here, :].T.astype(BF16)
+            else:
+                low[index][:, here] = wide[index][:, here].astype(BF16)
+
+        keeps[index].start()
 
     def target(index):
-        width = inputs[index].shape[1] // 4
+        width = low[index].shape[1] // 4
         if index < narrow:
             return wholes[0].at[at, pl.ds(index * width, width)]
         return wholes[index - narrow + 1].at[at]
@@ -291,7 +314,7 @@
     ]
     keeps.append(pltpu.make_async_copy(places, all_places.at[rank], local.at[count]))
     keeps.append(pltpu.make_async_copy(packed.at[me], landed.at[me], local.at[count + 1]))
-    for keep in keeps:
+    for keep in keeps[count:]:
         keep.start()
 
     def device(shift):
@@ -305,6 +328,8 @@
     def _(shift):
         pl.semaphore_signal(barrier, inc=1, device_id=device(shift), device_id_type=MESH)
 
+    for index in range(narrow):
+        fill(index)
     pl.semaphore_wait(barrier, devices - 1)
     copies = {}
 
@@ -334,6 +359,8 @@
             device_id_type=MESH,
         ).start()
 
+    for index in range(narrow, count):
+        fill(index)
     for index in range(narrow):
         arrive(index)
     ride.begin()
@@ -351,18 +378,19 @@
     pltpu.make_async_copy(packed.at[most], packed.at[most], rows_send).wait()
 
 
-def dispatch(weights, narrow, places, packed, steps, name):
-    rows = weights[0].shape[0]
+def dispatch(weights, turned, narrow, places, packed, steps, name):
+    flat = [w.shape[::-1] if flip_it else w.shape for w, flip_it in zip(weights, turned)]
+    rows = flat[0][0]
     total = lax.axis_size("z")
     anywhere = pl.BlockSpec(memory_space=pltpu.HBM)
     count = len(weights)
-    widths = [sum(weight.shape[1] // 4 for weight in weights[:narrow])]
-    widths += [weight.shape[1] // 4 for weight in weights[narrow:]]
+    widths = [sum(shape[1] // 4 for shape in flat[:narrow])]
+    widths += [shape[1] // 4 for shape in flat[narrow:]]
     shapes = [jax.ShapeDtypeStruct((total * 4 * rows, width), BF16) for width in widths]
     shapes.append(jax.ShapeDtypeStruct((4, *places.shape), places.dtype))
     shapes.append(jax.ShapeDtypeStruct(packed.shape, packed.dtype))
     return pl.pallas_call(
-        functools.partial(dispatch_kernel, count, narrow, steps),
+        functools.partial(dispatch_kernel, tuple(turned), narrow, steps),
         in_specs=[anywhere] * (count + 2),
         out_specs=[anywhere] * len(shapes),
         out_shape=shapes,
@@ -374,7 +402,10 @@
             pltpu.SemaphoreType.DMA(()),
             pltpu.SemaphoreType.DMA((steps,)),
             pltpu.SemaphoreType.DMA((steps,)),
-        ],
+            pltpu.SemaphoreType.DMA((count,)),
+        ]
+        + [pltpu.VMEM(weight.shape, F32) for weight in weights]
+        + [pltpu.VMEM(shape, BF16) for shape in flat],
         compiler_params=pltpu.CompilerParams(
             collective_id=IDS.index(name), has_side_effects=True, vmem_limit_bytes=VMEM_BYTES
         ),
@@ -443,6 +474,63 @@
         pass
 
 
+def gather_turns_body(inputs, outputs, scratch, ride):
+    own, table_ref, places_ref = inputs
+    out, cos_ref, sin_ref = outputs
+    stages = gather_stages(own, out, *scratch, ride)
+    next(stages)
+    size, width = table_ref.shape[0], 2 * HEAD_DIM
+    count, _, block = places_ref.shape
+    for index in range(count):
+        at = pl.ds(index * block, block)
+        entry = lax.broadcasted_iota(jnp.int32, (size, block), 0)
+        pick = (entry == places_ref[index]).astype(F32).astype(BF16)
+        rows = outer_sum(pick, table_ref[:, :width])
+        rows += outer_sum(pick, table_ref[:, width : 2 * width])
+        rows += outer_sum(pick, table_ref[:, 2 * width :])
+        cos_ref[at, :] = rows[:, :HEAD_DIM]
+        sin_ref[at, :] = rows[:, HEAD_DIM:]
+
+    for _ in stages:
+        pass
+
+
+def rotation_table(size):
+    half_dim = HEAD_DIM // 2
+    frequency = jnp.exp(-jnp.arange(half_dim, dtype=F32) * (2.0 * math.log(10000.0) / HEAD_DIM))
+    angles = jnp.arange(size, dtype=jnp.int32).astype(F32)[:, None] * frequency[None, :]
+    cos_half, sin_half = jnp.cos(angles), jnp.sin(angles)
+    rest = jnp.concatenate([cos_half, cos_half, -sin_half, sin_half], axis=1)
+    terms = []
+    for _ in range(3):
+        term = lax.reduce_precision(rest, 8, 7)
+        terms.append(term.astype(BF16))
+        rest = rest - term
+    return jnp.concatenate(terms, axis=1)
+
+
+def plane_gather_turns(rows, table, places, name, ride):
+    anywhere = pl.BlockSpec(memory_space=pltpu.HBM)
+    near = pl.BlockSpec(memory_space=pltpu.VMEM)
+    total = 8 * rows.shape[0]
+    got = communicate(
+        gather_turns_body,
+        [rows, table, places],
+        [anywhere, near, near],
+        [jax.ShapeDtypeStruct((total, rows.shape[1]), rows.dtype)]
+        + [jax.ShapeDtypeStruct((total, HEAD_DIM), F32)] * 2,
+        [anywhere, near, near],
+        [
+            pltpu.SemaphoreType.DMA((13,)),
+            pltpu.SemaphoreType.DMA((13,)),
+            pltpu.SemaphoreType.DMA(()),
+        ],
+        name,
+        ride,
+    )
+    return got[:3], got[3:]
+
+
 def outer_tiles(sources, targets, tiles, stage, loads, stores, between=lambda: None):
     count = tiles[0].shape[0]
     tile = tiles[0].shape[2]
@@ -950,11 +1038,11 @@
     return values * cos_rows + pltpu.roll(values, HEAD_DIM // 2, 1) * sin_rows
 
 
-def visible_of(places):
-    size = places.shape[0]
+def visible_of(follow):
+    size = follow.shape[1]
     row = lax.broadcasted_iota(jnp.int32, (size, size), 0)
     column = lax.broadcasted_iota(jnp.int32, (size, size), 1)
-    return (column <= row) & (row - column <= places)
+    return (column <= row) & (row - column <= follow)
 
 
 def soft_of(queries, keys, visible):
@@ -965,11 +1053,11 @@
 
 
 def attend_body(inputs, outputs):
-    seen_ref, weight_ref, cos_ref, sin_ref, place_ref = inputs
+    seen_ref, weight_ref, cos_ref, sin_ref, follow_ref = inputs
     low_ref, out_ref = outputs
     width = out_ref.shape[1]
     cos_rows, sin_rows = cos_ref[...], sin_ref[...]
-    visible = visible_of(place_ref[...])
+    visible = visible_of(follow_ref[0])
     lin = project(seen_ref[...], weight_ref[...])
     for start in range(0, width, HEAD_DIM):
         here = slice(start, start + HEAD_DIM)
@@ -986,7 +1074,7 @@
 
 
 def attend_back_body(blocks, inputs, outputs, grads_held):
-    low_ref, seen_ref, weight_ref, cos_ref, sin_ref, place_ref = inputs[:6]
+    low_ref, seen_ref, weight_ref, cos_ref, sin_ref, follow_ref = inputs[:6]
     seen_tile, grad_tile, attended_ref = inputs[6:]
     out_ref, outer_ref = outputs
     step = pl.program_id(0)
@@ -1005,10 +1093,10 @@
 
 
 def attend_back_block(inputs, out_ref):
-    low_ref, seen_ref, weight_ref, cos_ref, sin_ref, place_ref = inputs
+    low_ref, seen_ref, weight_ref, cos_ref, sin_ref, follow_ref = inputs
     width = weight_ref.shape[1]
     cos_rows, sin_rows = cos_ref[...], -sin_ref[...]
-    visible = visible_of(place_ref[...])
+    visible = visible_of(follow_ref[0])
     scale = 1.0 / math.sqrt(HEAD_DIM)
     grad_all = project(seen_ref[...], weight_ref[...]).astype(BF16)
     for start in range(0, width, HEAD_DIM):
@@ -1146,7 +1234,7 @@
             pl.BlockSpec((depth, 3 * width), lambda i: (0, 0)),
             row_spec(block, HEAD_DIM),
             row_spec(block, HEAD_DIM),
-            row_spec(block, 1),
+            pl.BlockSpec((1, 1, block), lambda i: (i, 0, 0)),
         ],
         [
             jax.ShapeDtypeStruct((rows, 3 * width), BF16),
@@ -1182,7 +1270,7 @@
             pl.BlockSpec((depth, width), lambda i: (0, 3)),
             early(HEAD_DIM),
             early(HEAD_DIM),
-            early(1),
+            pl.BlockSpec((1, 1, block), lambda i: (jnp.minimum(i, blocks - 1), 0, 0)),
             pl.BlockSpec((rows, tile), lambda i: (0, late(i))),
             pl.BlockSpec((rows, tile), lambda i: (0, late(i))),
             pl.BlockSpec((rows, width), lambda i: (0, 0)),
@@ -1204,14 +1292,16 @@
     return got[:last], got[last:]
 
 
-def plane_places(segments):
+def plane_places(segments, block):
     groups, size = segments.shape
     numbers = jnp.arange(SEGS, dtype=jnp.int32)
     starts = jnp.sum((segments[:, :, None] < numbers).astype(jnp.int32), axis=1)
+    ends = jnp.sum((segments[:, :, None] <= numbers).astype(jnp.int32), axis=1)
     onehot = segments[:, :, None] == numbers
-    offset = jnp.sum(jnp.where(onehot, starts[:, None, :], 0), axis=2)
-    places = jnp.arange(size, dtype=jnp.int32)[None, :] - offset
-    return places.reshape(-1, 1)
+    row = jnp.arange(size, dtype=jnp.int32)[None, :]
+    places = row - jnp.sum(jnp.where(onehot, starts[:, None, :], 0), axis=2)
+    follow = jnp.sum(jnp.where(onehot, ends[:, None, :], 0), axis=2) - 1 - row
+    return places.reshape(-1, 1, block), follow.reshape(-1, 1, block)
 
 
 def after(values, *gates):
@@ -1255,9 +1345,11 @@
     recv_pick = (recv_slot[:, None] == row_index[None, :]).astype(BF16)
 
     packed = outer_sum(send_pick, tokens_in).astype(BF16)
-    weights = [w_query, w_key, w_value, w_out.T, w_gate, w_up, w_down.T]
+    table = rotation_table(tok_rows)
+    weights = [w_query, w_key, w_value, w_out, w_gate, w_up, w_down]
     attention_whole, gate_whole, up_whole, down_whole, segments, landed = dispatch(
-        [weight.astype(BF16) for weight in weights],
+        weights,
+        [False, False, False, True, False, False, True],
         4,
         segment_ids.reshape(-1, 128),
         packed.reshape(devices, per_peer, -1),
@@ -1268,16 +1360,7 @@
     attention_w, gate_w = Gathered(attention_whole, 2), Gathered(gate_whole)
     up_w, down_w = Gathered(up_whole), Gathered(down_whole)
     head_width = w_query.shape[1] // 4
-    places = plane_places(segments.reshape(4, -1))
-    half_dim = HEAD_DIM // 2
-    frequency = jnp.exp(
-        -jnp.arange(half_dim, dtype=F32) * (2.0 * math.log(10000.0) / HEAD_DIM)
-    )
-    angles = places.astype(F32) * frequency[None, :]
-    cos_half, sin_half = jnp.cos(angles), jnp.sin(angles)
-    cos_rows = jnp.concatenate([cos_half, cos_half], axis=1)
-    sin_rows = jnp.concatenate([-sin_half, sin_half], axis=1)
-
+    places, follow = plane_places(segments.reshape(4, -1), tok_rows)
     normed_one, scale_one = norm_parts(arrived)
     def send_back(rows):
         return exchange(outer_sum(recv_pick, rows.astype(BF16)).astype(BF16))
@@ -1292,8 +1375,10 @@
             item.land(value)
         return result
 
-    seen_one = riding(
-        lambda ride: plane_gather(normed_one.astype(BF16), "gather_one", ride),
+    seen_one, cos_rows, sin_rows = riding(
+        lambda ride: plane_gather_turns(
+            normed_one.astype(BF16), table, places, "gather_one", ride
+        ),
         [(attention_w, 1), (gate_w, 1)],
     )
     attention = attention_w.finish()
@@ -1303,7 +1388,7 @@
     ).astype(BF16)
     upstream = upstream_low.astype(F32)
     qkv_low, attended = riding(
-        lambda ride: attend(seen_one, attention, cos_rows, sin_rows, places, tok_rows, ride),
+        lambda ride: attend(seen_one, attention, cos_rows, sin_rows, follow, tok_rows, ride),
         [(gate_w, 1)],
     )
     middle = arrived + riding(
@@ -1353,7 +1438,7 @@
             after(grad_middle.astype(BF16), output), "gather_middle", ride
         ),
         (),
-        [(summed_gate, 1)],
+        [(summed_gate, 1), (summed_up, 1)],
     )
     grad_qkv, weight_attention, own_down, own_gate = riding(
         lambda ride: attend_back(
@@ -1362,7 +1447,7 @@
             attention,
             cos_rows,
             sin_rows,
-            places,
+            follow,
             seen_one,
             attended,
             tok_rows,
@@ -1370,7 +1455,7 @@
             (summed_down.finish(), summed_gate.finish()),
         ),
         (),
-        [(summed_up, 3)],
+        [(summed_up, 2)],
     )
     summed_attention = Summed(weight_attention)
     grad_normed_one = riding(

time: 772 us -> 758 us (0.982)
  other arithmetic: 46.6 us -> 31.8 us
    pallas_call x8, Pallas kernels: 453 us -> 471 us  [communicate(): pl.pallas_call(kernel, in_specs=list(specs) + [anywhere] * len(ride.opera...]
    pallas_call x2, Pallas kernels: 116 us -> 103 us  [by_blocks(): pl.pallas_call(kernel, grid=(blocks,), in_specs=list(specs) + [anywhere]...]
    convert_element_type x5 -> x2, other arithmetic: 9.39 us -> 0.19 us  [the longest x1 0.18 us: rotation_table(): terms.append(term.astype(BF16))]
  transfers between devices with their start and end apart: 10 -> 10, of which waited for: 4 -> 5; matrix products, arithmetic and copies ran while one was open for 5% -> 4% of each run, Pallas kernels for 24% -> 28%
where the time goes in v5:
time: 758 us; the launch traced here: 751 us
  Pallas kernels  655 us (86%)
  other arithmetic  31.8 us (4%)
  waiting for transfers between devices  21.9 us (3%)
  starting transfers between devices  20.3 us (3%)
  matrix products  14.6 us (2%)
    pallas_call x8, Pallas kernels, communicate(): pl.pallas_call(kernel, in_specs=list(specs) + [anywhere] * len(ride.opera...  471 us
    pallas_call x2, Pallas kernels, by_blocks(): pl.pallas_call(kernel, grid=(blocks,), in_specs=list(specs) + [anywhere]...  103 us
    pallas_call x1, Pallas kernels, dispatch(): pl.pallas_call(functools.partial(dispatch_kernel, tuple(turned), narrow,...  80.7 us
    ppermute x2, waiting for transfers between devices, from_plane(): by_y = lax.ppermute(piece(1 - me_y, me_x), 'y', ((0, 1), (1, 0)))  16 us
  transfers between devices with their start and end apart: 10, of which 5 were waited for; matrix products, arithmetic and copies ran while one was open for 4% of the time, Pallas kernels for 28%

profile of v5, /device:TPU:0, one launch (start us, length us, event | category | flops | bytes accessed | tf_op | source)
XLA Modules:
  0.0 751.4 jit_solution(17791928627089774307)
XLA Ops:
  1.5 1.0 convert_reduce_fusion.1
  2.7 1.5 fusion.refs_8_
  4.2 80.7 %dispatch.1 = (bf16[2048,1024]{1,0:T(8,128)(2,1)}, bf16[2048,1024]{1,0:T(8,128)(2,1)}, bf16[2048,1024]{1,0:T(8,128)(2,1)}, bf16[2048,1024]{1,0:T(8,128)(2,1)}, s...) custom-call(f32[128,1024]{1,0:T(8,128)} %refs_0_.1, f32[128,1024]{1,0:T(8,128)} %refs_1_.1, f32[128,1024]{1,0:T(8,128)} %refs_2_.1, ...), custom_call_target="tpu_custom_call" | custom-call | bytes 125829120 | tf_op jit(solution)/shard_map/dispatch/pallas_call | solution.py:392
  84.9 1.8 fusion.38
  87.0 1.3 fusion.4.refs_0_
  91.0 51.7 %gather_one.1 = (bf16[2048,2048]{1,0:T(8,128)(2,1)}, f32[2048,128]{1,0:T(8,128)}, f32[2048,128]{1,0:T(8,128)}, bf16[2048,1024]{1,0:T(8,128)(2,1)}, bf16[2048,1024]{1,0:T(8,128)(2,1)}) custom-call(bf16[256,2048]{1,0:T(8,128)(2,1)} %fusion.4.refs_0_, bf16[256,768]{1,0:T(8,128)(2,1)} %pad_maximum_fusion.1.refs_1_, ...), custom_call_target="tpu_custom_call", output_to_operand_aliasing={{3}: (3, {}), {4}: (4, {})} | custom-call | bytes 125829120 | tf_op jit(solution)/shard_map/gather_one/pallas_call | solution.py:233
  142.7 1.5 fusion.1
  144.2 4.3 all-to-all-start
  148.5 45.0 %attend.1 = (bf16[2048,768]{1,0:T(8,128)(2,1)}, bf16[2048,256]{1,0:T(8,128)(2,1)}, bf16[2048,1024]{1,0:T(8,128)(2,1)}) custom-call(bf16[2048,2048]{1,0:T(8,128)(2,1)} %get-tuple-element.62.refs_0_.refs_6_, bf16[2048,1024]{1,0:T(8,128)(2,1)} %get-tuple-element.63.refs_1_.refs_2_, ...), custom_call_target="tpu_custom_call", output_to_operand_aliasing={{2}: (5, {})} | custom-call | flops 6979321856 | bytes 41943040 | tf_op jit(solution)/shard_map/attend/pallas_call | solution.py:1207
  193.4 56.2 %product_out.1 = (f32[256,2048]{1,0:T(8,128)}, bf16[2048,1024]{1,0:T(8,128)(2,1)}, bf16[2048,1024]{1,0:T(8,128)(2,1)}) custom-call(bf16[2048,256]{1,0:T(8,128)(2,1)} %get-tuple-element.67.refs_0_.refs_8_, bf16[2048,1024]{1,0:T(8,128)(2,1)} %get-tuple-element.63.refs_1_.refs_2_, ...), custom_call_target="tpu_custom_call", output_to_operand_aliasing={{1}: (2, {}), {2}: (3, {})} | custom-call | flops 2147483648 | bytes 125829120 | tf_op jit(solution)/shard_map/product_out/pallas_call | solution.py:233
  249.6 1.9 fusion.32
  251.9 1.3 fusion.5.refs_0_
  253.2 48.8 %gather_two.1 = (bf16[2048,2048]{1,0:T(8,128)(2,1)}, bf16[2048,1024]{1,0:T(8,128)(2,1)}) custom-call(bf16[256,2048]{1,0:T(8,128)(2,1)} %fusion.5.refs_0_, bf16[2048,1024]{1,0:T(8,128)(2,1)} %get-tuple-element.72.refs_1_), custom_call_target="tpu_custom_call", output_to_operand_aliasing={{1}: (1, {})} | custom-call | bytes 125829120 | tf_op jit(solution)/shard_map/gather_two/pallas_call | solution.py:233
  302.0 1.5 convolution_convert_fusion.2.refs_0_
  303.5 73.8 %gather_up.1 = (bf16[2048,2048]{1,0:T(8,128)(2,1)}, bf16[2048,1024]{1,0:T(8,128)(2,1)}, bf16[2048,1024]{1,0:T(8,128)(2,1)}, bf16[2048,1024]{1,0:T(8,128)(2,1)}, ...) custom-call(bf16[256,2048]{1,0:T(8,128)(2,1)} %convolution_convert_fusion.2.refs_0_, ...), custom_call_target="tpu_custom_call", output_to_operand_aliasing={{5}: (4, {})} | custom-call | flops 25769803776 | bytes 125829120 | tf_op jit(solution)/shard_map/gather_up/pallas_call | solution.py:233
  377.2 73.4 %product_forward.1 = (f32[256,2048]{1,0:T(8,128)}, bf16[2048,1024]{1,0:T(8,128)(2,1)}, bf16[2048,1024]{1,0:T(8,128)(2,1)}, bf16[512,1024]{1,0:T(8,128)(2,1)}) custom-call(bf16[2048,1024]{1,0:T(8,128)(2,1)} %get-tuple-element.78.refs_0_, bf16[2048,1024]{1,0:T(8,128)(2,1)} %get-tuple-element.74.refs_2_.refs_1_, bf16[2048,1024]{1,0:T(8,128)(2,1)} %get-tuple-element.79.refs_2_, ...), custom_call_target="tpu_custom_call" | custom-call | flops 42949672960 | bytes 125829120 | tf_op jit(solution)/shard_map/product_forward/pallas_call | solution.py:233
  450.6 52.9 %product_down.1 = (f32[256,2048]{1,0:T(8,128)}, bf16[512,1024]{1,0:T(8,128)(2,1)}) custom-call(bf16[2048,1024]{1,0:T(8,128)(2,1)} %get-tuple-element.84.refs_0_, bf16[2048,1024]{1,0:T(8,128)(2,1)} %get-tuple-element.81.refs_5_.refs_1_, bf16[2048,1024]{1,0:T(8,128)(2,1)} %get-tuple-element.85.refs_2_), custom_call_target="tpu_custom_call" | custom-call | flops 8589934592 | bytes 125829120 | tf_op jit(solution)/shard_map/product_down/pallas_call | solution.py:233
  503.6 2.5 add.98
  506.1 1.5 fusion.2
  507.6 3.7 all-to-all-start.1
  511.3 2.8 fusion.30
  514.8 3.8 fusion.31
  518.6 62.7 %gather_middle.1 = (bf16[2048,2048]{1,0:T(8,128)(2,1)}, bf16[512,1024]{1,0:T(8,128)(2,1)}, bf16[512,1024]{1,0:T(8,128)(2,1)}) custom-call(bf16[256,2048]{1,0:T(8,128)(2,1)} %get-tuple-element.89.refs_0_, bf16[512,1024]{1,0:T(8,128)(2,1)} %get-tuple-element.90.refs_1_, bf16[2048,1024]{1,0:T(8,128)(2,1)} %get-tuple-element.85.refs_2_, ...), custom_call_target="tpu_custom_call" | custom-call | bytes 125829120 | tf_op jit(solution)/shard_map/gather_middle/pallas_call | solution.py:233
  581.2 1.2 all-to-all-done.1
  582.4 58.5 %attend_back.1 = (bf16[2048,768]{1,0:T(8,128)(2,1)}, bf16[2048,1024]{1,0:T(8,128)(2,1)}, bf16[4,128,1024]{2,1,0:T(8,128)(2,1)}, bf16[4,128,1024]{2,1,0:T(8,128)(2,1)}, bf16[512,1024]{1,0:T(8,128)(2,1)}) custom-call(bf16[2048,768]{1,0:T(8,128)(2,1)} %get-tuple-element.88.refs_0_, bf16[2048,2048]{1,0:T(8,128)(2,1)} %get-tuple-element.92.refs_1_.refs_7_, ...), custom_call_target="tpu_custom_call" | custom-call | flops 12079595520 | bytes 41943040 | tf_op jit(solution)/shard_map/attend_back/pallas_call | solution.py:1207
  641.0 51.2 %product_qkv.1 = (f32[256,2048]{1,0:T(8,128)}, bf16[512,1024]{1,0:T(8,128)(2,1)}) custom-call(bf16[2048,768]{1,0:T(8,128)(2,1)} %get-tuple-element.96.refs_0_, bf16[2048,1024]{1,0:T(8,128)(2,1)} %get-tuple-element.63.refs_1_.refs_2_, bf16[2048,1024]{1,0:T(8,128)(2,1)} %get-tuple-element.97.refs_2_), custom_call_target="tpu_custom_call" | custom-call | flops 6442450944 | bytes 125829120 | tf_op jit(solution)/shard_map/product_qkv/pallas_call | solution.py:233
  692.2 2.2 fusion.29
  694.4 1.1 collective-permute-start
  695.5 2.0 fusion.3
  697.5 4.2 all-to-all-start.2
  701.8 1.8 collective-permute-start.5
  703.5 1.5 collective-permute-start.6
  705.3 1.8 fusion.18
  707.1 11.6 %collective-permute-done.5 = bf16[128,1024]{1,0:T(8,128)(2,1)S(1)} collective-permute-done((bf16[128,1024]{1,0:T(8,128)(2,1)S(1)}, bf16[128,1024]{1,0:T(8,128)(2,1)S(1)}, u32[]{:S(2)}, u32[]{:S(2)}) %collective-permute-start.5) | collective-permute-done | bytes 262176 | tf_op jit(solution)/shard_map/ppermute | solution.py:1021
  719.2 3.8 collective-permute-done
  723.0 1.9 add_convert_fusion
  724.9 0.9 constant_dynamic-slice_fusion.5
  726.2 1.7 collective-permute-start.3
  727.9 1.4 collective-permute-start.1
  730.2 1.0 slice_bitcast_fusion.7
  731.6 1.8 copy.34
  733.4 2.7 maximum_convert_fusion
  736.1 1.5 maximum_convert_fusion.1
  737.6 4.5 collective-permute-done.2
  742.1 0.9 collective-permute-done.1
  743.0 1.4 broadcast_select_fusion.11
  744.6 1.0 copy.33
  748.1 3.0 fusion.6
  (83 shorter events, 10.0 us)
Async XLA Ops:
  0.6 2.0 copy-start
  87.0 1.3 copy-start.15
  91.0 51.7 %copy-start.9 = (bf16[256,2048]{1,0:T(8,128)(2,1)S(1)}, bf16[256,2048]{1,0:T(8,128)(2,1)}, u32[]{:S(2)}) copy-start(bf16[256,2048]{1,0:T(8,128)(2,1)} %param.13) | copy-start | bytes 3145732
  144.2 157.8 %all-to-all-start = ((bf16[32,8,2048]{2,1,0:T(8,128)(2,1)}), bf16[32,8,2048]{2,1,0:T(8,128)(2,1)S(1)}, u32[]{:S(2)}, u32[]{:S(2)}) async-start(bf16[32,8,2048]{2,1,0:T(8,128)(2,1)} %fusion.1), calls=%async_computation | async-start | bytes 2097152 | tf_op jit(solution)/shard_map/all_to_all | solution.py:1315
  251.5 1.7 copy-start.2
  507.6 74.8 %all-to-all-start.1 = ((bf16[32,8,2048]{2,1,0:T(8,128)(2,1)}), bf16[32,8,2048]{2,1,0:T(8,128)(2,1)S(1)}, u32[]{:S(2)}, u32[]{:S(2)}) async-start(bf16[32,8,2048]{2,1,0:T(8,128)(2,1)} %fusion.2), calls=%async_computation.1 | async-start | bytes 2097152 | tf_op jit(solution)/shard_map/all_to_all | solution.py:1315
  511.3 2.9 copy-start.3
  511.3 3.5 copy-start.5
  692.2 3.4 copy-start.4
  692.2 3.4 copy-start.6
  694.4 28.6 %collective-permute-start = (bf16[512,1024]{1,0:T(8,128)(2,1)}, bf16[512,1024]{1,0:T(8,128)(2,1)}, u32[]{:S(2)}, u32[]{:S(2)}) collective-permute-start(bf16[512,1024]{1,0:T(8,128)(2,1)} %get-tuple-element.100), channel_id=1, source_target_pairs={{0,8},{8,16},{16,24},{24,0},{1,9},{9,17},{17,25},{25,1},{2,10},{10... | collective-permute-start | bytes 3145736 | tf_op jit(solution)/shard_map/ppermute | solution.py:950
  697.5 4.2 copy-start.10
  697.5 50.6 %all-to-all-start.2 = ((bf16[32,8,2048]{2,1,0:T(8,128)(2,1)}), bf16[32,8,2048]{2,1,0:T(8,128)(2,1)}, u32[]{:S(2)}, u32[]{:S(2)}) async-start(bf16[32,8,2048]{2,1,0:T(8,128)(2,1)} %fusion.3), calls=%async_computation.2 | async-start | bytes 2097152 | tf_op jit(solution)/shard_map/all_to_all | solution.py:1315
  701.8 16.9 %collective-permute-start.5 = (bf16[128,1024]{1,0:T(8,128)(2,1)S(1)}, bf16[128,1024]{1,0:T(8,128)(2,1)S(1)}, u32[]{:S(2)}, u32[]{:S(2)}) collective-permute-start(bf16[128,1024]{1,0:T(8,128)(2,1)S(1)} %get-tuple-element.162), channel_id=1, source_target_pairs={{0,4},{4,0},{1,5},{5,1},{2,6},{6,2},{3,7},{7,3},{8,12},{12,8},{9,1... | collective-permute-start | bytes 786440 | tf_op jit(solution)/shard_map/ppermute | solution.py:1021
  703.5 15.2 %collective-permute-start.6 = (bf16[128,1024]{1,0:T(8,128)(2,1)S(1)}, bf16[128,1024]{1,0:T(8,128)(2,1)S(1)}, u32[]{:S(2)}, u32[]{:S(2)}) collective-permute-start(bf16[128,1024]{1,0:T(8,128)(2,1)S(1)} %get-tuple-element.161), channel_id=1, source_target_pairs={{0,6},{2,4},{4,2},{6,0},{1,7},{3,5},{5,3},{7,1},{8,14},{10,12},{12... | collective-permute-start | bytes 786440 | tf_op jit(solution)/shard_map/ppermute | solution.py:1022
  705.0 13.7 %collective-permute-start.4 = (bf16[128,1024]{1,0:T(8,128)(2,1)S(1)}, bf16[128,1024]{1,0:T(8,128)(2,1)S(1)}, u32[]{:S(2)}, u32[]{:S(2)}) collective-permute-start(bf16[128,1024]{1,0:T(8,128)(2,1)S(1)} %get-tuple-element.160), channel_id=1, source_target_pairs={{0,2},{2,0},{1,3},{3,1},{4,6},{6,4},{5,7},{7,5},{8,10},{10,8},{9,1... | collective-permute-start | bytes 786440 | tf_op jit(solution)/shard_map/ppermute | solution.py:1020
  719.2 10.2 %copy-start.8 = (bf16[4,128,1024]{2,1,0:T(8,128)(2,1)S(1)}, bf16[4,128,1024]{2,1,0:T(8,128)(2,1)}, u32[]{:S(2)}) copy-start(bf16[4,128,1024]{2,1,0:T(8,128)(2,1)} %get-tuple-element.102) | copy-start | bytes 3145732
  725.8 16.3 %collective-permute-start.2 = (bf16[128,1024]{1,0:T(8,128)(2,1)}, bf16[128,1024]{1,0:T(8,128)(2,1)}, u32[]{:S(2)}, u32[]{:S(2)}) collective-permute-start(bf16[128,1024]{1,0:T(8,128)(2,1)} %get-tuple-element.169), channel_id=1, source_target_pairs={{0,4},{4,0},{1,5},{5,1},{2,6},{6,2},{3,7},{7,3},{8,12},{12,8},{9,1... | collective-permute-start | bytes 786440 | tf_op jit(solution)/shard_map/ppermute | solution.py:1021
  726.2 15.9 %collective-permute-start.3 = (bf16[128,1024]{1,0:T(8,128)(2,1)}, bf16[128,1024]{1,0:T(8,128)(2,1)}, u32[]{:S(2)}, u32[]{:S(2)}) collective-permute-start(bf16[128,1024]{1,0:T(8,128)(2,1)} %get-tuple-element.168), channel_id=1, source_target_pairs={{0,6},{2,4},{4,2},{6,0},{1,7},{3,5},{5,3},{7,1},{8,14},{10,12},{12... | collective-permute-start | bytes 786440 | tf_op jit(solution)/shard_map/ppermute | solution.py:1022
  727.9 15.1 %collective-permute-start.1 = (bf16[128,1024]{1,0:T(8,128)(2,1)}, bf16[128,1024]{1,0:T(8,128)(2,1)}, u32[]{:S(2)}, u32[]{:S(2)}) collective-permute-start(bf16[128,1024]{1,0:T(8,128)(2,1)} %get-tuple-element.167), channel_id=1, source_target_pairs={{0,2},{2,0},{1,3},{3,1},{4,6},{6,4},{5,7},{7,5},{8,10},{10,8},{9,1... | collective-permute-start | bytes 786440 | tf_op jit(solution)/shard_map/ppermute | solution.py:1020
  729.3 1.9 copy-start.7
  733.4 2.7 copy-start.11
  733.4 2.7 copy-start.12
  733.4 2.7 copy-start.13
  733.4 2.7 copy-start.14
  746.4 4.7 copy-start.1

commit v6 on v5

--- a/solution.py
+++ b/solution.py
@@ -91,6 +91,8 @@
 
 
 class Ride:
+    sides = 2
+
     def __init__(self, gathers=(), sums=()):
         self.gathers, self.sums = tuple(gathers), tuple(sums)
         self.operands, self.shapes, self.scratch = [], [], []
@@ -113,8 +115,8 @@
             ]
         if self.steps:
             self.scratch += [
-                pltpu.SemaphoreType.DMA((self.steps,)),
-                pltpu.SemaphoreType.DMA((self.steps,)),
+                pltpu.SemaphoreType.DMA((2 * self.steps,)),
+                pltpu.SemaphoreType.DMA((2 * self.steps,)),
             ]
 
     def board(self, inputs, outputs, scratch):
@@ -132,25 +134,31 @@
             return whole.at[pl.ds(pl.multiple_of(owner_at(step % total) * rows, rows), rows)]
 
         def plan(source, target, prepare=None):
-            slot = len(self.copies)
+            half = source.shape[0] // self.sides
+            slot = self.sides * len(self.copies)
             self.copies.append(
-                pltpu.make_async_remote_copy(
-                    src_ref=source,
-                    dst_ref=target,
-                    send_sem=send.at[slot],
-                    recv_sem=recv.at[slot],
-                    device_id=ahead,
-                    device_id_type=MESH,
-                )
+                [
+                    pltpu.make_async_remote_copy(
+                        src_ref=source.at[pl.ds(side * half, half)],
+                        dst_ref=target.at[pl.ds(side * half, half)],
+                        send_sem=send.at[slot + side],
+                        recv_sem=recv.at[slot + side],
+                        device_id=ahead,
+                        device_id_type=MESH,
+                    )
+                    for side in range(self.sides)
+                ]
             )
             self.prepares.append(prepare)
 
         def adding(load, landed, own):
-            def prepare():
-                load.wait()
+            def prepare(side):
+                if side == 0:
+                    load.wait()
                 height = 64
-
-                @pl.loop(0, own.shape[0] // height)
+                count = own.shape[0] // (2 * height)
+
+                @pl.loop(side * count, side * count + count)
                 def _(index):
                     at = pl.ds(pl.multiple_of(index * height, height), height)
                     own[at, :] = (own[at, :].astype(F32) + landed[at, :].astype(F32)).astype(BF16)
@@ -179,33 +187,43 @@
             keep = pltpu.make_async_copy(own.at[count - 1], final, loaded.at[count])
             self.ends.append((last, prepare, keep))
 
-    def start(self, number):
+    def start(self, number, side):
         if self.prepares[number]:
-            self.prepares[number]()
-        self.copies[number].start()
-        self.begun = number + 1
+            self.prepares[number](side)
+        self.copies[number][side].start()
 
     def begin(self):
         for load in self.loads:
             load.start()
         if self.copies:
-            self.start(0)
+            for side in range(self.sides):
+                self.start(0, side)
+            self.begun = 1
 
     def advance(self):
         if 0 < self.begun < len(self.copies):
-            self.copies[self.begun - 1].wait_recv()
-            self.start(self.begun)
+            for side in range(self.sides):
+                self.copies[self.begun - 1][side].wait_recv()
+                self.start(self.begun, side)
+            self.begun += 1
 
     def finish(self):
         while self.begun < len(self.copies):
             self.advance()
-        if self.copies:
-            self.copies[-1].wait_recv()
-        for _, prepare, keep in self.ends:
-            prepare()
+        for side in range(self.sides):
+            if self.copies:
+                self.copies[-1][side].wait_recv()
+            for number, prepare, _ in self.ends:
+                if side == 0 and number < len(self.copies) - 1:
+                    prepare(0)
+                    prepare(1)
+                elif number == len(self.copies) - 1:
+                    prepare(side)
+        for _, _, keep in self.ends:
             keep.start()
-        for copy in self.copies:
-            copy.wait_send()
+        for pair in self.copies:
+            for copy in pair:
+                copy.wait_send()
         for _, _, keep in self.ends:
             keep.wait()
 
@@ -249,6 +267,8 @@
 
 
 class OwnRide(Ride):
+    sides = 1
+
     def __init__(self, count):
         super().__init__()
         self.steps = count
@@ -400,8 +420,8 @@
             pltpu.SemaphoreType.DMA((count + 2,)),
             pltpu.SemaphoreType.DMA(()),
             pltpu.SemaphoreType.DMA(()),
-            pltpu.SemaphoreType.DMA((steps,)),
-            pltpu.SemaphoreType.DMA((steps,)),
+            pltpu.SemaphoreType.DMA((2 * steps,)),
+            pltpu.SemaphoreType.DMA((2 * steps,)),
             pltpu.SemaphoreType.DMA((count,)),
         ]
         + [pltpu.VMEM(weight.shape, F32) for weight in weights]

time: 758 us -> 750 us (0.989)
  no operation moved by 1% of the time
where the time goes in v6:
time: 750 us; the launch traced here: 745 us
  Pallas kernels  648 us (86%)
  other arithmetic  31.8 us (4%)
  waiting for transfers between devices  23.5 us (3%)
  starting transfers between devices  18.8 us (3%)
  matrix products  14.6 us (2%)
    pallas_call x8, Pallas kernels, communicate(): pl.pallas_call(kernel, in_specs=list(specs) + [anywhere] * len(ride.opera...  468 us
    pallas_call x2, Pallas kernels, by_blocks(): pl.pallas_call(kernel, grid=(blocks,), in_specs=list(specs) + [anywhere]...  99.3 us
    pallas_call x1, Pallas kernels, dispatch(): pl.pallas_call(functools.partial(dispatch_kernel, tuple(turned), narrow,...  80.7 us
    ppermute x2, waiting for transfers between devices, from_plane(): by_y = lax.ppermute(piece(1 - me_y, me_x), 'y', ((0, 1), (1, 0)))  16.5 us
  transfers between devices with their start and end apart: 10, of which 5 were waited for; matrix products, arithmetic and copies ran while one was open for 4% of the time, Pallas kernels for 28%

profile of v6, /device:TPU:0, one launch (start us, length us, event | category | flops | bytes accessed | tf_op | source)
XLA Modules:
  0.0 744.8 jit_solution(18287785265264687370)
XLA Ops:
  1.5 1.0 convert_reduce_fusion.1
  2.7 1.5 fusion.refs_8_
  4.2 80.7 %dispatch.1 = (bf16[2048,1024]{1,0:T(8,128)(2,1)}, bf16[2048,1024]{1,0:T(8,128)(2,1)}, bf16[2048,1024]{1,0:T(8,128)(2,1)}, bf16[2048,1024]{1,0:T(8,128)(2,1)}, s...) custom-call(f32[128,1024]{1,0:T(8,128)} %refs_0_.1, f32[128,1024]{1,0:T(8,128)} %refs_1_.1, f32[128,1024]{1,0:T(8,128)} %refs_2_.1, ...), custom_call_target="tpu_custom_call" | custom-call | bytes 125829120 | tf_op jit(solution)/shard_map/dispatch/pallas_call | solution.py:412
  84.9 1.8 fusion.38
  87.1 1.3 fusion.4.refs_0_
  91.0 51.7 %gather_one.1 = (bf16[2048,2048]{1,0:T(8,128)(2,1)}, f32[2048,128]{1,0:T(8,128)}, f32[2048,128]{1,0:T(8,128)}, bf16[2048,1024]{1,0:T(8,128)(2,1)}, bf16[2048,1024]{1,0:T(8,128)(2,1)}) custom-call(bf16[256,2048]{1,0:T(8,128)(2,1)} %fusion.4.refs_0_, bf16[256,768]{1,0:T(8,128)(2,1)} %pad_maximum_fusion.1.refs_1_, ...), custom_call_target="tpu_custom_call", output_to_operand_aliasing={{3}: (3, {}), {4}: (4, {})} | custom-call | bytes 125829120 | tf_op jit(solution)/shard_map/gather_one/pallas_call | solution.py:251
  142.7 1.5 fusion.1
  144.3 4.3 all-to-all-start
  148.6 45.0 %attend.1 = (bf16[2048,768]{1,0:T(8,128)(2,1)}, bf16[2048,256]{1,0:T(8,128)(2,1)}, bf16[2048,1024]{1,0:T(8,128)(2,1)}) custom-call(bf16[2048,2048]{1,0:T(8,128)(2,1)} %get-tuple-element.62.refs_0_.refs_6_, bf16[2048,1024]{1,0:T(8,128)(2,1)} %get-tuple-element.63.refs_1_.refs_2_, ...), custom_call_target="tpu_custom_call", output_to_operand_aliasing={{2}: (5, {})} | custom-call | flops 6979321856 | bytes 41943040 | tf_op jit(solution)/shard_map/attend/pallas_call | solution.py:1227
  193.6 51.0 %product_out.1 = (f32[256,2048]{1,0:T(8,128)}, bf16[2048,1024]{1,0:T(8,128)(2,1)}, bf16[2048,1024]{1,0:T(8,128)(2,1)}) custom-call(bf16[2048,256]{1,0:T(8,128)(2,1)} %get-tuple-element.67.refs_0_.refs_8_, bf16[2048,1024]{1,0:T(8,128)(2,1)} %get-tuple-element.63.refs_1_.refs_2_, ...), custom_call_target="tpu_custom_call", output_to_operand_aliasing={{1}: (2, {}), {2}: (3, {})} | custom-call | flops 2147483648 | bytes 125829120 | tf_op jit(solution)/shard_map/product_out/pallas_call | solution.py:251
  244.6 1.9 fusion.32
  246.9 1.3 fusion.5.refs_0_
  248.2 53.6 %gather_two.1 = (bf16[2048,2048]{1,0:T(8,128)(2,1)}, bf16[2048,1024]{1,0:T(8,128)(2,1)}) custom-call(bf16[256,2048]{1,0:T(8,128)(2,1)} %fusion.5.refs_0_, bf16[2048,1024]{1,0:T(8,128)(2,1)} %get-tuple-element.72.refs_1_), custom_call_target="tpu_custom_call", output_to_operand_aliasing={{1}: (1, {})} | custom-call | bytes 125829120 | tf_op jit(solution)/shard_map/gather_two/pallas_call | solution.py:251
  301.8 1.5 convolution_convert_fusion.2.refs_0_
  303.2 71.1 %gather_up.1 = (bf16[2048,2048]{1,0:T(8,128)(2,1)}, bf16[2048,1024]{1,0:T(8,128)(2,1)}, bf16[2048,1024]{1,0:T(8,128)(2,1)}, bf16[2048,1024]{1,0:T(8,128)(2,1)}, ...) custom-call(bf16[256,2048]{1,0:T(8,128)(2,1)} %convolution_convert_fusion.2.refs_0_, ...), custom_call_target="tpu_custom_call", output_to_operand_aliasing={{5}: (4, {})} | custom-call | flops 25769803776 | bytes 125829120 | tf_op jit(solution)/shard_map/gather_up/pallas_call | solution.py:251
  374.3 71.7 %product_forward.1 = (f32[256,2048]{1,0:T(8,128)}, bf16[2048,1024]{1,0:T(8,128)(2,1)}, bf16[2048,1024]{1,0:T(8,128)(2,1)}, bf16[512,1024]{1,0:T(8,128)(2,1)}) custom-call(bf16[2048,1024]{1,0:T(8,128)(2,1)} %get-tuple-element.78.refs_0_, bf16[2048,1024]{1,0:T(8,128)(2,1)} %get-tuple-element.74.refs_2_.refs_1_, bf16[2048,1024]{1,0:T(8,128)(2,1)} %get-tuple-element.79.refs_2_, ...), custom_call_target="tpu_custom_call" | custom-call | flops 42949672960 | bytes 125829120 | tf_op jit(solution)/shard_map/product_forward/pallas_call | solution.py:251
  446.1 55.1 %product_down.1 = (f32[256,2048]{1,0:T(8,128)}, bf16[512,1024]{1,0:T(8,128)(2,1)}) custom-call(bf16[2048,1024]{1,0:T(8,128)(2,1)} %get-tuple-element.84.refs_0_, bf16[2048,1024]{1,0:T(8,128)(2,1)} %get-tuple-element.81.refs_5_.refs_1_, bf16[2048,1024]{1,0:T(8,128)(2,1)} %get-tuple-element.85.refs_2_), custom_call_target="tpu_custom_call" | custom-call | flops 8589934592 | bytes 125829120 | tf_op jit(solution)/shard_map/product_down/pallas_call | solution.py:251
  501.1 2.5 add.98
  503.6 1.5 fusion.2
  505.2 2.8 all-to-all-start.1
  508.0 2.8 fusion.30
  511.5 3.8 fusion.31
  515.3 61.1 %gather_middle.1 = (bf16[2048,2048]{1,0:T(8,128)(2,1)}, bf16[512,1024]{1,0:T(8,128)(2,1)}, bf16[512,1024]{1,0:T(8,128)(2,1)}) custom-call(bf16[256,2048]{1,0:T(8,128)(2,1)} %get-tuple-element.89.refs_0_, bf16[512,1024]{1,0:T(8,128)(2,1)} %get-tuple-element.90.refs_1_, bf16[2048,1024]{1,0:T(8,128)(2,1)} %get-tuple-element.85.refs_2_, ...), custom_call_target="tpu_custom_call" | custom-call | bytes 125829120 | tf_op jit(solution)/shard_map/gather_middle/pallas_call | solution.py:251
  576.3 2.8 all-to-all-done.1
  579.1 54.3 %attend_back.1 = (bf16[2048,768]{1,0:T(8,128)(2,1)}, bf16[2048,1024]{1,0:T(8,128)(2,1)}, bf16[4,128,1024]{2,1,0:T(8,128)(2,1)}, bf16[4,128,1024]{2,1,0:T(8,128)(2,1)}, bf16[512,1024]{1,0:T(8,128)(2,1)}) custom-call(bf16[2048,768]{1,0:T(8,128)(2,1)} %get-tuple-element.88.refs_0_, bf16[2048,2048]{1,0:T(8,128)(2,1)} %get-tuple-element.92.refs_1_.refs_7_, ...), custom_call_target="tpu_custom_call" | custom-call | flops 12079595520 | bytes 41943040 | tf_op jit(solution)/shard_map/attend_back/pallas_call | solution.py:1227
  633.4 52.5 %product_qkv.1 = (f32[256,2048]{1,0:T(8,128)}, bf16[512,1024]{1,0:T(8,128)(2,1)}) custom-call(bf16[2048,768]{1,0:T(8,128)(2,1)} %get-tuple-element.96.refs_0_, bf16[2048,1024]{1,0:T(8,128)(2,1)} %get-tuple-element.63.refs_1_.refs_2_, bf16[2048,1024]{1,0:T(8,128)(2,1)} %get-tuple-element.97.refs_2_), custom_call_target="tpu_custom_call" | custom-call | flops 6442450944 | bytes 125829120 | tf_op jit(solution)/shard_map/product_qkv/pallas_call | solution.py:251
  686.0 2.2 fusion.29
  688.8 2.0 fusion.3
  690.8 4.4 all-to-all-start.2
  695.3 1.8 collective-permute-start.5
  697.0 1.5 collective-permute-start.6
  698.8 1.8 fusion.18
  700.6 11.7 %collective-permute-done.5 = bf16[128,1024]{1,0:T(8,128)(2,1)S(1)} collective-permute-done((bf16[128,1024]{1,0:T(8,128)(2,1)S(1)}, bf16[128,1024]{1,0:T(8,128)(2,1)S(1)}, u32[]{:S(2)}, u32[]{:S(2)}) %collective-permute-start.5) | collective-permute-done | bytes 262176 | tf_op jit(solution)/shard_map/ppermute | solution.py:1041
  712.8 4.0 collective-permute-done
  716.8 1.9 add_convert_fusion
  718.8 0.9 constant_dynamic-slice_fusion.5
  720.2 1.7 collective-permute-start.3
  721.9 1.3 collective-permute-start.1
  723.2 0.9 slice_bitcast_fusion.11
  724.1 1.0 slice_bitcast_fusion.7
  725.4 1.8 copy.34
  727.2 2.7 maximum_convert_fusion
  730.0 1.5 maximum_convert_fusion.1
  731.5 4.8 collective-permute-done.2
  736.5 1.4 broadcast_select_fusion.11
  738.0 1.0 copy.33
  739.0 0.8 maximum_convert_fusion.2
  741.6 3.0 fusion.6
  (83 shorter events, 9.2 us)
Async XLA Ops:
  0.6 2.0 copy-start
  87.1 1.3 copy-start.15
  91.0 51.7 %copy-start.9 = (bf16[256,2048]{1,0:T(8,128)(2,1)S(1)}, bf16[256,2048]{1,0:T(8,128)(2,1)}, u32[]{:S(2)}) copy-start(bf16[256,2048]{1,0:T(8,128)(2,1)} %param.13) | copy-start | bytes 3145732
  144.3 157.5 %all-to-all-start = ((bf16[32,8,2048]{2,1,0:T(8,128)(2,1)}), bf16[32,8,2048]{2,1,0:T(8,128)(2,1)S(1)}, u32[]{:S(2)}, u32[]{:S(2)}) async-start(bf16[32,8,2048]{2,1,0:T(8,128)(2,1)} %fusion.1), calls=%async_computation | async-start | bytes 2097152 | tf_op jit(solution)/shard_map/all_to_all | solution.py:1335
  246.5 1.7 copy-start.2
  505.2 74.0 %all-to-all-start.1 = ((bf16[32,8,2048]{2,1,0:T(8,128)(2,1)}), bf16[32,8,2048]{2,1,0:T(8,128)(2,1)S(1)}, u32[]{:S(2)}, u32[]{:S(2)}) async-start(bf16[32,8,2048]{2,1,0:T(8,128)(2,1)} %fusion.2), calls=%async_computation.1 | async-start | bytes 2097152 | tf_op jit(solution)/shard_map/all_to_all | solution.py:1335
  508.0 2.9 copy-start.3
  508.0 3.5 copy-start.5
  686.0 2.5 copy-start.4
  686.0 2.8 copy-start.6
  688.2 28.6 %collective-permute-start = (bf16[512,1024]{1,0:T(8,128)(2,1)}, bf16[512,1024]{1,0:T(8,128)(2,1)}, u32[]{:S(2)}, u32[]{:S(2)}) collective-permute-start(bf16[512,1024]{1,0:T(8,128)(2,1)} %get-tuple-element.100), channel_id=1, source_target_pairs={{0,8},{8,16},{16,24},{24,0},{1,9},{9,17},{17,25},{25,1},{2,10},{10... | collective-permute-start | bytes 3145736 | tf_op jit(solution)/shard_map/ppermute | solution.py:970
  690.8 4.4 copy-start.10
  690.8 50.8 %all-to-all-start.2 = ((bf16[32,8,2048]{2,1,0:T(8,128)(2,1)}), bf16[32,8,2048]{2,1,0:T(8,128)(2,1)}, u32[]{:S(2)}, u32[]{:S(2)}) async-start(bf16[32,8,2048]{2,1,0:T(8,128)(2,1)} %fusion.3), calls=%async_computation.2 | async-start | bytes 2097152 | tf_op jit(solution)/shard_map/all_to_all | solution.py:1335
  695.3 17.1 %collective-permute-start.5 = (bf16[128,1024]{1,0:T(8,128)(2,1)S(1)}, bf16[128,1024]{1,0:T(8,128)(2,1)S(1)}, u32[]{:S(2)}, u32[]{:S(2)}) collective-permute-start(bf16[128,1024]{1,0:T(8,128)(2,1)S(1)} %get-tuple-element.162), channel_id=1, source_target_pairs={{0,4},{4,0},{1,5},{5,1},{2,6},{6,2},{3,7},{7,3},{8,12},{12,8},{9,1... | collective-permute-start | bytes 786440 | tf_op jit(solution)/shard_map/ppermute | solution.py:1041
  697.0 15.3 %collective-permute-start.6 = (bf16[128,1024]{1,0:T(8,128)(2,1)S(1)}, bf16[128,1024]{1,0:T(8,128)(2,1)S(1)}, u32[]{:S(2)}, u32[]{:S(2)}) collective-permute-start(bf16[128,1024]{1,0:T(8,128)(2,1)S(1)} %get-tuple-element.161), channel_id=1, source_target_pairs={{0,6},{2,4},{4,2},{6,0},{1,7},{3,5},{5,3},{7,1},{8,14},{10,12},{12... | collective-permute-start | bytes 786440 | tf_op jit(solution)/shard_map/ppermute | solution.py:1042
  698.5 13.9 %collective-permute-start.4 = (bf16[128,1024]{1,0:T(8,128)(2,1)S(1)}, bf16[128,1024]{1,0:T(8,128)(2,1)S(1)}, u32[]{:S(2)}, u32[]{:S(2)}) collective-permute-start(bf16[128,1024]{1,0:T(8,128)(2,1)S(1)} %get-tuple-element.160), channel_id=1, source_target_pairs={{0,2},{2,0},{1,3},{3,1},{4,6},{6,4},{5,7},{7,5},{8,10},{10,8},{9,1... | collective-permute-start | bytes 786440 | tf_op jit(solution)/shard_map/ppermute | solution.py:1040
  712.8 10.3 %copy-start.8 = (bf16[4,128,1024]{2,1,0:T(8,128)(2,1)S(1)}, bf16[4,128,1024]{2,1,0:T(8,128)(2,1)}, u32[]{:S(2)}) copy-start(bf16[4,128,1024]{2,1,0:T(8,128)(2,1)} %get-tuple-element.102) | copy-start | bytes 3145732
  719.7 16.6 %collective-permute-start.2 = (bf16[128,1024]{1,0:T(8,128)(2,1)}, bf16[128,1024]{1,0:T(8,128)(2,1)}, u32[]{:S(2)}, u32[]{:S(2)}) collective-permute-start(bf16[128,1024]{1,0:T(8,128)(2,1)} %get-tuple-element.169), channel_id=1, source_target_pairs={{0,4},{4,0},{1,5},{5,1},{2,6},{6,2},{3,7},{7,3},{8,12},{12,8},{9,1... | collective-permute-start | bytes 786440 | tf_op jit(solution)/shard_map/ppermute | solution.py:1041
  720.2 16.1 %collective-permute-start.3 = (bf16[128,1024]{1,0:T(8,128)(2,1)}, bf16[128,1024]{1,0:T(8,128)(2,1)}, u32[]{:S(2)}, u32[]{:S(2)}) collective-permute-start(bf16[128,1024]{1,0:T(8,128)(2,1)} %get-tuple-element.168), channel_id=1, source_target_pairs={{0,6},{2,4},{4,2},{6,0},{1,7},{3,5},{5,3},{7,1},{8,14},{10,12},{12... | collective-permute-start | bytes 786440 | tf_op jit(solution)/shard_map/ppermute | solution.py:1042
  721.9 14.6 %collective-permute-start.1 = (bf16[128,1024]{1,0:T(8,128)(2,1)}, bf16[128,1024]{1,0:T(8,128)(2,1)}, u32[]{:S(2)}, u32[]{:S(2)}) collective-permute-start(bf16[128,1024]{1,0:T(8,128)(2,1)} %get-tuple-element.167), channel_id=1, source_target_pairs={{0,2},{2,0},{1,3},{3,1},{4,6},{6,4},{5,7},{7,5},{8,10},{10,8},{9,1... | collective-permute-start | bytes 786440 | tf_op jit(solution)/shard_map/ppermute | solution.py:1040
  723.2 1.9 copy-start.7
  727.2 2.7 copy-start.11
  727.2 2.7 copy-start.12
  727.2 2.7 copy-start.13
  727.2 2.7 copy-start.14
  739.9 4.7 copy-start.1

commit v7 on v6

--- a/solution.py
+++ b/solution.py
@@ -3,6 +3,7 @@
 
 import jax
 import jax.numpy as jnp
+import numpy as np
 from jax import lax
 from jax.experimental import pallas as pl
 from jax.experimental.pallas import tpu as pltpu
@@ -387,8 +388,8 @@
     for index in range(narrow, count):
         share(index, functools.partial(piece, index), target(index))
     most = pl.ds(0, devices - 1)
+    ride.advance()
     pltpu.make_async_copy(packed.at[most], landed.at[most], rows_recv).wait()
-    ride.advance()
     for index in range(narrow, count + 1):
         arrive(index)
     keeps[count + 1].wait()
@@ -517,16 +518,15 @@
 
 def rotation_table(size):
     half_dim = HEAD_DIM // 2
-    frequency = jnp.exp(-jnp.arange(half_dim, dtype=F32) * (2.0 * math.log(10000.0) / HEAD_DIM))
-    angles = jnp.arange(size, dtype=jnp.int32).astype(F32)[:, None] * frequency[None, :]
-    cos_half, sin_half = jnp.cos(angles), jnp.sin(angles)
-    rest = jnp.concatenate([cos_half, cos_half, -sin_half, sin_half], axis=1)
+    steps = -np.arange(half_dim, dtype=np.float32) * np.float32(2.0 * math.log(10000.0) / HEAD_DIM)
+    angles = np.arange(size, dtype=np.float32)[:, None] * np.exp(steps)[None, :]
+    cos_half, sin_half = np.cos(angles), np.sin(angles)
+    rest = np.concatenate([cos_half, cos_half, -sin_half, sin_half], axis=1)
     terms = []
     for _ in range(3):
-        term = lax.reduce_precision(rest, 8, 7)
-        terms.append(term.astype(BF16))
-        rest = rest - term
-    return jnp.concatenate(terms, axis=1)
+        terms.append(rest.astype(BF16))
+        rest = rest - terms[-1].astype(np.float32)
+    return jnp.asarray(np.concatenate(terms, axis=1))
 
 
 def plane_gather_turns(rows, table, places, name, ride):

time: 750 us -> 747 us (level)
  no operation moved by 1% of the time
where the time goes in v7:
time: 747 us; the launch traced here: 742 us
  Pallas kernels  648 us (87%)
  other arithmetic  30.3 us (4%)
  waiting for transfers between devices  23.5 us (3%)
  starting transfers between devices  17.4 us (2%)
  matrix products  14.6 us (2%)
    pallas_call x8, Pallas kernels, communicate(): pl.pallas_call(kernel, in_specs=list(specs) + [anywhere] * len(ride.opera...  468 us
    pallas_call x2, Pallas kernels, by_blocks(): pl.pallas_call(kernel, grid=(blocks,), in_specs=list(specs) + [anywhere]...  99.3 us
    pallas_call x1, Pallas kernels, dispatch(): pl.pallas_call(functools.partial(dispatch_kernel, tuple(turned), narrow,...  80.7 us
    ppermute x2, waiting for transfers between devices, from_plane(): by_y = lax.ppermute(piece(1 - me_y, me_x), 'y', ((0, 1), (1, 0)))  16.5 us
  transfers between devices with their start and end apart: 10, of which 5 were waited for; matrix products, arithmetic and copies ran while one was open for 4% of the time, Pallas kernels for 28%

profile of v7, /device:TPU:0, one launch (start us, length us, event | category | flops | bytes accessed | tf_op | source)
XLA Modules:
  0.0 741.7 jit_solution(287006894415533096)
XLA Ops:
  1.5 1.0 convert_reduce_fusion.1
  2.6 1.5 fusion.refs_8_
  4.2 80.7 %dispatch.1 = (bf16[2048,1024]{1,0:T(8,128)(2,1)}, bf16[2048,1024]{1,0:T(8,128)(2,1)}, bf16[2048,1024]{1,0:T(8,128)(2,1)}, bf16[2048,1024]{1,0:T(8,128)(2,1)}, s...) custom-call(f32[128,1024]{1,0:T(8,128)} %refs_0_.1, f32[128,1024]{1,0:T(8,128)} %refs_1_.2, f32[128,1024]{1,0:T(8,128)} %refs_2_.1, ...), custom_call_target="tpu_custom_call" | custom-call | bytes 125829120 | tf_op jit(solution)/shard_map/dispatch/pallas_call | solution.py:413
  84.9 1.8 fusion.35
  87.1 1.3 fusion.4.refs_0_
  89.5 51.7 %gather_one.1 = (bf16[2048,2048]{1,0:T(8,128)(2,1)}, f32[2048,128]{1,0:T(8,128)}, f32[2048,128]{1,0:T(8,128)}, bf16[2048,1024]{1,0:T(8,128)(2,1)}, bf16[2048,1024]{1,0:T(8,128)(2,1)}) custom-call(bf16[256,2048]{1,0:T(8,128)(2,1)} %fusion.4.refs_0_, bf16[256,768]{1,0:T(8,128)(2,1)} %constant.76.clone.refs_1_, ...), custom_call_target="tpu_custom_call", output_to_operand_aliasing={{3}: (3, {}), {4}: (4, {})} | custom-call | bytes 125829120 | tf_op jit(solution)/shard_map/gather_one/pallas_call | solution.py:252
  141.2 1.5 fusion.1
  142.8 2.8 all-to-all-start
  145.6 45.0 %attend.1 = (bf16[2048,768]{1,0:T(8,128)(2,1)}, bf16[2048,256]{1,0:T(8,128)(2,1)}, bf16[2048,1024]{1,0:T(8,128)(2,1)}) custom-call(bf16[2048,2048]{1,0:T(8,128)(2,1)} %get-tuple-element.62.refs_0_.refs_6_, bf16[2048,1024]{1,0:T(8,128)(2,1)} %get-tuple-element.63.refs_1_.refs_2_, ...), custom_call_target="tpu_custom_call", output_to_operand_aliasing={{2}: (5, {})} | custom-call | flops 6979321856 | bytes 41943040 | tf_op jit(solution)/shard_map/attend/pallas_call | solution.py:1227
  190.6 51.0 %product_out.1 = (f32[256,2048]{1,0:T(8,128)}, bf16[2048,1024]{1,0:T(8,128)(2,1)}, bf16[2048,1024]{1,0:T(8,128)(2,1)}) custom-call(bf16[2048,256]{1,0:T(8,128)(2,1)} %get-tuple-element.67.refs_0_.refs_8_, bf16[2048,1024]{1,0:T(8,128)(2,1)} %get-tuple-element.63.refs_1_.refs_2_, ...), custom_call_target="tpu_custom_call", output_to_operand_aliasing={{1}: (2, {}), {2}: (3, {})} | custom-call | flops 2147483648 | bytes 125829120 | tf_op jit(solution)/shard_map/product_out/pallas_call | solution.py:252
  241.6 1.9 fusion.29
  243.9 1.3 fusion.5.refs_0_
  245.1 53.5 %gather_two.1 = (bf16[2048,2048]{1,0:T(8,128)(2,1)}, bf16[2048,1024]{1,0:T(8,128)(2,1)}) custom-call(bf16[256,2048]{1,0:T(8,128)(2,1)} %fusion.5.refs_0_, bf16[2048,1024]{1,0:T(8,128)(2,1)} %get-tuple-element.72.refs_1_), custom_call_target="tpu_custom_call", output_to_operand_aliasing={{1}: (1, {})} | custom-call | bytes 125829120 | tf_op jit(solution)/shard_map/gather_two/pallas_call | solution.py:252
  298.7 1.5 convolution_convert_fusion.2.refs_0_
  300.1 71.1 %gather_up.1 = (bf16[2048,2048]{1,0:T(8,128)(2,1)}, bf16[2048,1024]{1,0:T(8,128)(2,1)}, bf16[2048,1024]{1,0:T(8,128)(2,1)}, bf16[2048,1024]{1,0:T(8,128)(2,1)}, ...) custom-call(bf16[256,2048]{1,0:T(8,128)(2,1)} %convolution_convert_fusion.2.refs_0_, ...), custom_call_target="tpu_custom_call", output_to_operand_aliasing={{5}: (4, {})} | custom-call | flops 25769803776 | bytes 125829120 | tf_op jit(solution)/shard_map/gather_up/pallas_call | solution.py:252
  371.2 71.7 %product_forward.1 = (f32[256,2048]{1,0:T(8,128)}, bf16[2048,1024]{1,0:T(8,128)(2,1)}, bf16[2048,1024]{1,0:T(8,128)(2,1)}, bf16[512,1024]{1,0:T(8,128)(2,1)}) custom-call(bf16[2048,1024]{1,0:T(8,128)(2,1)} %get-tuple-element.78.refs_0_, bf16[2048,1024]{1,0:T(8,128)(2,1)} %get-tuple-element.74.refs_2_.refs_1_, bf16[2048,1024]{1,0:T(8,128)(2,1)} %get-tuple-element.79.refs_2_, ...), custom_call_target="tpu_custom_call" | custom-call | flops 42949672960 | bytes 125829120 | tf_op jit(solution)/shard_map/product_forward/pallas_call | solution.py:252
  442.9 55.1 %product_down.1 = (f32[256,2048]{1,0:T(8,128)}, bf16[512,1024]{1,0:T(8,128)(2,1)}) custom-call(bf16[2048,1024]{1,0:T(8,128)(2,1)} %get-tuple-element.84.refs_0_, bf16[2048,1024]{1,0:T(8,128)(2,1)} %get-tuple-element.81.refs_5_.refs_1_, bf16[2048,1024]{1,0:T(8,128)(2,1)} %get-tuple-element.85.refs_2_), custom_call_target="tpu_custom_call" | custom-call | flops 8589934592 | bytes 125829120 | tf_op jit(solution)/shard_map/product_down/pallas_call | solution.py:252
  498.0 2.5 add.98
  500.5 1.5 fusion.2
  502.0 2.8 all-to-all-start.1
  504.9 2.8 fusion.27
  508.4 3.8 fusion.28
  512.1 61.0 %gather_middle.1 = (bf16[2048,2048]{1,0:T(8,128)(2,1)}, bf16[512,1024]{1,0:T(8,128)(2,1)}, bf16[512,1024]{1,0:T(8,128)(2,1)}) custom-call(bf16[256,2048]{1,0:T(8,128)(2,1)} %get-tuple-element.89.refs_0_, bf16[512,1024]{1,0:T(8,128)(2,1)} %get-tuple-element.90.refs_1_, bf16[2048,1024]{1,0:T(8,128)(2,1)} %get-tuple-element.85.refs_2_, ...), custom_call_target="tpu_custom_call" | custom-call | bytes 125829120 | tf_op jit(solution)/shard_map/gather_middle/pallas_call | solution.py:252
  573.2 2.8 all-to-all-done.1
  576.0 54.3 %attend_back.1 = (bf16[2048,768]{1,0:T(8,128)(2,1)}, bf16[2048,1024]{1,0:T(8,128)(2,1)}, bf16[4,128,1024]{2,1,0:T(8,128)(2,1)}, bf16[4,128,1024]{2,1,0:T(8,128)(2,1)}, bf16[512,1024]{1,0:T(8,128)(2,1)}) custom-call(bf16[2048,768]{1,0:T(8,128)(2,1)} %get-tuple-element.88.refs_0_, bf16[2048,2048]{1,0:T(8,128)(2,1)} %get-tuple-element.92.refs_1_.refs_7_, ...), custom_call_target="tpu_custom_call" | custom-call | flops 12079595520 | bytes 41943040 | tf_op jit(solution)/shard_map/attend_back/pallas_call | solution.py:1227
  630.3 52.5 %product_qkv.1 = (f32[256,2048]{1,0:T(8,128)}, bf16[512,1024]{1,0:T(8,128)(2,1)}) custom-call(bf16[2048,768]{1,0:T(8,128)(2,1)} %get-tuple-element.96.refs_0_, bf16[2048,1024]{1,0:T(8,128)(2,1)} %get-tuple-element.63.refs_1_.refs_2_, bf16[2048,1024]{1,0:T(8,128)(2,1)} %get-tuple-element.97.refs_2_), custom_call_target="tpu_custom_call" | custom-call | flops 6442450944 | bytes 125829120 | tf_op jit(solution)/shard_map/product_qkv/pallas_call | solution.py:252
  682.9 2.2 fusion.26
  685.7 2.0 fusion.3
  687.7 4.4 all-to-all-start.2
  692.2 1.8 collective-permute-start.5
  693.9 1.5 collective-permute-start.6
  695.7 1.8 fusion.16
  697.5 11.7 %collective-permute-done.5 = bf16[128,1024]{1,0:T(8,128)(2,1)S(1)} collective-permute-done((bf16[128,1024]{1,0:T(8,128)(2,1)S(1)}, bf16[128,1024]{1,0:T(8,128)(2,1)S(1)}, u32[]{:S(2)}, u32[]{:S(2)}) %collective-permute-start.5) | collective-permute-done | bytes 262176 | tf_op jit(solution)/shard_map/ppermute | solution.py:1041
  709.7 4.0 collective-permute-done
  713.7 1.9 add_convert_fusion
  715.7 0.9 constant_dynamic-slice_fusion.5
  717.1 1.7 collective-permute-start.3
  718.8 1.3 collective-permute-start.1
  720.1 0.9 slice_bitcast_fusion.11
  721.0 1.0 slice_bitcast_fusion.7
  722.3 1.8 copy.32
  724.1 2.7 maximum_convert_fusion
  726.9 1.5 maximum_convert_fusion.1
  728.4 4.7 collective-permute-done.2
  733.4 1.4 broadcast_select_fusion.11
  734.9 1.0 copy.31
  736.8 0.8 maximum_convert_fusion.3
  738.5 3.0 fusion.6
  (78 shorter events, 7.8 us)
Async XLA Ops:
  0.6 2.0 copy-start
  87.0 1.3 copy-start.15
  89.5 51.8 %copy-start.9 = (bf16[256,2048]{1,0:T(8,128)(2,1)S(1)}, bf16[256,2048]{1,0:T(8,128)(2,1)}, u32[]{:S(2)}) copy-start(bf16[256,2048]{1,0:T(8,128)(2,1)} %param.14) | copy-start | bytes 3145732
  142.8 155.9 %all-to-all-start = ((bf16[32,8,2048]{2,1,0:T(8,128)(2,1)}), bf16[32,8,2048]{2,1,0:T(8,128)(2,1)S(1)}, u32[]{:S(2)}, u32[]{:S(2)}) async-start(bf16[32,8,2048]{2,1,0:T(8,128)(2,1)} %fusion.1), calls=%async_computation | async-start | bytes 2097152 | tf_op jit(solution)/shard_map/all_to_all | solution.py:1335
  243.5 1.7 copy-start.2
  502.0 74.0 %all-to-all-start.1 = ((bf16[32,8,2048]{2,1,0:T(8,128)(2,1)}), bf16[32,8,2048]{2,1,0:T(8,128)(2,1)S(1)}, u32[]{:S(2)}, u32[]{:S(2)}) async-start(bf16[32,8,2048]{2,1,0:T(8,128)(2,1)} %fusion.2), calls=%async_computation.1 | async-start | bytes 2097152 | tf_op jit(solution)/shard_map/all_to_all | solution.py:1335
  504.9 2.9 copy-start.3
  504.9 3.5 copy-start.5
  682.9 2.5 copy-start.4
  682.9 2.8 copy-start.6
  685.1 28.6 %collective-permute-start = (bf16[512,1024]{1,0:T(8,128)(2,1)}, bf16[512,1024]{1,0:T(8,128)(2,1)}, u32[]{:S(2)}, u32[]{:S(2)}) collective-permute-start(bf16[512,1024]{1,0:T(8,128)(2,1)} %get-tuple-element.100), channel_id=1, source_target_pairs={{0,8},{8,16},{16,24},{24,0},{1,9},{9,17},{17,25},{25,1},{2,10},{10... | collective-permute-start | bytes 3145736 | tf_op jit(solution)/shard_map/ppermute | solution.py:970
  687.7 4.4 copy-start.10
  687.7 50.8 %all-to-all-start.2 = ((bf16[32,8,2048]{2,1,0:T(8,128)(2,1)}), bf16[32,8,2048]{2,1,0:T(8,128)(2,1)}, u32[]{:S(2)}, u32[]{:S(2)}) async-start(bf16[32,8,2048]{2,1,0:T(8,128)(2,1)} %fusion.3), calls=%async_computation.2 | async-start | bytes 2097152 | tf_op jit(solution)/shard_map/all_to_all | solution.py:1335
  692.2 17.1 %collective-permute-start.5 = (bf16[128,1024]{1,0:T(8,128)(2,1)S(1)}, bf16[128,1024]{1,0:T(8,128)(2,1)S(1)}, u32[]{:S(2)}, u32[]{:S(2)}) collective-permute-start(bf16[128,1024]{1,0:T(8,128)(2,1)S(1)} %get-tuple-element.153), channel_id=1, source_target_pairs={{0,4},{4,0},{1,5},{5,1},{2,6},{6,2},{3,7},{7,3},{8,12},{12,8},{9,1... | collective-permute-start | bytes 786440 | tf_op jit(solution)/shard_map/ppermute | solution.py:1041
  693.9 15.3 %collective-permute-start.6 = (bf16[128,1024]{1,0:T(8,128)(2,1)S(1)}, bf16[128,1024]{1,0:T(8,128)(2,1)S(1)}, u32[]{:S(2)}, u32[]{:S(2)}) collective-permute-start(bf16[128,1024]{1,0:T(8,128)(2,1)S(1)} %get-tuple-element.152), channel_id=1, source_target_pairs={{0,6},{2,4},{4,2},{6,0},{1,7},{3,5},{5,3},{7,1},{8,14},{10,12},{12... | collective-permute-start | bytes 786440 | tf_op jit(solution)/shard_map/ppermute | solution.py:1042
  695.4 13.9 %collective-permute-start.4 = (bf16[128,1024]{1,0:T(8,128)(2,1)S(1)}, bf16[128,1024]{1,0:T(8,128)(2,1)S(1)}, u32[]{:S(2)}, u32[]{:S(2)}) collective-permute-start(bf16[128,1024]{1,0:T(8,128)(2,1)S(1)} %get-tuple-element.151), channel_id=1, source_target_pairs={{0,2},{2,0},{1,3},{3,1},{4,6},{6,4},{5,7},{7,5},{8,10},{10,8},{9,1... | collective-permute-start | bytes 786440 | tf_op jit(solution)/shard_map/ppermute | solution.py:1040
  709.7 10.3 %copy-start.8 = (bf16[4,128,1024]{2,1,0:T(8,128)(2,1)S(1)}, bf16[4,128,1024]{2,1,0:T(8,128)(2,1)}, u32[]{:S(2)}) copy-start(bf16[4,128,1024]{2,1,0:T(8,128)(2,1)} %get-tuple-element.102) | copy-start | bytes 3145732
  716.6 16.6 %collective-permute-start.2 = (bf16[128,1024]{1,0:T(8,128)(2,1)}, bf16[128,1024]{1,0:T(8,128)(2,1)}, u32[]{:S(2)}, u32[]{:S(2)}) collective-permute-start(bf16[128,1024]{1,0:T(8,128)(2,1)} %get-tuple-element.160), channel_id=1, source_target_pairs={{0,4},{4,0},{1,5},{5,1},{2,6},{6,2},{3,7},{7,3},{8,12},{12,8},{9,1... | collective-permute-start | bytes 786440 | tf_op jit(solution)/shard_map/ppermute | solution.py:1041
  717.1 16.1 %collective-permute-start.3 = (bf16[128,1024]{1,0:T(8,128)(2,1)}, bf16[128,1024]{1,0:T(8,128)(2,1)}, u32[]{:S(2)}, u32[]{:S(2)}) collective-permute-start(bf16[128,1024]{1,0:T(8,128)(2,1)} %get-tuple-element.159), channel_id=1, source_target_pairs={{0,6},{2,4},{4,2},{6,0},{1,7},{3,5},{5,3},{7,1},{8,14},{10,12},{12... | collective-permute-start | bytes 786440 | tf_op jit(solution)/shard_map/ppermute | solution.py:1042
  718.8 14.6 %collective-permute-start.1 = (bf16[128,1024]{1,0:T(8,128)(2,1)}, bf16[128,1024]{1,0:T(8,128)(2,1)}, u32[]{:S(2)}, u32[]{:S(2)}) collective-permute-start(bf16[128,1024]{1,0:T(8,128)(2,1)} %get-tuple-element.158), channel_id=1, source_target_pairs={{0,2},{2,0},{1,3},{3,1},{4,6},{6,4},{5,7},{7,5},{8,10},{10,8},{9,1... | collective-permute-start | bytes 786440 | tf_op jit(solution)/shard_map/ppermute | solution.py:1040
  720.1 1.9 copy-start.7
  724.1 2.7 copy-start.11
  724.1 2.7 copy-start.12
  724.1 2.7 copy-start.13
  724.1 2.7 copy-start.14
  736.8 4.7 copy-start.1
